TPU v7x, 32 devices: a whole 2x2x4 slice. The times are simulated.
32 devices in a mesh: pix: 8 (over y, x, core), tm: 4 (over z).
Axes of the slice: x: 2, y: 2, z: 4, core: 2. Of those that a mesh axis runs over, the one named last changes fastest.
Arguments:
- fields: float32 [256, 8, 2, 1024], P('pix', None, None, 'tm'), may hold values from -6 to 6
- profiles: bfloat16 [16384, 256], P('pix'), may hold values from -0.5 to 0.5
- phase: float32 [256, 1024], P(('pix', 'tm')), may hold values from -3.140625 to 3.140625
Outputs:
- advanced: float32 [256, 8, 2, 1024], P('pix', None, None, 'tm')
All inputs are finite; a program needn't handle non-finite values.
Results may differ from a plain program's by a relative error of at most 0.003.
Values may be sent and summed in bfloat16 or wider, within the bound.
No kernel may reach another device: no remote copies, remote signals or barrier semaphores. Data moves between devices by JAX's collectives and lax.ppermute only.
A program may use at most 64 MiB of HBM per device.

v0:
```python
import functools
import math

import jax
import jax.numpy as jnp
import numpy as np
from jax import lax
from jax.experimental import pallas as pl
from jax.experimental.pallas import tpu as pltpu
from jax.sharding import PartitionSpec as P

BF16 = jnp.bfloat16
F32 = jnp.float32
CHUNKS = (1,)
VMEM = pl.BlockSpec(memory_space=pltpu.VMEM)


def call(kernel, name, outs, scratch=(), cost=None):
    def run(*args):
        return pl.pallas_call(
            kernel,
            out_shape=tuple(jax.ShapeDtypeStruct(*out) for out in outs),
            in_specs=[VMEM] * len(args),
            out_specs=tuple(VMEM for _ in outs),
            scratch_shapes=[pltpu.VMEM(*item) for item in scratch],
            compiler_params=pltpu.CompilerParams(vmem_limit_bytes=56 * 2**20),
            cost_estimate=None
            if cost is None
            else pl.CostEstimate(flops=cost[0], bytes_accessed=cost[1], transcendentals=0),
            name=name,
        )(*args)

    return run


def swap_pix(value, mask, size):
    return lax.ppermute(value, "pix", [(i, i ^ mask) for i in range(size)])


def swap_tm(value, mask, size):
    return lax.ppermute(value, "tm", [(i, i ^ mask) for i in range(size)])


def split_kernel(starts, sizes, fields, *outs):
    half = fields.shape[1] // 2
    core = lax.axis_index("pix") % 2
    for n, (start, nb) in enumerate(zip(starts, sizes)):
        own, other = outs[2 * n], outs[2 * n + 1]
        for c in range(2):
            for b in range(nb):
                own[c * nb + b] = fields[:, core * half + start + b, c, :]
                other[c * nb + b] = fields[:, (1 - core) * half + start + b, c, :]


def modal_kernel(own, other, full, modal):
    rows = own.shape[1]
    core = lax.axis_index("pix") % 2
    mine = pl.multiple_of(core * rows, rows)
    theirs = pl.multiple_of((1 - core) * rows, rows)
    for k in range(own.shape[0]):
        value = own[k]
        full[k, pl.ds(mine, rows), :] = value
        modal[k, pl.ds(mine, rows), :] = value.astype(BF16)
        value = other[k]
        full[k, pl.ds(theirs, rows), :] = value
        modal[k, pl.ds(theirs, rows), :] = value.astype(BF16)


def turn_kernel(rows, chips, profiles, turned):
    chip = lax.axis_index("pix") // 2
    step = 256
    for i in range(profiles.shape[0] // step):
        block = profiles[i * step : (i + 1) * step, :].T
        for j in range(chips):
            place = pl.multiple_of((chip ^ j) * rows, rows)
            turned[pl.ds(place, rows), i * step : (i + 1) * step] = block[j * rows : (j + 1) * rows]


def kerr_kernel(nb, chips, tile, *refs):
    profiles, turned = refs[0:2], refs[2:4]
    blocks = refs[4 : 4 + chips]
    outs = refs[4 + chips : 4 + 2 * chips]
    gathered, cubed = refs[4 + 2 * chips :]
    chip = lax.axis_index("pix") // 2
    rows, time = blocks[0].shape[1:]
    pixels = profiles[0].shape[0]

    def one(b, carry):
        for j in range(chips):
            place = pl.multiple_of((chip ^ j) * rows, rows)
            for c in range(2):
                gathered[pl.ds(place, rows), c * time : (c + 1) * time] = blocks[j][c * nb + b]
        modal = gathered[...]
        for h in range(2):
            for i in range(pixels // tile):
                spatial = jnp.dot(
                    profiles[h][i * tile : (i + 1) * tile, :], modal, preferred_element_type=F32
                )
                real, imag = spatial[:, :time], spatial[:, time:]
                power = real * real + imag * imag
                at = h * pixels + i * tile
                cubed[at : at + tile, :time] = (power * real).astype(BF16)
                cubed[at : at + tile, time:] = (power * imag).astype(BF16)
        kerr = jnp.dot(turned[0][...], cubed[:pixels], preferred_element_type=F32) + jnp.dot(
            turned[1][...], cubed[pixels:], preferred_element_type=F32
        )
        for j in range(chips):
            for c in range(2):
                outs[j][c * nb + b] = kerr[
                    j * rows : (j + 1) * rows, c * time : (c + 1) * time
                ].astype(outs[j].dtype)
        return carry

    lax.fori_loop(0, nb, one, 0)


def step_kernel(nb, scale, times, full, *refs):
    chips = len(refs) - times - 1
    parts, outs, stepped = refs[:chips], refs[chips:-1], refs[-1]
    z = lax.axis_index("tm")
    rows = full.shape[1]
    cut = rows // 2 // times

    def total(k):
        value = parts[0][k]
        for part in parts[1:]:
            value = value + part[k].astype(F32)
        return value * scale

    for b in range(nb):
        stepped[b] = full[b] - total(nb + b)
        stepped[nb + b] = full[nb + b] + total(b)
    for j in range(times):
        for h in range(2):
            at = pl.multiple_of(h * (rows // 2) + (z ^ j) * cut, cut)
            for k in range(2 * nb):
                outs[j][k, h * cut : (h + 1) * cut, :] = stepped[k, pl.ds(at, cut), :].astype(
                    outs[j].dtype
                )


def product(value, high, low):
    top = value.astype(BF16)
    rest = (value - top.astype(F32)).astype(BF16)
    out = jnp.dot(top, high, preferred_element_type=F32)
    out = out + jnp.dot(rest, high, preferred_element_type=F32)
    return out + jnp.dot(top, low, preferred_element_type=F32)


def weighted(terms, powers):
    real, imag = None, None
    for (re, im), power in zip(terms, powers):
        re, im = ((re, im), (-im, re), (-re, -im), (im, -re))[power % 4]
        real = re if real is None else real + re
        imag = im if imag is None else imag + im
    return real, imag


def wave_kernel(nb, times, *refs):
    blocks = refs[:times]
    phase_cos, phase_sin, cos_high, cos_low, sin_high, sin_low, twist_cos, twist_sin = refs[
        times : times + 8
    ]
    outs = refs[times + 8 : 2 * times + 8]
    held, back = refs[2 * times + 8 :]
    z = lax.axis_index("tm")
    rows, time = blocks[0].shape[1:]
    size = nb * rows
    length = times * time
    for j in range(times):
        held[z ^ j] = blocks[j][...].astype(F32)
    here = [
        (held[a, :nb].reshape(size, time), held[a, nb:].reshape(size, time)) for a in range(times)
    ]
    real, imag = [], []
    for s in range(times):
        re, im = weighted(here, [-a * s for a in range(times)])
        tc, ts = twist_cos[s : s + 1, :], twist_sin[s : s + 1, :]
        real.append(re * tc + im * ts)
        imag.append(im * tc - re * ts)
    real, imag = jnp.concatenate(real, axis=0), jnp.concatenate(imag, axis=0)
    ch, cl, sh, sl = cos_high[...], cos_low[...], sin_high[...], sin_low[...]
    freq_re = product(real, ch, cl) + product(imag, sh, sl)
    freq_im = product(imag, ch, cl) - product(real, sh, sl)
    shape = (times, nb, rows, time)
    pc = jnp.broadcast_to(phase_cos[...][:, None], shape).reshape(times * size, time)
    ps = jnp.broadcast_to(phase_sin[...][:, None], shape).reshape(times * size, time)
    spun_re = freq_re * pc - freq_im * ps
    spun_im = freq_re * ps + freq_im * pc
    back_re = product(spun_re, ch, cl) - product(spun_im, sh, sl)
    back_im = product(spun_im, ch, cl) + product(spun_re, sh, sl)
    terms = []
    for s in range(times):
        tc, ts = twist_cos[s : s + 1, :] / length, twist_sin[s : s + 1, :] / length
        re, im = back_re[s * size : (s + 1) * size], back_im[s * size : (s + 1) * size]
        terms.append((re * tc - im * ts, im * tc + re * ts))
    for a in range(times):
        re, im = weighted(terms, [a * s for s in range(times)])
        back[a, :nb] = re.reshape(nb, rows, time)
        back[a, nb:] = im.reshape(nb, rows, time)
    for j in range(times):
        outs[j][...] = back[z ^ j].astype(outs[j].dtype)


def part_kernel(times, *refs):
    blocks, (own, other), (held,) = refs[:times], refs[times : times + 2], refs[times + 2 :]
    core = lax.axis_index("pix") % 2
    z = lax.axis_index("tm")
    cut = blocks[0].shape[1] // 2
    for j in range(times):
        held[...] = blocks[j][...].astype(F32)
        at = pl.multiple_of((z ^ j) * cut, cut)
        mine = pl.multiple_of(core * cut, cut)
        theirs = pl.multiple_of((1 - core) * cut, cut)
        own[:, pl.ds(at, cut), :] = held[:, pl.ds(mine, cut), :]
        other[:, pl.ds(at, cut), :] = held[:, pl.ds(theirs, cut), :]


def join_kernel(starts, sizes, *refs):
    out = refs[-1]
    half = out.shape[1] // 2
    core = lax.axis_index("pix") % 2
    for n, (start, nb) in enumerate(zip(starts, sizes)):
        own, other = refs[2 * n], refs[2 * n + 1]
        for c in range(2):
            for b in range(nb):
                out[:, core * half + start + b, c, :] = own[c * nb + b]
                out[:, (1 - core) * half + start + b, c, :] = other[c * nb + b].astype(F32)


def tables(times, time):
    index = np.arange(time)
    angle = 2.0 * np.pi / time * (index[:, None] * index[None, :] % time)
    length = times * time
    twist = 2.0 * np.pi / length * (np.arange(times)[:, None] * index[None, :] % length)
    out = []
    for table in (np.cos(angle), np.sin(angle)):
        high = table.astype(np.float32).astype(jnp.bfloat16)
        low = (table - high.astype(np.float64)).astype(np.float32).astype(jnp.bfloat16)
        out += [jnp.asarray(high), jnp.asarray(low)]
    return out + [jnp.asarray(f(twist).astype(np.float32)) for f in (np.cos, np.sin)]


def fast_body(pix, times, fields, profiles, phase):
    modes, batch, _, time = fields.shape
    chips, half = pix // 2, batch // 2
    pixels = profiles.shape[0]
    rows = 2 * modes
    cut = rows // times
    scale = 1.0 / math.sqrt(pixels * pix)
    sizes = [half * part // sum(CHUNKS) for part in CHUNKS]
    starts = [sum(sizes[:n]) for n in range(len(sizes))]
    core = lax.axis_index("pix") % 2

    halves = call(
        functools.partial(split_kernel, starts, sizes),
        "split",
        [((2 * nb, modes, time), F32) for nb in sizes for _ in range(2)],
    )(fields)
    others = [swap_pix(halves[2 * n + 1], 1, pix) for n in range(len(sizes))]
    profiles_other = swap_pix(profiles, 1, pix)
    phase_other = swap_pix(phase, 1, pix)

    fulls, gathers = [], []
    for n, nb in enumerate(sizes):
        full, modal = call(
            modal_kernel, "modal", [((2 * nb, rows, time), F32), ((2 * nb, rows, time), BF16)]
        )(halves[2 * n], others[n])
        fulls.append(full)
        gathers.append([modal] + [swap_pix(modal, 2 * j, pix) for j in range(1, chips)])

    turn = call(
        functools.partial(turn_kernel, rows, chips), "turn", [((chips * rows, pixels), BF16)]
    )
    turned = turn(profiles)[0], turn(profiles_other)[0]

    low = jnp.where(core == 0, phase, phase_other)
    high = jnp.where(core == 0, phase_other, phase)
    angles = jnp.concatenate([low, high], axis=0).reshape(cut, time, times).transpose(2, 0, 1)
    phase_cos, phase_sin = jnp.cos(angles), jnp.sin(angles)
    consts = tables(times, time)

    finals = []
    for n, nb in enumerate(sizes):
        block = (2 * nb, rows, time)
        parts = call(
            functools.partial(kerr_kernel, nb, chips, 512),
            "kerr",
            [(block, F32)] + [(block, BF16)] * (chips - 1),
            [((chips * rows, 2 * time), BF16), ((2 * pixels, 2 * time), BF16)],
        )(profiles, profiles_other, *turned, *gathers[n])
        sums = [parts[0]] + [swap_pix(parts[j], 2 * j, pix) for j in range(1, chips)]
        block = (2 * nb, cut, time)
        pieces = call(
            functools.partial(step_kernel, nb, scale, times),
            "step",
            [(block, F32)] + [(block, BF16)] * (times - 1),
            [((2 * nb, rows, time), F32)],
        )(fulls[n], *sums)
        pieces = [pieces[0]] + [swap_tm(pieces[j], j, times) for j in range(1, times)]
        pieces = call(
            functools.partial(wave_kernel, nb, times),
            "wave",
            [(block, F32)] + [(block, BF16)] * (times - 1),
            [((times,) + block, F32)] * 2,
        )(*pieces, phase_cos, phase_sin, *consts)
        pieces = [pieces[0]] + [swap_tm(pieces[j], j, times) for j in range(1, times)]
        own, other = call(
            functools.partial(part_kernel, times),
            "part",
            [((2 * nb, modes, time), F32), ((2 * nb, modes, time), F32)],
            [(block, F32)],
        )(*pieces)
        finals += [own, swap_pix(other, 1, pix)]
    return call(functools.partial(join_kernel, starts, sizes), "join", [(fields.shape, F32)])(
        *finals
    )[0]


def split_length(length):
    first = 2 ** ((length.bit_length() - 1) // 2)
    return (first, length // first)


def small_table(size):
    index = jnp.arange(size, dtype=jnp.int32)
    product = index[:, None] * index[None, :] % size
    angles = product.astype(jnp.float32) * (2.0 * math.pi / size)
    return (jnp.cos(angles), jnp.sin(angles))


def twiddles(first, second, length):
    rows = jnp.arange(first, dtype=jnp.int32)
    cols = jnp.arange(second, dtype=jnp.int32)
    product = rows[:, None] * cols[None, :] % length
    angles = product.astype(jnp.float32) * (2.0 * math.pi / length)
    return (jnp.cos(angles), jnp.sin(angles))


def contract_last(values, table):
    return jnp.einsum(
        "mbkv,vq->mbkq",
        values,
        table,
        precision=lax.Precision.HIGHEST,
        preferred_element_type=jnp.float32,
    )


def contract_third(values, table):
    return jnp.einsum(
        "mbuv,uk->mbkv",
        values,
        table,
        precision=lax.Precision.HIGHEST,
        preferred_element_type=jnp.float32,
    )


def dispersed(values, phase_rows, length):
    first, second = split_length(length)
    cos_first, sin_first = small_table(first)
    cos_second, sin_second = small_table(second)
    twist_cos, twist_sin = twiddles(first, second, length)
    modes_here = values.shape[0]
    batch = values.shape[1]
    real_part = values[:, :, 0].reshape(modes_here, batch, first, second)
    imag_part = values[:, :, 1].reshape(modes_here, batch, first, second)
    section_re = contract_third(real_part, cos_first) + contract_third(imag_part, sin_first)
    section_im = contract_third(imag_part, cos_first) - contract_third(real_part, sin_first)
    turned_re = section_re * twist_cos + section_im * twist_sin
    turned_im = section_im * twist_cos - section_re * twist_sin
    freq_re = contract_last(turned_re, cos_second) + contract_last(turned_im, sin_second)
    freq_im = contract_last(turned_im, cos_second) - contract_last(turned_re, sin_second)
    ordered = jnp.transpose(phase_rows.reshape(modes_here, second, first), (0, 2, 1))[:, None]
    phase_cos = jnp.cos(ordered)
    phase_sin = jnp.sin(ordered)
    spun_re = freq_re * phase_cos - freq_im * phase_sin
    spun_im = freq_re * phase_sin + freq_im * phase_cos
    back_re = contract_last(spun_re, cos_second) - contract_last(spun_im, sin_second)
    back_im = contract_last(spun_im, cos_second) + contract_last(spun_re, sin_second)
    again_re = back_re * twist_cos - back_im * twist_sin
    again_im = back_im * twist_cos + back_re * twist_sin
    out_re = contract_third(again_re, cos_first) - contract_third(again_im, sin_first)
    out_im = contract_third(again_im, cos_first) + contract_third(again_re, sin_first)
    out_re = out_re.reshape(modes_here, batch, length) / length
    out_im = out_im.reshape(modes_here, batch, length) / length
    return jnp.stack([out_re, out_im], axis=2)


def body(fields, profiles, phase):
    mode_local = fields.shape[0]
    batch = fields.shape[1]
    time_local = fields.shape[3]
    pixel_local = profiles.shape[0]
    length = time_local * lax.axis_size("tm")
    scale = 1.0 / math.sqrt(pixel_local * lax.axis_size("pix"))
    modal = fields.astype(jnp.bfloat16)
    piece = lax.all_gather(modal, "pix", axis=0, tiled=True)
    columns = profiles
    spatial = jnp.dot(
        columns, piece.reshape(piece.shape[0], -1), preferred_element_type=jnp.float32
    )
    spatial = spatial.reshape(pixel_local, batch, 2, time_local)
    real_part = spatial[:, :, 0]
    imag_part = spatial[:, :, 1]
    power = real_part * real_part + imag_part * imag_part
    nonlin = (
        jnp.stack([power * real_part, power * imag_part], axis=2)
        .astype(jnp.bfloat16)
        .reshape(pixel_local, -1)
    )
    columns = profiles
    kerr = lax.psum_scatter(
        lax.dot_general(
            columns, nonlin, (((0,), (0,)), ((), ())), preferred_element_type=jnp.float32
        ),
        "pix",
        scatter_dimension=0,
        tiled=True,
    )
    kerr = kerr.reshape(mode_local, batch, 2, time_local) * scale
    stepped = jnp.stack([fields[:, :, 0] - kerr[:, :, 1], fields[:, :, 1] + kerr[:, :, 0]], axis=2)
    result = dispersed(
        lax.all_to_all(stepped, "tm", split_axis=0, concat_axis=3, tiled=True), phase, length
    )
    return lax.all_to_all(result, "tm", split_axis=3, concat_axis=0, tiled=True)


def solution(mesh):
    pix, times = mesh.shape["pix"], mesh.shape["tm"]

    def run(fields, profiles, phase):
        modes, batch, _, time = fields.shape
        fits = (
            pix % 2 == 0
            and pix & (pix - 1) == 0
            and times == 4
            and modes % (8 * times) == 0
            and batch % 2 == 0
            and time % 256 == 0
            and profiles.shape[0] % 512 == 0
        )
        if fits:
            return fast_body(pix, times, fields, profiles, phase)
        return body(fields, profiles, phase)

    return jax.shard_map(
        run,
        mesh=mesh,
        in_specs=(P("pix", None, None, "tm"), P("pix", None), P(("pix", "tm"), None)),
        out_specs=P("pix", None, None, "tm"),
        check_vma=False,
    )
```

profile of v0, /device:TPU:0, one launch (start us, length us, event | category | flops | bytes accessed | tf_op | source)
XLA Modules:
  0.0 84.7 jit_solution(2571537694094011394)
XLA Ops:
  0.5 2.0 %split.1 = (f32[8,32,256]{2,1,0:T(8,128)}, f32[8,32,256]{2,1,0:T(8,128)}) custom-call(f32[32,8,2,256]{3,2,1,0:T(2,128)} %fields.1), custom_call_target="tpu_custom_call" | custom-call | tf_op jit(solution)/shard_map/split/pallas_call | solution.py:20
  2.5 1.7 %collective-permute-done.other = f32[8,32,256]{2,1,0:T(8,128)S(1)} collective-permute-done((f32[8,32,256]{2,1,0:T(8,128)}, f32[8,32,256]{2,1,0:T(8,128)S(1)}, u32[]{:S(2)}, u32[]{:S(2)}) %collective-permute-start) | collective-permute-done | bytes 262176 | tf_op jit(solution)/shard_map/ppermute | solution.py:37
  5.0 2.0 %modal.1 = (f32[8,64,256]{2,1,0:T(8,128)}, bf16[8,64,256]{2,1,0:T(8,128)(2,1)}) custom-call(f32[8,32,256]{2,1,0:T(8,128)} %get-tuple-element.23.own, f32[8,32,256]{2,1,0:T(8,128)} %copy-done.7), custom_call_target="tpu_custom_call" | custom-call | tf_op jit(solution)/shard_map/modal/pallas_call | solution.py:20
  6.9 2.6 %collective-permute-start.2 = (bf16[8,64,256]{2,1,0:T(8,128)(2,1)}, bf16[8,64,256]{2,1,0:T(8,128)(2,1)S(1)}, u32[]{:S(2)}, u32[]{:S(2)}) collective-permute-start(bf16[8,64,256]{2,1,0:T(8,128)(2,1)} %get-tuple-element.26.refs_4_), channel_id=1, source_target_pairs={{0,8},{4,12},{8,0},{12,4},{16,24},{20,28},{24,16},{28,20},{1,9},{5... | collective-permute-start | bytes 786440 | tf_op jit(solution)/shard_map/ppermute | solution.py:37
  9.5 1.5 %collective-permute-start.3 = (bf16[8,64,256]{2,1,0:T(8,128)(2,1)}, bf16[8,64,256]{2,1,0:T(8,128)(2,1)S(1)}, u32[]{:S(2)}, u32[]{:S(2)}) collective-permute-start(bf16[8,64,256]{2,1,0:T(8,128)(2,1)} %get-tuple-element.26.refs_4_), channel_id=1, source_target_pairs={{0,16},{4,20},{8,24},{12,28},{16,0},{20,4},{24,8},{28,12},{1,17},{... | collective-permute-start | bytes 786440 | tf_op jit(solution)/shard_map/ppermute | solution.py:37
  11.1 2.5 %turn.2.refs_2_ = bf16[256,2048]{1,0:T(8,128)(2,1)} custom-call(bf16[2048,256]{1,0:T(8,128)(2,1)} %refs_0_.1), custom_call_target="tpu_custom_call" | custom-call | tf_op jit(solution)/shard_map/turn/pallas_call | solution.py:20
  13.6 1.0 %copy-done = bf16[2048,256]{1,0:T(8,128)(2,1)} copy-done((bf16[2048,256]{1,0:T(8,128)(2,1)}, bf16[2048,256]{1,0:T(8,128)(2,1)S(1)}, u32[]{:S(2)}) %copy-start) | copy-done | bytes 1048600
  14.6 2.6 %turn.3.refs_3_ = bf16[256,2048]{1,0:T(8,128)(2,1)} custom-call(bf16[2048,256]{1,0:T(8,128)(2,1)} %copy-done), custom_call_target="tpu_custom_call" | custom-call | tf_op jit(solution)/shard_map/turn/pallas_call | solution.py:20
  17.2 6.5 %collective-permute-done.3.refs_6_ = bf16[8,64,256]{2,1,0:T(8,128)(2,1)S(1)} collective-permute-done((bf16[8,64,256]{2,1,0:T(8,128)(2,1)}, bf16[8,64,256]{2,1,0:T(8,128)(2,1)S(1)}, u32[]{:S(2)}, u32[]{:S(2)}) %collective-permute-start.3) | collective-permute-done | bytes 262176 | tf_op jit(solution)/shard_map/ppermute | solution.py:37
  24.4 0.7 copy-done.6
  25.1 13.0 %kerr.1 = (f32[8,64,256]{2,1,0:T(8,128)}, bf16[8,64,256]{2,1,0:T(8,128)(2,1)}, bf16[8,64,256]{2,1,0:T(8,128)(2,1)}, bf16[8,64,256]{2,1,0:T(8,128)(2,1)}) custom-call(bf16[2048,256]{1,0:T(8,128)(2,1)} %refs_0_.1, bf16[2048,256]{1,0:T(8,128)(2,1)} %copy-done, bf16[256,2048]{1,0:T(8,128)(2,1)} %turn.2.refs_2_, bf16[256,2048]{1,0:T(8,128)(2,1)} %turn.3.refs_3_, ...), custom_call_target="tpu_custom_call" | custom-call | tf_op jit(solution)/shard_map/kerr/pallas_call | solution.py:20
  38.6 1.5 %collective-permute-start.6 = (bf16[8,64,256]{2,1,0:T(8,128)(2,1)}, bf16[8,64,256]{2,1,0:T(8,128)(2,1)S(1)}, u32[]{:S(2)}, u32[]{:S(2)}) collective-permute-start(bf16[8,64,256]{2,1,0:T(8,128)(2,1)} %get-tuple-element.29), channel_id=1, source_target_pairs={{0,16},{4,20},{8,24},{12,28},{16,0},{20,4},{24,8},{28,12},{1,17},{... | collective-permute-start | bytes 786440 | tf_op jit(solution)/shard_map/ppermute | solution.py:37
  40.1 1.4 %collective-permute-start.7 = (bf16[8,64,256]{2,1,0:T(8,128)(2,1)}, bf16[8,64,256]{2,1,0:T(8,128)(2,1)S(1)}, u32[]{:S(2)}, u32[]{:S(2)}) collective-permute-start(bf16[8,64,256]{2,1,0:T(8,128)(2,1)} %get-tuple-element.30), channel_id=1, source_target_pairs={{0,24},{4,28},{8,16},{12,20},{16,8},{20,12},{24,0},{28,4},{1,25},{... | collective-permute-start | bytes 786440 | tf_op jit(solution)/shard_map/ppermute | solution.py:37
  41.6 1.2 %collective-permute-done.11 = f32[8,1024]{1,0:T(8,128)S(1)} collective-permute-done((f32[8,1024]{1,0:T(8,128)S(1)}, f32[8,1024]{1,0:T(8,128)S(1)}, u32[]{:S(2)}, u32[]{:S(2)}) %collective-permute-start.11) | collective-permute-done | bytes 32800 | tf_op jit(solution)/shard_map/ppermute | solution.py:37
  42.8 4.7 %collective-permute-done.5.refs_1_ = bf16[8,64,256]{2,1,0:T(8,128)(2,1)S(1)} collective-permute-done((bf16[8,64,256]{2,1,0:T(8,128)(2,1)}, bf16[8,64,256]{2,1,0:T(8,128)(2,1)S(1)}, u32[]{:S(2)}, u32[]{:S(2)}) %collective-permute-start.5) | collective-permute-done | bytes 262176 | tf_op jit(solution)/shard_map/ppermute | solution.py:37
  47.4 3.1 %collective-permute-done.6.refs_2_ = bf16[8,64,256]{2,1,0:T(8,128)(2,1)S(1)} collective-permute-done((bf16[8,64,256]{2,1,0:T(8,128)(2,1)}, bf16[8,64,256]{2,1,0:T(8,128)(2,1)S(1)}, u32[]{:S(2)}, u32[]{:S(2)}) %collective-permute-start.6) | collective-permute-done | bytes 262176 | tf_op jit(solution)/shard_map/ppermute | solution.py:37
  50.5 1.8 %collective-permute-done.7.refs_3_ = bf16[8,64,256]{2,1,0:T(8,128)(2,1)S(1)} collective-permute-done((bf16[8,64,256]{2,1,0:T(8,128)(2,1)}, bf16[8,64,256]{2,1,0:T(8,128)(2,1)S(1)}, u32[]{:S(2)}, u32[]{:S(2)}) %collective-permute-start.7) | collective-permute-done | bytes 262176 | tf_op jit(solution)/shard_map/ppermute | solution.py:37
  53.0 2.3 %step.1 = (f32[8,16,256]{2,1,0:T(8,128)}, bf16[8,16,256]{2,1,0:T(8,128)(2,1)}, bf16[8,16,256]{2,1,0:T(8,128)(2,1)}, bf16[8,16,256]{2,1,0:T(8,128)(2,1)}) custom-call(f32[8,64,256]{2,1,0:T(8,128)} %get-tuple-element.25.full, f32[8,64,256]{2,1,0:T(8,128)} %get-tuple-element.27.refs_0_, bf16[8,64,256]{2,1,0:T(8,128)(2,1)} %copy-done.1, ...), custom_call_target="tpu_custom_call" | custom-call | tf_op jit(solution)/shard_map/step/pallas_call | solution.py:20
  55.3 1.6 %collective-permute-start.8 = (bf16[8,16,256]{2,1,0:T(8,128)(2,1)}, bf16[8,16,256]{2,1,0:T(8,128)(2,1)S(1)}, u32[]{:S(2)}, u32[]{:S(2)}) collective-permute-start(bf16[8,16,256]{2,1,0:T(8,128)(2,1)} %get-tuple-element.32), channel_id=1, source_target_pairs={{0,1},{1,0},{2,3},{3,2},{4,5},{5,4},{6,7},{7,6},{8,9},{9,8},{10,11... | collective-permute-start | bytes 196616 | tf_op jit(solution)/shard_map/ppermute | solution.py:41
  56.9 2.6 %collective-permute-start.9 = (bf16[8,16,256]{2,1,0:T(8,128)(2,1)}, bf16[8,16,256]{2,1,0:T(8,128)(2,1)S(1)}, u32[]{:S(2)}, u32[]{:S(2)}) collective-permute-start(bf16[8,16,256]{2,1,0:T(8,128)(2,1)} %get-tuple-element.33), channel_id=1, source_target_pairs={{0,2},{1,3},{2,0},{3,1},{4,6},{5,7},{6,4},{7,5},{8,10},{9,11},{10,... | collective-permute-start | bytes 196616 | tf_op jit(solution)/shard_map/ppermute | solution.py:41
  60.1 0.8 copy.11
  61.1 0.8 copy.13
  62.0 1.7 %collective-permute-done.9.refs_2_ = bf16[8,16,256]{2,1,0:T(8,128)(2,1)S(1)} collective-permute-done((bf16[8,16,256]{2,1,0:T(8,128)(2,1)}, bf16[8,16,256]{2,1,0:T(8,128)(2,1)S(1)}, u32[]{:S(2)}, u32[]{:S(2)}) %collective-permute-start.9) | collective-permute-done | bytes 65568 | tf_op jit(solution)/shard_map/ppermute | solution.py:41
  63.7 2.1 %collective-permute-done.10.refs_3_ = bf16[8,16,256]{2,1,0:T(8,128)(2,1)S(1)} collective-permute-done((bf16[8,16,256]{2,1,0:T(8,128)(2,1)}, bf16[8,16,256]{2,1,0:T(8,128)(2,1)S(1)}, u32[]{:S(2)}, u32[]{:S(2)}) %collective-permute-start.10) | collective-permute-done | bytes 65568 | tf_op jit(solution)/shard_map/ppermute | solution.py:41
  66.4 3.7 %wave.1 = (f32[8,16,256]{2,1,0:T(8,128)}, bf16[8,16,256]{2,1,0:T(8,128)(2,1)}, bf16[8,16,256]{2,1,0:T(8,128)(2,1)}, bf16[8,16,256]{2,1,0:T(8,128)(2,1)}) custom-call(f32[8,16,256]{2,1,0:T(8,128)} %get-tuple-element.31.refs_0_, bf16[8,16,256]{2,1,0:T(8,128)(2,1)} %copy-done.12, bf16[8,16,256]{2,1,0:T(8,128)(2,1)} %copy-done.13, ...), custom_call_target="tpu_custom_call" | custom-call | tf_op jit(solution)/shard_map/wave/pallas_call | solution.py:20
  70.1 1.4 %collective-permute-start.13 = (bf16[8,16,256]{2,1,0:T(8,128)(2,1)}, bf16[8,16,256]{2,1,0:T(8,128)(2,1)S(1)}, u32[]{:S(2)}, u32[]{:S(2)}) collective-permute-start(bf16[8,16,256]{2,1,0:T(8,128)(2,1)} %get-tuple-element.37), channel_id=1, source_target_pairs={{0,2},{1,3},{2,0},{3,1},{4,6},{5,7},{6,4},{7,5},{8,10},{9,11},{10,... | collective-permute-start | bytes 196616 | tf_op jit(solution)/shard_map/ppermute | solution.py:41
  71.5 3.0 %collective-permute-start.14 = (bf16[8,16,256]{2,1,0:T(8,128)(2,1)}, bf16[8,16,256]{2,1,0:T(8,128)(2,1)S(1)}, u32[]{:S(2)}, u32[]{:S(2)}) collective-permute-start(bf16[8,16,256]{2,1,0:T(8,128)(2,1)} %get-tuple-element.38), channel_id=1, source_target_pairs={{0,3},{1,2},{2,1},{3,0},{4,7},{5,6},{6,5},{7,4},{8,11},{9,10},{10,... | collective-permute-start | bytes 196616 | tf_op jit(solution)/shard_map/ppermute | solution.py:41
  74.6 1.0 %collective-permute-done.13.refs_2_ = bf16[8,16,256]{2,1,0:T(8,128)(2,1)S(1)} collective-permute-done((bf16[8,16,256]{2,1,0:T(8,128)(2,1)}, bf16[8,16,256]{2,1,0:T(8,128)(2,1)S(1)}, u32[]{:S(2)}, u32[]{:S(2)}) %collective-permute-start.13) | collective-permute-done | bytes 65568 | tf_op jit(solution)/shard_map/ppermute | solution.py:41
  75.6 2.2 %collective-permute-done.14.refs_3_ = bf16[8,16,256]{2,1,0:T(8,128)(2,1)S(1)} collective-permute-done((bf16[8,16,256]{2,1,0:T(8,128)(2,1)}, bf16[8,16,256]{2,1,0:T(8,128)(2,1)S(1)}, u32[]{:S(2)}, u32[]{:S(2)}) %collective-permute-start.14) | collective-permute-done | bytes 65568 | tf_op jit(solution)/shard_map/ppermute | solution.py:41
  78.4 1.8 %part.1 = (f32[8,32,256]{2,1,0:T(8,128)}, f32[8,32,256]{2,1,0:T(8,128)}) custom-call(f32[8,16,256]{2,1,0:T(8,128)} %get-tuple-element.35.refs_0_, bf16[8,16,256]{2,1,0:T(8,128)(2,1)} %copy-done.9, bf16[8,16,256]{2,1,0:T(8,128)(2,1)} %copy-done.10, bf16[8,16,256]{2,1,0:T(8,128)(2,1)} %copy-done.11), custom_call_target="tpu_custom_call" | custom-call | tf_op jit(solution)/shard_map/part/pallas_call | solution.py:20
  80.2 1.7 %collective-permute-done.15.refs_1_ = f32[8,32,256]{2,1,0:T(8,128)S(1)} collective-permute-done((f32[8,32,256]{2,1,0:T(8,128)}, f32[8,32,256]{2,1,0:T(8,128)S(1)}, u32[]{:S(2)}, u32[]{:S(2)}) %collective-permute-start.15) | collective-permute-done | bytes 262176 | tf_op jit(solution)/shard_map/ppermute | solution.py:37
  82.7 2.0 %join.1 = f32[32,8,2,256]{3,2,1,0:T(2,128)} custom-call(f32[8,32,256]{2,1,0:T(8,128)} %get-tuple-element.39.refs_0_, f32[8,32,256]{2,1,0:T(8,128)} %copy-done.8), custom_call_target="tpu_custom_call" | custom-call | tf_op jit(solution)/shard_map/join/pallas_call | solution.py:20
  (47 shorter events, 6.0 us)
Async XLA Ops:
  0.0 13.6 %collective-permute-start.1 = (bf16[2048,256]{1,0:T(8,128)(2,1)}, bf16[2048,256]{1,0:T(8,128)(2,1)S(1)}, u32[]{:S(2)}, u32[]{:S(2)}) collective-permute-start(bf16[2048,256]{1,0:T(8,128)(2,1)} %refs_0_.1), channel_id=1, source_target_pairs={{0,4},{4,0},{8,12},{12,8},{16,20},{20,16},{24,28},{28,24},{1,5},{5... | collective-permute-start | bytes 3145736 | tf_op jit(solution)/shard_map/ppermute | solution.py:37
  2.5 1.7 %collective-permute-start = (f32[8,32,256]{2,1,0:T(8,128)}, f32[8,32,256]{2,1,0:T(8,128)S(1)}, u32[]{:S(2)}, u32[]{:S(2)}) collective-permute-start(f32[8,32,256]{2,1,0:T(8,128)} %get-tuple-element.24), channel_id=1, source_target_pairs={{0,4},{4,0},{8,12},{12,8},{16,20},{20,16},{24,28},{28,24},{1,5},{5... | collective-permute-start | bytes 786440 | tf_op jit(solution)/shard_map/ppermute | solution.py:37
  4.3 0.7 copy-start.7
  6.9 10.2 %collective-permute-start.2 = (bf16[8,64,256]{2,1,0:T(8,128)(2,1)}, bf16[8,64,256]{2,1,0:T(8,128)(2,1)S(1)}, u32[]{:S(2)}, u32[]{:S(2)}) collective-permute-start(bf16[8,64,256]{2,1,0:T(8,128)(2,1)} %get-tuple-element.26.refs_4_), channel_id=1, source_target_pairs={{0,8},{4,12},{8,0},{12,4},{16,24},{20,28},{24,16},{28,20},{1,9},{5... | collective-permute-start | bytes 786440 | tf_op jit(solution)/shard_map/ppermute | solution.py:37
  9.5 14.1 %collective-permute-start.3 = (bf16[8,64,256]{2,1,0:T(8,128)(2,1)}, bf16[8,64,256]{2,1,0:T(8,128)(2,1)S(1)}, u32[]{:S(2)}, u32[]{:S(2)}) collective-permute-start(bf16[8,64,256]{2,1,0:T(8,128)(2,1)} %get-tuple-element.26.refs_4_), channel_id=1, source_target_pairs={{0,16},{4,20},{8,24},{12,28},{16,0},{20,4},{24,8},{28,12},{1,17},{... | collective-permute-start | bytes 786440 | tf_op jit(solution)/shard_map/ppermute | solution.py:37
  11.1 12.6 %collective-permute-start.4 = (bf16[8,64,256]{2,1,0:T(8,128)(2,1)}, bf16[8,64,256]{2,1,0:T(8,128)(2,1)S(1)}, u32[]{:S(2)}, u32[]{:S(2)}) collective-permute-start(bf16[8,64,256]{2,1,0:T(8,128)(2,1)} %get-tuple-element.26.refs_4_), channel_id=1, source_target_pairs={{0,24},{4,28},{8,16},{12,20},{16,8},{20,12},{24,0},{28,4},{1,25},{... | collective-permute-start | bytes 786440 | tf_op jit(solution)/shard_map/ppermute | solution.py:37
  13.6 1.0 %copy-start = (bf16[2048,256]{1,0:T(8,128)(2,1)}, bf16[2048,256]{1,0:T(8,128)(2,1)S(1)}, u32[]{:S(2)}) copy-start(bf16[2048,256]{1,0:T(8,128)(2,1)S(1)} %collective-permute-done.1.profiles.refs_1_) | copy-start | bytes 3145732
  17.2 24.4 %copy-start.15 = (f32[8,1024]{1,0:T(8,128)S(1)}, f32[8,1024]{1,0:T(8,128)}, u32[]{:S(2)}) copy-start(f32[8,1024]{1,0:T(8,128)} %param.11) | copy-start | bytes 98308
  17.2 6.5 %copy-start.4 = (bf16[8,64,256]{2,1,0:T(8,128)(2,1)}, bf16[8,64,256]{2,1,0:T(8,128)(2,1)S(1)}, u32[]{:S(2)}) copy-start(bf16[8,64,256]{2,1,0:T(8,128)(2,1)S(1)} %collective-permute-done.2.refs_5_) | copy-start | bytes 786436
  23.7 0.7 copy-start.5
  24.4 0.7 copy-start.6
  38.1 9.4 %collective-permute-start.5 = (bf16[8,64,256]{2,1,0:T(8,128)(2,1)}, bf16[8,64,256]{2,1,0:T(8,128)(2,1)S(1)}, u32[]{:S(2)}, u32[]{:S(2)}) collective-permute-start(bf16[8,64,256]{2,1,0:T(8,128)(2,1)} %get-tuple-element.28), channel_id=1, source_target_pairs={{0,8},{4,12},{8,0},{12,4},{16,24},{20,28},{24,16},{28,20},{1,9},{5... | collective-permute-start | bytes 786440 | tf_op jit(solution)/shard_map/ppermute | solution.py:37
  38.6 11.9 %collective-permute-start.6 = (bf16[8,64,256]{2,1,0:T(8,128)(2,1)}, bf16[8,64,256]{2,1,0:T(8,128)(2,1)S(1)}, u32[]{:S(2)}, u32[]{:S(2)}) collective-permute-start(bf16[8,64,256]{2,1,0:T(8,128)(2,1)} %get-tuple-element.29), channel_id=1, source_target_pairs={{0,16},{4,20},{8,24},{12,28},{16,0},{20,4},{24,8},{28,12},{1,17},{... | collective-permute-start | bytes 786440 | tf_op jit(solution)/shard_map/ppermute | solution.py:37
  40.1 12.2 %collective-permute-start.7 = (bf16[8,64,256]{2,1,0:T(8,128)(2,1)}, bf16[8,64,256]{2,1,0:T(8,128)(2,1)S(1)}, u32[]{:S(2)}, u32[]{:S(2)}) collective-permute-start(bf16[8,64,256]{2,1,0:T(8,128)(2,1)} %get-tuple-element.30), channel_id=1, source_target_pairs={{0,24},{4,28},{8,16},{12,20},{16,8},{20,12},{24,0},{28,4},{1,25},{... | collective-permute-start | bytes 786440 | tf_op jit(solution)/shard_map/ppermute | solution.py:37
  41.5 1.2 %collective-permute-start.11 = (f32[8,1024]{1,0:T(8,128)S(1)}, f32[8,1024]{1,0:T(8,128)S(1)}, u32[]{:S(2)}, u32[]{:S(2)}) collective-permute-start(f32[8,1024]{1,0:T(8,128)S(1)} %copy-done.15), channel_id=1, source_target_pairs={{0,4},{4,0},{8,12},{12,8},{16,20},{20,16},{24,28},{28,24},{1,5},{5... | collective-permute-start | bytes 98312 | tf_op jit(solution)/shard_map/ppermute | solution.py:37
  47.4 4.9 %copy-start.1 = (bf16[8,64,256]{2,1,0:T(8,128)(2,1)}, bf16[8,64,256]{2,1,0:T(8,128)(2,1)S(1)}, u32[]{:S(2)}) copy-start(bf16[8,64,256]{2,1,0:T(8,128)(2,1)S(1)} %collective-permute-done.5.refs_1_) | copy-start | bytes 786436
  50.5 1.8 %copy-start.2 = (bf16[8,64,256]{2,1,0:T(8,128)(2,1)}, bf16[8,64,256]{2,1,0:T(8,128)(2,1)S(1)}, u32[]{:S(2)}) copy-start(bf16[8,64,256]{2,1,0:T(8,128)(2,1)S(1)} %collective-permute-done.6.refs_2_) | copy-start | bytes 786436
  52.3 0.7 copy-start.3
  55.3 6.7 %collective-permute-start.8 = (bf16[8,16,256]{2,1,0:T(8,128)(2,1)}, bf16[8,16,256]{2,1,0:T(8,128)(2,1)S(1)}, u32[]{:S(2)}, u32[]{:S(2)}) collective-permute-start(bf16[8,16,256]{2,1,0:T(8,128)(2,1)} %get-tuple-element.32), channel_id=1, source_target_pairs={{0,1},{1,0},{2,3},{3,2},{4,5},{5,4},{6,7},{7,6},{8,9},{9,8},{10,11... | collective-permute-start | bytes 196616 | tf_op jit(solution)/shard_map/ppermute | solution.py:41
  56.9 6.8 %collective-permute-start.9 = (bf16[8,16,256]{2,1,0:T(8,128)(2,1)}, bf16[8,16,256]{2,1,0:T(8,128)(2,1)S(1)}, u32[]{:S(2)}, u32[]{:S(2)}) collective-permute-start(bf16[8,16,256]{2,1,0:T(8,128)(2,1)} %get-tuple-element.33), channel_id=1, source_target_pairs={{0,2},{1,3},{2,0},{3,1},{4,6},{5,7},{6,4},{7,5},{8,10},{9,11},{10,... | collective-permute-start | bytes 196616 | tf_op jit(solution)/shard_map/ppermute | solution.py:41
  59.5 6.3 %collective-permute-start.10 = (bf16[8,16,256]{2,1,0:T(8,128)(2,1)}, bf16[8,16,256]{2,1,0:T(8,128)(2,1)S(1)}, u32[]{:S(2)}, u32[]{:S(2)}) collective-permute-start(bf16[8,16,256]{2,1,0:T(8,128)(2,1)} %get-tuple-element.34), channel_id=1, source_target_pairs={{0,3},{1,2},{2,1},{3,0},{4,7},{5,6},{6,5},{7,4},{8,11},{9,10},{10,... | collective-permute-start | bytes 196616 | tf_op jit(solution)/shard_map/ppermute | solution.py:41
  62.0 3.8 %copy-start.12 = (bf16[8,16,256]{2,1,0:T(8,128)(2,1)}, bf16[8,16,256]{2,1,0:T(8,128)(2,1)S(1)}, u32[]{:S(2)}) copy-start(bf16[8,16,256]{2,1,0:T(8,128)(2,1)S(1)} %collective-permute-done.8.refs_1_) | copy-start | bytes 196612
  63.7 2.1 %copy-start.13 = (bf16[8,16,256]{2,1,0:T(8,128)(2,1)}, bf16[8,16,256]{2,1,0:T(8,128)(2,1)S(1)}, u32[]{:S(2)}) copy-start(bf16[8,16,256]{2,1,0:T(8,128)(2,1)S(1)} %collective-permute-done.9.refs_2_) | copy-start | bytes 196612
  65.8 0.6 copy-start.14
  70.1 4.5 %collective-permute-start.12 = (bf16[8,16,256]{2,1,0:T(8,128)(2,1)}, bf16[8,16,256]{2,1,0:T(8,128)(2,1)S(1)}, u32[]{:S(2)}, u32[]{:S(2)}) collective-permute-start(bf16[8,16,256]{2,1,0:T(8,128)(2,1)} %get-tuple-element.36), channel_id=1, source_target_pairs={{0,1},{1,0},{2,3},{3,2},{4,5},{5,4},{6,7},{7,6},{8,9},{9,8},{10,11... | collective-permute-start | bytes 196616 | tf_op jit(solution)/shard_map/ppermute | solution.py:41
  70.1 5.4 %collective-permute-start.13 = (bf16[8,16,256]{2,1,0:T(8,128)(2,1)}, bf16[8,16,256]{2,1,0:T(8,128)(2,1)S(1)}, u32[]{:S(2)}, u32[]{:S(2)}) collective-permute-start(bf16[8,16,256]{2,1,0:T(8,128)(2,1)} %get-tuple-element.37), channel_id=1, source_target_pairs={{0,2},{1,3},{2,0},{3,1},{4,6},{5,7},{6,4},{7,5},{8,10},{9,11},{10,... | collective-permute-start | bytes 196616 | tf_op jit(solution)/shard_map/ppermute | solution.py:41
  71.5 6.3 %collective-permute-start.14 = (bf16[8,16,256]{2,1,0:T(8,128)(2,1)}, bf16[8,16,256]{2,1,0:T(8,128)(2,1)S(1)}, u32[]{:S(2)}, u32[]{:S(2)}) collective-permute-start(bf16[8,16,256]{2,1,0:T(8,128)(2,1)} %get-tuple-element.38), channel_id=1, source_target_pairs={{0,3},{1,2},{2,1},{3,0},{4,7},{5,6},{6,5},{7,4},{8,11},{9,10},{10,... | collective-permute-start | bytes 196616 | tf_op jit(solution)/shard_map/ppermute | solution.py:41
  74.6 3.2 %copy-start.9 = (bf16[8,16,256]{2,1,0:T(8,128)(2,1)}, bf16[8,16,256]{2,1,0:T(8,128)(2,1)S(1)}, u32[]{:S(2)}) copy-start(bf16[8,16,256]{2,1,0:T(8,128)(2,1)S(1)} %collective-permute-done.12.refs_1_) | copy-start | bytes 196612
  75.6 2.2 %copy-start.10 = (bf16[8,16,256]{2,1,0:T(8,128)(2,1)}, bf16[8,16,256]{2,1,0:T(8,128)(2,1)S(1)}, u32[]{:S(2)}) copy-start(bf16[8,16,256]{2,1,0:T(8,128)(2,1)S(1)} %collective-permute-done.13.refs_2_) | copy-start | bytes 196612
  77.8 0.6 copy-start.11
  80.2 1.7 %collective-permute-start.15 = (f32[8,32,256]{2,1,0:T(8,128)}, f32[8,32,256]{2,1,0:T(8,128)S(1)}, u32[]{:S(2)}, u32[]{:S(2)}) collective-permute-start(f32[8,32,256]{2,1,0:T(8,128)} %get-tuple-element.40), channel_id=1, source_target_pairs={{0,4},{4,0},{8,12},{12,8},{16,20},{20,16},{24,28},{28,24},{1,5},{5... | collective-permute-start | bytes 786440 | tf_op jit(solution)/shard_map/ppermute | solution.py:37
  82.0 0.7 copy-start.8
where the time goes:
time: 85 us; the launch traced here: 84.7 us
  Pallas kernels  32 us (38%)
  waiting for transfers between devices  27.8 us (33%)
  starting transfers between devices  16.9 us (20%)
  local copies, waits for them, and re-layouts  7.71 us (9%)
    pallas_call x9, Pallas kernels, run(): pl.pallas_call(kernel, out_shape=tuple((jax.ShapeDtypeStruct(*out) for ou...  32 us
    ppermute x10, waiting for transfers between devices, swap_pix(): return lax.ppermute(value, 'pix', [(i, i ^ mask) for i in range(size)])  20.7 us
    ppermute x6, starting transfers between devices, swap_tm(): return lax.ppermute(value, 'tm', [(i, i ^ mask) for i in range(size)])  8.77 us
    ppermute x10, starting transfers between devices, swap_pix(): return lax.ppermute(value, 'pix', [(i, i ^ mask) for i in range(size)])  8.14 us
    ppermute x6, waiting for transfers between devices, swap_tm(): return lax.ppermute(value, 'tm', [(i, i ^ mask) for i in range(size)])  7.04 us
    unnamed x32, local copies, waits for them, and re-layouts  5.7 us
  transfers between devices with their start and end apart: 16, of which 12 were waited for; matrix products, arithmetic and copies ran while one was open for 3% of the time, Pallas kernels for 11%

commit v1 on v0

--- a/solution.py
+++ b/solution.py
@@ -15,18 +15,23 @@
 VMEM = pl.BlockSpec(memory_space=pltpu.VMEM)
 
 
-def call(kernel, name, outs, scratch=(), cost=None):
+def size_of(shape, dtype):
+    return math.prod(shape) * jnp.dtype(dtype).itemsize
+
+
+def call(kernel, name, outs, scratch=(), flops=0):
     def run(*args):
+        moved = sum(size_of(item.shape, item.dtype) for item in args)
+        moved += sum(size_of(*out) for out in outs)
+        held = sum(size_of(*item) for item in scratch)
         return pl.pallas_call(
             kernel,
             out_shape=tuple(jax.ShapeDtypeStruct(*out) for out in outs),
             in_specs=[VMEM] * len(args),
             out_specs=tuple(VMEM for _ in outs),
             scratch_shapes=[pltpu.VMEM(*item) for item in scratch],
-            compiler_params=pltpu.CompilerParams(vmem_limit_bytes=56 * 2**20),
-            cost_estimate=None
-            if cost is None
-            else pl.CostEstimate(flops=cost[0], bytes_accessed=cost[1], transcendentals=0),
+            compiler_params=pltpu.CompilerParams(vmem_limit_bytes=moved + held + 3 * 2**20),
+            cost_estimate=pl.CostEstimate(flops=flops, bytes_accessed=moved, transcendentals=0),
             name=name,
         )(*args)
 

time: 85 us -> 66.3 us (0.78)
  Pallas kernels: 32 us -> 13.4 us
  local copies, waits for them, and re-layouts: 7.71 us -> 1.86 us
  waiting for transfers between devices: 27.8 us -> 32.8 us
    pallas_call x9, Pallas kernels: 32 us -> 13.4 us  [run(): pl.pallas_call(kernel, out_shape=tuple((jax.ShapeDtypeStruct(*out) for ou...]
    unnamed x32 -> x18, local copies, waits for them, and re-layouts: 5.7 us -> 1.09 us
    ppermute x10, waiting for transfers between devices: 20.7 us -> 25 us  [swap_pix(): return lax.ppermute(value, 'pix', [(i, i ^ mask) for i in range(size)])]
  transfers between devices with their start and end apart: 16 -> 16, of which waited for: 12 -> 11; matrix products, arithmetic and copies ran while one was open for 3% -> 2% of each run, Pallas kernels for 11% -> 1%
where the time goes in v1:
time: 66.3 us; the launch traced here: 66.1 us
  waiting for transfers between devices  32.8 us (49%)
  starting transfers between devices  17.6 us (27%)
  Pallas kernels  13.4 us (20%)
  local copies, waits for them, and re-layouts  1.86 us (3%)
    ppermute x10, waiting for transfers between devices, swap_pix(): return lax.ppermute(value, 'pix', [(i, i ^ mask) for i in range(size)])  25 us
    pallas_call x9, Pallas kernels, run(): pl.pallas_call(kernel, out_shape=tuple((jax.ShapeDtypeStruct(*out) for ou...  13.4 us
    ppermute x6, starting transfers between devices, swap_tm(): return lax.ppermute(value, 'tm', [(i, i ^ mask) for i in range(size)])  8.9 us
    ppermute x10, starting transfers between devices, swap_pix(): return lax.ppermute(value, 'pix', [(i, i ^ mask) for i in range(size)])  8.74 us
    ppermute x6, waiting for transfers between devices, swap_tm(): return lax.ppermute(value, 'tm', [(i, i ^ mask) for i in range(size)])  7.79 us
  transfers between devices with their start and end apart: 16, of which 11 were waited for; matrix products, arithmetic and copies ran while one was open for 2% of the time, Pallas kernels for 1%

profile of v1, /device:TPU:0, one launch (start us, length us, event | category | flops | bytes accessed | tf_op | source)
XLA Modules:
  0.0 66.1 jit_solution(5456653333547845314)
XLA Ops:
  0.0 0.5 collective-permute-start.1
  0.5 1.0 %copy-done.1 = f32[32,8,2,256]{3,2,1,0:T(2,128)S(1)} copy-done((f32[32,8,2,256]{3,2,1,0:T(2,128)S(1)}, f32[32,8,2,256]{3,2,1,0:T(2,128)}, u32[]{:S(2)}) %copy-start.1) | copy-done | bytes 524312
  1.5 0.2 split.1
  1.9 1.5 %collective-permute-done.other = f32[8,32,256]{2,1,0:T(8,128)S(1)} collective-permute-done((f32[8,32,256]{2,1,0:T(8,128)S(1)}, f32[8,32,256]{2,1,0:T(8,128)S(1)}, u32[]{:S(2)}, u32[]{:S(2)}) %collective-permute-start) | collective-permute-done | bytes 262176 | tf_op jit(solution)/shard_map/ppermute | solution.py:42
  3.4 2.9 %collective-permute-start.2 = (bf16[8,64,256]{2,1,0:T(8,128)(2,1)S(1)}, bf16[8,64,256]{2,1,0:T(8,128)(2,1)S(1)}, u32[]{:S(2)}, u32[]{:S(2)}) collective-permute-start(bf16[8,64,256]{2,1,0:T(8,128)(2,1)S(1)} %get-tuple-element.26.refs_4_), channel_id=1, source_target_pairs={{0,8},{4,12},{8,0},{12,4},{16,24},{20,28},{24,16},{28,20},{1,9},{5... | collective-permute-start | bytes 786440 | tf_op jit(solution)/shard_map/ppermute | solution.py:42
  6.4 1.5 %collective-permute-start.3 = (bf16[8,64,256]{2,1,0:T(8,128)(2,1)S(1)}, bf16[8,64,256]{2,1,0:T(8,128)(2,1)S(1)}, u32[]{:S(2)}, u32[]{:S(2)}) collective-permute-start(bf16[8,64,256]{2,1,0:T(8,128)(2,1)S(1)} %get-tuple-element.26.refs_4_), channel_id=1, source_target_pairs={{0,16},{4,20},{8,24},{12,28},{16,0},{20,4},{24,8},{28,12},{1,17},{... | collective-permute-start | bytes 786440 | tf_op jit(solution)/shard_map/ppermute | solution.py:42
  7.9 0.3 turn.2.refs_2_
  8.3 0.3 turn.3.refs_3_
  8.6 4.9 %collective-permute-done.2.refs_5_ = bf16[8,64,256]{2,1,0:T(8,128)(2,1)S(1)} collective-permute-done((bf16[8,64,256]{2,1,0:T(8,128)(2,1)S(1)}, bf16[8,64,256]{2,1,0:T(8,128)(2,1)S(1)}, u32[]{:S(2)}, u32[]{:S(2)}) %collective-permute-start.2) | collective-permute-done | bytes 262176 | tf_op jit(solution)/shard_map/ppermute | solution.py:42
  13.5 6.5 %collective-permute-done.3.refs_6_ = bf16[8,64,256]{2,1,0:T(8,128)(2,1)S(1)} collective-permute-done((bf16[8,64,256]{2,1,0:T(8,128)(2,1)S(1)}, bf16[8,64,256]{2,1,0:T(8,128)(2,1)S(1)}, u32[]{:S(2)}, u32[]{:S(2)}) %collective-permute-start.3) | collective-permute-done | bytes 262176 | tf_op jit(solution)/shard_map/ppermute | solution.py:42
  20.0 9.5 %kerr.1 = (f32[8,64,256]{2,1,0:T(8,128)S(1)}, bf16[8,64,256]{2,1,0:T(8,128)(2,1)S(1)}, bf16[8,64,256]{2,1,0:T(8,128)(2,1)S(1)}, bf16[8,64,256]{2,1,0:T(8,128)(2,1)S(1)}) custom-call(bf16[2048,256]{1,0:T(8,128)(2,1)S(1)} %copy-done, bf16[2048,256]{1,0:T(8,128)(2,1)S(1)} %collective-permute-done.1.profiles.refs_1_, bf16[256,2048]{1,0:T(8,128)(2,1)S(1)} %turn.2.refs_2_, ...), custom_call_target="tpu_custom_call" | custom-call | bytes 6553600 | tf_op jit(solution)/shard_map/kerr/pallas_call | solution.py:27
  29.5 1.3 %collective-permute-start.5 = (bf16[8,64,256]{2,1,0:T(8,128)(2,1)S(1)}, bf16[8,64,256]{2,1,0:T(8,128)(2,1)S(1)}, u32[]{:S(2)}, u32[]{:S(2)}) collective-permute-start(bf16[8,64,256]{2,1,0:T(8,128)(2,1)S(1)} %get-tuple-element.28), channel_id=1, source_target_pairs={{0,8},{4,12},{8,0},{12,4},{16,24},{20,28},{24,16},{28,20},{1,9},{5... | collective-permute-start | bytes 786440 | tf_op jit(solution)/shard_map/ppermute | solution.py:42
  30.8 0.8 %collective-permute-start.6 = (bf16[8,64,256]{2,1,0:T(8,128)(2,1)S(1)}, bf16[8,64,256]{2,1,0:T(8,128)(2,1)S(1)}, u32[]{:S(2)}, u32[]{:S(2)}) collective-permute-start(bf16[8,64,256]{2,1,0:T(8,128)(2,1)S(1)} %get-tuple-element.29), channel_id=1, source_target_pairs={{0,16},{4,20},{8,24},{12,28},{16,0},{20,4},{24,8},{28,12},{1,17},{... | collective-permute-start | bytes 786440 | tf_op jit(solution)/shard_map/ppermute | solution.py:42
  31.7 1.4 %collective-permute-start.7 = (bf16[8,64,256]{2,1,0:T(8,128)(2,1)S(1)}, bf16[8,64,256]{2,1,0:T(8,128)(2,1)S(1)}, u32[]{:S(2)}, u32[]{:S(2)}) collective-permute-start(bf16[8,64,256]{2,1,0:T(8,128)(2,1)S(1)} %get-tuple-element.30), channel_id=1, source_target_pairs={{0,24},{4,28},{8,16},{12,20},{16,8},{20,12},{24,0},{28,4},{1,25},{... | collective-permute-start | bytes 786440 | tf_op jit(solution)/shard_map/ppermute | solution.py:42
  33.1 1.2 %collective-permute-done.11 = f32[8,1024]{1,0:T(8,128)S(1)} collective-permute-done((f32[8,1024]{1,0:T(8,128)S(1)}, f32[8,1024]{1,0:T(8,128)S(1)}, u32[]{:S(2)}, u32[]{:S(2)}) %collective-permute-start.11) | collective-permute-done | bytes 32800 | tf_op jit(solution)/shard_map/ppermute | solution.py:42
  34.3 4.5 %collective-permute-done.5.refs_1_ = bf16[8,64,256]{2,1,0:T(8,128)(2,1)S(1)} collective-permute-done((bf16[8,64,256]{2,1,0:T(8,128)(2,1)S(1)}, bf16[8,64,256]{2,1,0:T(8,128)(2,1)S(1)}, u32[]{:S(2)}, u32[]{:S(2)}) %collective-permute-start.5) | collective-permute-done | bytes 262176 | tf_op jit(solution)/shard_map/ppermute | solution.py:42
  38.8 4.9 %collective-permute-done.6.refs_2_ = bf16[8,64,256]{2,1,0:T(8,128)(2,1)S(1)} collective-permute-done((bf16[8,64,256]{2,1,0:T(8,128)(2,1)S(1)}, bf16[8,64,256]{2,1,0:T(8,128)(2,1)S(1)}, u32[]{:S(2)}, u32[]{:S(2)}) %collective-permute-start.6) | collective-permute-done | bytes 262176 | tf_op jit(solution)/shard_map/ppermute | solution.py:42
  43.8 1.6 %collective-permute-start.8 = (bf16[8,16,256]{2,1,0:T(8,128)(2,1)S(1)}, bf16[8,16,256]{2,1,0:T(8,128)(2,1)S(1)}, u32[]{:S(2)}, u32[]{:S(2)}) collective-permute-start(bf16[8,16,256]{2,1,0:T(8,128)(2,1)S(1)} %get-tuple-element.32), channel_id=1, source_target_pairs={{0,1},{1,0},{2,3},{3,2},{4,5},{5,4},{6,7},{7,6},{8,9},{9,8},{10,11... | collective-permute-start | bytes 196616 | tf_op jit(solution)/shard_map/ppermute | solution.py:46
  45.5 2.6 %collective-permute-start.9 = (bf16[8,16,256]{2,1,0:T(8,128)(2,1)S(1)}, bf16[8,16,256]{2,1,0:T(8,128)(2,1)S(1)}, u32[]{:S(2)}, u32[]{:S(2)}) collective-permute-start(bf16[8,16,256]{2,1,0:T(8,128)(2,1)S(1)} %get-tuple-element.33), channel_id=1, source_target_pairs={{0,2},{1,3},{2,0},{3,1},{4,6},{5,7},{6,4},{7,5},{8,10},{9,11},{10,... | collective-permute-start | bytes 196616 | tf_op jit(solution)/shard_map/ppermute | solution.py:46
  48.1 0.2 collective-permute-start.10
  48.3 0.2 fusion
  48.5 0.2 copy.10
  48.9 0.2 copy.12
  49.4 2.6 %collective-permute-done.9.refs_2_ = bf16[8,16,256]{2,1,0:T(8,128)(2,1)S(1)} collective-permute-done((bf16[8,16,256]{2,1,0:T(8,128)(2,1)S(1)}, bf16[8,16,256]{2,1,0:T(8,128)(2,1)S(1)}, u32[]{:S(2)}, u32[]{:S(2)}) %collective-permute-start.9) | collective-permute-done | bytes 65568 | tf_op jit(solution)/shard_map/ppermute | solution.py:46
  52.0 2.2 %collective-permute-done.10.refs_3_ = bf16[8,16,256]{2,1,0:T(8,128)(2,1)S(1)} collective-permute-done((bf16[8,16,256]{2,1,0:T(8,128)(2,1)S(1)}, bf16[8,16,256]{2,1,0:T(8,128)(2,1)S(1)}, u32[]{:S(2)}, u32[]{:S(2)}) %collective-permute-start.10) | collective-permute-done | bytes 65568 | tf_op jit(solution)/shard_map/ppermute | solution.py:46
  54.2 1.8 %wave.1 = (f32[8,16,256]{2,1,0:T(8,128)S(1)}, bf16[8,16,256]{2,1,0:T(8,128)(2,1)S(1)}, bf16[8,16,256]{2,1,0:T(8,128)(2,1)S(1)}, bf16[8,16,256]{2,1,0:T(8,128)(2,1)S(1)}) custom-call(f32[8,16,256]{2,1,0:T(8,128)S(1)} %get-tuple-element.31.refs_0_, bf16[8,16,256]{2,1,0:T(8,128)(2,1)S(1)} %collective-permute-done.8.refs_1_, ...), custom_call_target="tpu_custom_call" | custom-call | bytes 1318912 | tf_op jit(solution)/shard_map/wave/pallas_call | solution.py:27
  56.0 1.4 %collective-permute-start.13 = (bf16[8,16,256]{2,1,0:T(8,128)(2,1)S(1)}, bf16[8,16,256]{2,1,0:T(8,128)(2,1)S(1)}, u32[]{:S(2)}, u32[]{:S(2)}) collective-permute-start(bf16[8,16,256]{2,1,0:T(8,128)(2,1)S(1)} %get-tuple-element.37), channel_id=1, source_target_pairs={{0,2},{1,3},{2,0},{3,1},{4,6},{5,7},{6,4},{7,5},{8,10},{9,11},{10,... | collective-permute-start | bytes 196616 | tf_op jit(solution)/shard_map/ppermute | solution.py:46
  57.4 3.0 %collective-permute-start.14 = (bf16[8,16,256]{2,1,0:T(8,128)(2,1)S(1)}, bf16[8,16,256]{2,1,0:T(8,128)(2,1)S(1)}, u32[]{:S(2)}, u32[]{:S(2)}) collective-permute-start(bf16[8,16,256]{2,1,0:T(8,128)(2,1)S(1)} %get-tuple-element.38), channel_id=1, source_target_pairs={{0,3},{1,2},{2,1},{3,0},{4,7},{5,6},{6,5},{7,4},{8,11},{9,10},{10,... | collective-permute-start | bytes 196616 | tf_op jit(solution)/shard_map/ppermute | solution.py:46
  60.4 0.9 %collective-permute-done.13.refs_2_ = bf16[8,16,256]{2,1,0:T(8,128)(2,1)S(1)} collective-permute-done((bf16[8,16,256]{2,1,0:T(8,128)(2,1)S(1)}, bf16[8,16,256]{2,1,0:T(8,128)(2,1)S(1)}, u32[]{:S(2)}, u32[]{:S(2)}) %collective-permute-start.13) | collective-permute-done | bytes 65568 | tf_op jit(solution)/shard_map/ppermute | solution.py:46
  61.2 2.2 %collective-permute-done.14.refs_3_ = bf16[8,16,256]{2,1,0:T(8,128)(2,1)S(1)} collective-permute-done((bf16[8,16,256]{2,1,0:T(8,128)(2,1)S(1)}, bf16[8,16,256]{2,1,0:T(8,128)(2,1)S(1)}, u32[]{:S(2)}, u32[]{:S(2)}) %collective-permute-start.14) | collective-permute-done | bytes 65568 | tf_op jit(solution)/shard_map/ppermute | solution.py:46
  63.6 1.5 %collective-permute-done.15.refs_1_ = f32[8,32,256]{2,1,0:T(8,128)S(1)} collective-permute-done((f32[8,32,256]{2,1,0:T(8,128)S(1)}, f32[8,32,256]{2,1,0:T(8,128)S(1)}, u32[]{:S(2)}, u32[]{:S(2)}) %collective-permute-start.15) | collective-permute-done | bytes 262176 | tf_op jit(solution)/shard_map/ppermute | solution.py:42
  65.1 1.0 %join.1 = f32[32,8,2,256]{3,2,1,0:T(2,128)} custom-call(f32[8,32,256]{2,1,0:T(8,128)S(1)} %get-tuple-element.39.refs_0_, f32[8,32,256]{2,1,0:T(8,128)S(1)} %collective-permute-done.15.refs_1_), custom_call_target="tpu_custom_call" | custom-call | bytes 1048576 | tf_op jit(solution)/shard_map/join/pallas_call | solution.py:27
  (33 shorter events, 1.1 us)
Async XLA Ops:
  0.0 7.9 %copy-start = (bf16[2048,256]{1,0:T(8,128)(2,1)S(1)}, bf16[2048,256]{1,0:T(8,128)(2,1)}, u32[]{:S(2)}) copy-start(bf16[2048,256]{1,0:T(8,128)(2,1)} %refs_0_.1) | copy-start | bytes 3145732
  0.0 8.2 %collective-permute-start.1 = (bf16[2048,256]{1,0:T(8,128)(2,1)}, bf16[2048,256]{1,0:T(8,128)(2,1)S(1)}, u32[]{:S(2)}, u32[]{:S(2)}) collective-permute-start(bf16[2048,256]{1,0:T(8,128)(2,1)} %refs_0_.1), channel_id=1, source_target_pairs={{0,4},{4,0},{8,12},{12,8},{16,20},{20,16},{24,28},{28,24},{1,5},{5... | collective-permute-start | bytes 3145736 | tf_op jit(solution)/shard_map/ppermute | solution.py:42
  0.5 1.0 %copy-start.1 = (f32[32,8,2,256]{3,2,1,0:T(2,128)S(1)}, f32[32,8,2,256]{3,2,1,0:T(2,128)}, u32[]{:S(2)}) copy-start(f32[32,8,2,256]{3,2,1,0:T(2,128)} %fields.1) | copy-start | bytes 1572868
  1.7 1.6 %collective-permute-start = (f32[8,32,256]{2,1,0:T(8,128)S(1)}, f32[8,32,256]{2,1,0:T(8,128)S(1)}, u32[]{:S(2)}, u32[]{:S(2)}) collective-permute-start(f32[8,32,256]{2,1,0:T(8,128)S(1)} %get-tuple-element.24), channel_id=1, source_target_pairs={{0,4},{4,0},{8,12},{12,8},{16,20},{20,16},{24,28},{28,24},{1,5},{5... | collective-permute-start | bytes 786440 | tf_op jit(solution)/shard_map/ppermute | solution.py:42
  3.4 10.1 %collective-permute-start.2 = (bf16[8,64,256]{2,1,0:T(8,128)(2,1)S(1)}, bf16[8,64,256]{2,1,0:T(8,128)(2,1)S(1)}, u32[]{:S(2)}, u32[]{:S(2)}) collective-permute-start(bf16[8,64,256]{2,1,0:T(8,128)(2,1)S(1)} %get-tuple-element.26.refs_4_), channel_id=1, source_target_pairs={{0,8},{4,12},{8,0},{12,4},{16,24},{20,28},{24,16},{28,20},{1,9},{5... | collective-permute-start | bytes 786440 | tf_op jit(solution)/shard_map/ppermute | solution.py:42
  6.4 13.7 %collective-permute-start.3 = (bf16[8,64,256]{2,1,0:T(8,128)(2,1)S(1)}, bf16[8,64,256]{2,1,0:T(8,128)(2,1)S(1)}, u32[]{:S(2)}, u32[]{:S(2)}) collective-permute-start(bf16[8,64,256]{2,1,0:T(8,128)(2,1)S(1)} %get-tuple-element.26.refs_4_), channel_id=1, source_target_pairs={{0,16},{4,20},{8,24},{12,28},{16,0},{20,4},{24,8},{28,12},{1,17},{... | collective-permute-start | bytes 786440 | tf_op jit(solution)/shard_map/ppermute | solution.py:42
  7.9 12.2 %collective-permute-start.4 = (bf16[8,64,256]{2,1,0:T(8,128)(2,1)S(1)}, bf16[8,64,256]{2,1,0:T(8,128)(2,1)S(1)}, u32[]{:S(2)}, u32[]{:S(2)}) collective-permute-start(bf16[8,64,256]{2,1,0:T(8,128)(2,1)S(1)} %get-tuple-element.26.refs_4_), channel_id=1, source_target_pairs={{0,24},{4,28},{8,16},{12,20},{16,8},{20,12},{24,0},{28,4},{1,25},{... | collective-permute-start | bytes 786440 | tf_op jit(solution)/shard_map/ppermute | solution.py:42
  8.6 24.5 %copy-start.8 = (f32[8,1024]{1,0:T(8,128)S(1)}, f32[8,1024]{1,0:T(8,128)}, u32[]{:S(2)}) copy-start(f32[8,1024]{1,0:T(8,128)} %param.11) | copy-start | bytes 98308
  29.5 9.2 %collective-permute-start.5 = (bf16[8,64,256]{2,1,0:T(8,128)(2,1)S(1)}, bf16[8,64,256]{2,1,0:T(8,128)(2,1)S(1)}, u32[]{:S(2)}, u32[]{:S(2)}) collective-permute-start(bf16[8,64,256]{2,1,0:T(8,128)(2,1)S(1)} %get-tuple-element.28), channel_id=1, source_target_pairs={{0,8},{4,12},{8,0},{12,4},{16,24},{20,28},{24,16},{28,20},{1,9},{5... | collective-permute-start | bytes 786440 | tf_op jit(solution)/shard_map/ppermute | solution.py:42
  30.8 12.8 %collective-permute-start.6 = (bf16[8,64,256]{2,1,0:T(8,128)(2,1)S(1)}, bf16[8,64,256]{2,1,0:T(8,128)(2,1)S(1)}, u32[]{:S(2)}, u32[]{:S(2)}) collective-permute-start(bf16[8,64,256]{2,1,0:T(8,128)(2,1)S(1)} %get-tuple-element.29), channel_id=1, source_target_pairs={{0,16},{4,20},{8,24},{12,28},{16,0},{20,4},{24,8},{28,12},{1,17},{... | collective-permute-start | bytes 786440 | tf_op jit(solution)/shard_map/ppermute | solution.py:42
  31.7 12.0 %collective-permute-start.7 = (bf16[8,64,256]{2,1,0:T(8,128)(2,1)S(1)}, bf16[8,64,256]{2,1,0:T(8,128)(2,1)S(1)}, u32[]{:S(2)}, u32[]{:S(2)}) collective-permute-start(bf16[8,64,256]{2,1,0:T(8,128)(2,1)S(1)} %get-tuple-element.30), channel_id=1, source_target_pairs={{0,24},{4,28},{8,16},{12,20},{16,8},{20,12},{24,0},{28,4},{1,25},{... | collective-permute-start | bytes 786440 | tf_op jit(solution)/shard_map/ppermute | solution.py:42
  33.1 1.2 %collective-permute-start.11 = (f32[8,1024]{1,0:T(8,128)S(1)}, f32[8,1024]{1,0:T(8,128)S(1)}, u32[]{:S(2)}, u32[]{:S(2)}) collective-permute-start(f32[8,1024]{1,0:T(8,128)S(1)} %copy-done.8), channel_id=1, source_target_pairs={{0,4},{4,0},{8,12},{12,8},{16,20},{20,16},{24,28},{28,24},{1,5},{5... | collective-permute-start | bytes 98312 | tf_op jit(solution)/shard_map/ppermute | solution.py:42
  43.8 5.5 %collective-permute-start.8 = (bf16[8,16,256]{2,1,0:T(8,128)(2,1)S(1)}, bf16[8,16,256]{2,1,0:T(8,128)(2,1)S(1)}, u32[]{:S(2)}, u32[]{:S(2)}) collective-permute-start(bf16[8,16,256]{2,1,0:T(8,128)(2,1)S(1)} %get-tuple-element.32), channel_id=1, source_target_pairs={{0,1},{1,0},{2,3},{3,2},{4,5},{5,4},{6,7},{7,6},{8,9},{9,8},{10,11... | collective-permute-start | bytes 196616 | tf_op jit(solution)/shard_map/ppermute | solution.py:46
  45.5 6.5 %collective-permute-start.9 = (bf16[8,16,256]{2,1,0:T(8,128)(2,1)S(1)}, bf16[8,16,256]{2,1,0:T(8,128)(2,1)S(1)}, u32[]{:S(2)}, u32[]{:S(2)}) collective-permute-start(bf16[8,16,256]{2,1,0:T(8,128)(2,1)S(1)} %get-tuple-element.33), channel_id=1, source_target_pairs={{0,2},{1,3},{2,0},{3,1},{4,6},{5,7},{6,4},{7,5},{8,10},{9,11},{10,... | collective-permute-start | bytes 196616 | tf_op jit(solution)/shard_map/ppermute | solution.py:46
  48.1 6.1 %collective-permute-start.10 = (bf16[8,16,256]{2,1,0:T(8,128)(2,1)S(1)}, bf16[8,16,256]{2,1,0:T(8,128)(2,1)S(1)}, u32[]{:S(2)}, u32[]{:S(2)}) collective-permute-start(bf16[8,16,256]{2,1,0:T(8,128)(2,1)S(1)} %get-tuple-element.34), channel_id=1, source_target_pairs={{0,3},{1,2},{2,1},{3,0},{4,7},{5,6},{6,5},{7,4},{8,11},{9,10},{10,... | collective-permute-start | bytes 196616 | tf_op jit(solution)/shard_map/ppermute | solution.py:46
  49.1 5.0 %copy-start.2 = (bf16[256,256]{1,0:T(8,128)(2,1)S(1)}, bf16[256,256]{1,0:T(8,128)(2,1)}, u32[]{:S(2)}) copy-start(bf16[256,256]{1,0:T(8,128)(2,1)} %constant.32.clone.refs_6_) | copy-start | bytes 393220
  49.1 5.0 %copy-start.3 = (bf16[256,256]{1,0:T(8,128)(2,1)S(1)}, bf16[256,256]{1,0:T(8,128)(2,1)}, u32[]{:S(2)}) copy-start(bf16[256,256]{1,0:T(8,128)(2,1)} %constant.33.clone.refs_7_) | copy-start | bytes 393220
  49.2 5.0 %copy-start.4 = (bf16[256,256]{1,0:T(8,128)(2,1)S(1)}, bf16[256,256]{1,0:T(8,128)(2,1)}, u32[]{:S(2)}) copy-start(bf16[256,256]{1,0:T(8,128)(2,1)} %constant.34.clone.refs_8_) | copy-start | bytes 393220
  49.2 5.0 %copy-start.5 = (bf16[256,256]{1,0:T(8,128)(2,1)S(1)}, bf16[256,256]{1,0:T(8,128)(2,1)}, u32[]{:S(2)}) copy-start(bf16[256,256]{1,0:T(8,128)(2,1)} %constant.35.clone.refs_9_) | copy-start | bytes 393220
  49.2 5.0 %copy-start.7 = (f32[4,256]{1,0:T(4,128)S(1)}, f32[4,256]{1,0:T(4,128)}, u32[]{:S(2)}) copy-start(f32[4,256]{1,0:T(4,128)} %constant.37.clone.refs_11_) | copy-start | bytes 12292
  49.4 4.8 %copy-start.6 = (f32[4,256]{1,0:T(4,128)S(1)}, f32[4,256]{1,0:T(4,128)}, u32[]{:S(2)}) copy-start(f32[4,256]{1,0:T(4,128)} %constant.36.clone.refs_10_) | copy-start | bytes 12292
  55.9 4.5 %collective-permute-start.12 = (bf16[8,16,256]{2,1,0:T(8,128)(2,1)S(1)}, bf16[8,16,256]{2,1,0:T(8,128)(2,1)S(1)}, u32[]{:S(2)}, u32[]{:S(2)}) collective-permute-start(bf16[8,16,256]{2,1,0:T(8,128)(2,1)S(1)} %get-tuple-element.36), channel_id=1, source_target_pairs={{0,1},{1,0},{2,3},{3,2},{4,5},{5,4},{6,7},{7,6},{8,9},{9,8},{10,11... | collective-permute-start | bytes 196616 | tf_op jit(solution)/shard_map/ppermute | solution.py:46
  56.0 5.2 %collective-permute-start.13 = (bf16[8,16,256]{2,1,0:T(8,128)(2,1)S(1)}, bf16[8,16,256]{2,1,0:T(8,128)(2,1)S(1)}, u32[]{:S(2)}, u32[]{:S(2)}) collective-permute-start(bf16[8,16,256]{2,1,0:T(8,128)(2,1)S(1)} %get-tuple-element.37), channel_id=1, source_target_pairs={{0,2},{1,3},{2,0},{3,1},{4,6},{5,7},{6,4},{7,5},{8,10},{9,11},{10,... | collective-permute-start | bytes 196616 | tf_op jit(solution)/shard_map/ppermute | solution.py:46
  57.4 6.1 %collective-permute-start.14 = (bf16[8,16,256]{2,1,0:T(8,128)(2,1)S(1)}, bf16[8,16,256]{2,1,0:T(8,128)(2,1)S(1)}, u32[]{:S(2)}, u32[]{:S(2)}) collective-permute-start(bf16[8,16,256]{2,1,0:T(8,128)(2,1)S(1)} %get-tuple-element.38), channel_id=1, source_target_pairs={{0,3},{1,2},{2,1},{3,0},{4,7},{5,6},{6,5},{7,4},{8,11},{9,10},{10,... | collective-permute-start | bytes 196616 | tf_op jit(solution)/shard_map/ppermute | solution.py:46
  63.5 1.6 %collective-permute-start.15 = (f32[8,32,256]{2,1,0:T(8,128)S(1)}, f32[8,32,256]{2,1,0:T(8,128)S(1)}, u32[]{:S(2)}, u32[]{:S(2)}) collective-permute-start(f32[8,32,256]{2,1,0:T(8,128)S(1)} %get-tuple-element.40), channel_id=1, source_target_pairs={{0,4},{4,0},{8,12},{12,8},{16,20},{20,16},{24,28},{28,24},{1,5},{5... | collective-permute-start | bytes 786440 | tf_op jit(solution)/shard_map/ppermute | solution.py:42

commit v2 on v1

--- a/solution.py
+++ b/solution.py
@@ -11,7 +11,7 @@
 
 BF16 = jnp.bfloat16
 F32 = jnp.float32
-CHUNKS = (1,)
+CHUNKS = (1, 1)
 VMEM = pl.BlockSpec(memory_space=pltpu.VMEM)
 
 
@@ -161,19 +161,27 @@
     return real, imag
 
 
-def wave_kernel(nb, times, *refs):
-    blocks = refs[:times]
+def wave_kernel(sizes, times, *refs):
+    count = len(sizes)
+    blocks = refs[: times * count]
     phase_cos, phase_sin, cos_high, cos_low, sin_high, sin_low, twist_cos, twist_sin = refs[
-        times : times + 8
+        times * count : times * count + 8
     ]
-    outs = refs[times + 8 : 2 * times + 8]
-    held, back = refs[2 * times + 8 :]
+    outs = refs[times * count + 8 : -2]
+    held, back = refs[-2:]
     z = lax.axis_index("tm")
+    nb = sum(sizes)
     rows, time = blocks[0].shape[1:]
     size = nb * rows
     length = times * time
-    for j in range(times):
-        held[z ^ j] = blocks[j][...].astype(F32)
+    start = 0
+    for n, part in enumerate(sizes):
+        for j in range(times):
+            block = blocks[n * times + j]
+            for c in range(2):
+                at = c * nb + start
+                held[z ^ j, at : at + part] = block[c * part : (c + 1) * part].astype(F32)
+        start += part
     here = [
         (held[a, :nb].reshape(size, time), held[a, nb:].reshape(size, time)) for a in range(times)
     ]
@@ -208,7 +216,7 @@
 
 
 def part_kernel(times, *refs):
-    blocks, (own, other), (held,) = refs[:times], refs[times : times + 2], refs[times + 2 :]
+    blocks, (own, other), (held, sent) = refs[:times], refs[times : times + 2], refs[times + 2 :]
     core = lax.axis_index("pix") % 2
     z = lax.axis_index("tm")
     cut = blocks[0].shape[1] // 2
@@ -218,19 +226,17 @@
         mine = pl.multiple_of(core * cut, cut)
         theirs = pl.multiple_of((1 - core) * cut, cut)
         own[:, pl.ds(at, cut), :] = held[:, pl.ds(mine, cut), :]
-        other[:, pl.ds(at, cut), :] = held[:, pl.ds(theirs, cut), :]
-
-
-def join_kernel(starts, sizes, *refs):
-    out = refs[-1]
+        sent[:, pl.ds(at, cut), :] = held[:, pl.ds(theirs, cut), :]
+    other[...] = sent[...].astype(other.dtype)
+
+
+def join_kernel(own, other, out):
     half = out.shape[1] // 2
     core = lax.axis_index("pix") % 2
-    for n, (start, nb) in enumerate(zip(starts, sizes)):
-        own, other = refs[2 * n], refs[2 * n + 1]
-        for c in range(2):
-            for b in range(nb):
-                out[:, core * half + start + b, c, :] = own[c * nb + b]
-                out[:, (1 - core) * half + start + b, c, :] = other[c * nb + b].astype(F32)
+    for c in range(2):
+        for b in range(half):
+            out[:, core * half + b, c, :] = own[c * half + b]
+            out[:, (1 - core) * half + b, c, :] = other[c * half + b].astype(F32)
 
 
 def tables(times, time):
@@ -285,7 +291,7 @@
     phase_cos, phase_sin = jnp.cos(angles), jnp.sin(angles)
     consts = tables(times, time)
 
-    finals = []
+    waves = []
     for n, nb in enumerate(sizes):
         block = (2 * nb, rows, time)
         parts = call(
@@ -293,6 +299,7 @@
             "kerr",
             [(block, F32)] + [(block, BF16)] * (chips - 1),
             [((chips * rows, 2 * time), BF16), ((2 * pixels, 2 * time), BF16)],
+            flops=16 * pixels * chips * rows * nb * time,
         )(profiles, profiles_other, *turned, *gathers[n])
         sums = [parts[0]] + [swap_pix(parts[j], 2 * j, pix) for j in range(1, chips)]
         block = (2 * nb, cut, time)
@@ -302,24 +309,24 @@
             [(block, F32)] + [(block, BF16)] * (times - 1),
             [((2 * nb, rows, time), F32)],
         )(fulls[n], *sums)
-        pieces = [pieces[0]] + [swap_tm(pieces[j], j, times) for j in range(1, times)]
-        pieces = call(
-            functools.partial(wave_kernel, nb, times),
-            "wave",
-            [(block, F32)] + [(block, BF16)] * (times - 1),
-            [((times,) + block, F32)] * 2,
-        )(*pieces, phase_cos, phase_sin, *consts)
-        pieces = [pieces[0]] + [swap_tm(pieces[j], j, times) for j in range(1, times)]
-        own, other = call(
-            functools.partial(part_kernel, times),
-            "part",
-            [((2 * nb, modes, time), F32), ((2 * nb, modes, time), F32)],
-            [(block, F32)],
-        )(*pieces)
-        finals += [own, swap_pix(other, 1, pix)]
-    return call(functools.partial(join_kernel, starts, sizes), "join", [(fields.shape, F32)])(
-        *finals
-    )[0]
+        waves += [pieces[0]] + [swap_tm(pieces[j], j, times) for j in range(1, times)]
+    block = (2 * half, cut, time)
+    pieces = call(
+        functools.partial(wave_kernel, sizes, times),
+        "wave",
+        [(block, F32)] + [(block, BF16)] * (times - 1),
+        [((times,) + block, F32)] * 2,
+        flops=10**9,
+    )(*waves, phase_cos, phase_sin, *consts)
+    pieces = [pieces[0]] + [swap_tm(pieces[j], j, times) for j in range(1, times)]
+    block = (2 * half, modes, time)
+    own, other = call(
+        functools.partial(part_kernel, times),
+        "part",
+        [(block, F32), (block, BF16)],
+        [((2 * half, cut, time), F32), (block, F32)],
+    )(*pieces)
+    return call(join_kernel, "join", [(fields.shape, F32)])(own, swap_pix(other, 1, pix))[0]
 
 
 def split_length(length):

time: 66.3 us -> 59.7 us (0.900)
  waiting for transfers between devices: 32.8 us -> 9.98 us
  starting transfers between devices: 17.6 us -> 32.4 us
  local copies, waits for them, and re-layouts: 1.86 us -> 3.08 us
    ppermute x10 -> x17, waiting for transfers between devices: 25 us -> 3.04 us  [swap_pix(): return lax.ppermute(value, 'pix', [(i, i ^ mask) for i in range(size)])]
    ppermute x10 -> x17, starting transfers between devices: 8.74 us -> 17.9 us  [swap_pix(): return lax.ppermute(value, 'pix', [(i, i ^ mask) for i in range(size)])]
    ppermute x6 -> x9, starting transfers between devices: 8.9 us -> 14.6 us  [swap_tm(): return lax.ppermute(value, 'tm', [(i, i ^ mask) for i in range(size)])]
    unnamed x18 -> x20, local copies, waits for them, and re-layouts: 1.09 us -> 2.31 us
    ppermute x6 -> x9, waiting for transfers between devices: 7.79 us -> 6.94 us  [swap_tm(): return lax.ppermute(value, 'tm', [(i, i ^ mask) for i in range(size)])]
    pallas_call x9 -> x12, Pallas kernels: 13.4 us -> 13.5 us  [run(): pl.pallas_call(kernel, out_shape=tuple((jax.ShapeDtypeStruct(*out) for ou...]
  transfers between devices with their start and end apart: 16 -> 26, of which waited for: 11 -> 6; matrix products, arithmetic and copies ran while one was open for 2% -> 2% of each run, Pallas kernels for 1% -> 18%
where the time goes in v2:
time: 59.7 us; the launch traced here: 59.5 us
  starting transfers between devices  32.4 us (54%)
  Pallas kernels  13.5 us (23%)
  waiting for transfers between devices  9.98 us (17%)
  local copies, waits for them, and re-layouts  3.08 us (5%)
    ppermute x17, starting transfers between devices, swap_pix(): return lax.ppermute(value, 'pix', [(i, i ^ mask) for i in range(size)])  17.9 us
    ppermute x9, starting transfers between devices, swap_tm(): return lax.ppermute(value, 'tm', [(i, i ^ mask) for i in range(size)])  14.6 us
    pallas_call x12, Pallas kernels, run(): pl.pallas_call(kernel, out_shape=tuple((jax.ShapeDtypeStruct(*out) for ou...  13.5 us
    ppermute x9, waiting for transfers between devices, swap_tm(): return lax.ppermute(value, 'tm', [(i, i ^ mask) for i in range(size)])  6.94 us
    ppermute x17, waiting for transfers between devices, swap_pix(): return lax.ppermute(value, 'pix', [(i, i ^ mask) for i in range(size)])  3.04 us
    unnamed x20, local copies, waits for them, and re-layouts  2.31 us
  transfers between devices with their start and end apart: 26, of which 6 were waited for; matrix products, arithmetic and copies ran while one was open for 2% of the time, Pallas kernels for 18%

profile of v2, /device:TPU:0, one launch (start us, length us, event | category | flops | bytes accessed | tf_op | source)
XLA Modules:
  0.0 59.5 jit_solution(18071709965813156432)
XLA Ops:
  0.0 0.5 collective-permute-start.1
  0.5 1.0 %copy-done.2 = f32[32,8,2,256]{3,2,1,0:T(2,128)S(1)} copy-done((f32[32,8,2,256]{3,2,1,0:T(2,128)S(1)}, f32[32,8,2,256]{3,2,1,0:T(2,128)}, u32[]{:S(2)}) %copy-start.2) | copy-done | bytes 524312
  2.3 0.9 %collective-permute-done.other = f32[4,32,256]{2,1,0:T(8,128)S(1)} collective-permute-done((f32[4,32,256]{2,1,0:T(8,128)S(1)}, f32[4,32,256]{2,1,0:T(8,128)S(1)}, u32[]{:S(2)}, u32[]{:S(2)}) %collective-permute-start) | collective-permute-done | bytes 131104 | tf_op jit(solution)/shard_map/ppermute | solution.py:42
  3.2 2.9 %collective-permute-start.2 = (bf16[4,64,256]{2,1,0:T(8,128)(2,1)S(1)}, bf16[4,64,256]{2,1,0:T(8,128)(2,1)S(1)}, u32[]{:S(2)}, u32[]{:S(2)}) collective-permute-start(bf16[4,64,256]{2,1,0:T(8,128)(2,1)S(1)} %get-tuple-element.38.refs_4_), channel_id=1, source_target_pairs={{0,8},{4,12},{8,0},{12,4},{16,24},{20,28},{24,16},{28,20},{1,9},{5... | collective-permute-start | bytes 393224 | tf_op jit(solution)/shard_map/ppermute | solution.py:42
  6.1 1.5 %collective-permute-start.3 = (bf16[4,64,256]{2,1,0:T(8,128)(2,1)S(1)}, bf16[4,64,256]{2,1,0:T(8,128)(2,1)S(1)}, u32[]{:S(2)}, u32[]{:S(2)}) collective-permute-start(bf16[4,64,256]{2,1,0:T(8,128)(2,1)S(1)} %get-tuple-element.38.refs_4_), channel_id=1, source_target_pairs={{0,16},{4,20},{8,24},{12,28},{16,0},{20,4},{24,8},{28,12},{1,17},{... | collective-permute-start | bytes 393224 | tf_op jit(solution)/shard_map/ppermute | solution.py:42
  7.7 1.2 %copy-done = bf16[2048,256]{1,0:T(8,128)(2,1)S(1)} copy-done((bf16[2048,256]{1,0:T(8,128)(2,1)S(1)}, bf16[2048,256]{1,0:T(8,128)(2,1)}, u32[]{:S(2)}) %copy-start) | copy-done | bytes 1048600
  9.4 2.0 %collective-permute-start.12 = (bf16[4,64,256]{2,1,0:T(8,128)(2,1)S(1)}, bf16[4,64,256]{2,1,0:T(8,128)(2,1)S(1)}, u32[]{:S(2)}, u32[]{:S(2)}) collective-permute-start(bf16[4,64,256]{2,1,0:T(8,128)(2,1)S(1)} %get-tuple-element.50.refs_4_), channel_id=1, source_target_pairs={{0,8},{4,12},{8,0},{12,4},{16,24},{20,28},{24,16},{28,20},{1,9},{5... | collective-permute-start | bytes 393224 | tf_op jit(solution)/shard_map/ppermute | solution.py:42
  11.8 1.6 %collective-permute-start.13 = (bf16[4,64,256]{2,1,0:T(8,128)(2,1)S(1)}, bf16[4,64,256]{2,1,0:T(8,128)(2,1)S(1)}, u32[]{:S(2)}, u32[]{:S(2)}) collective-permute-start(bf16[4,64,256]{2,1,0:T(8,128)(2,1)S(1)} %get-tuple-element.50.refs_4_), channel_id=1, source_target_pairs={{0,16},{4,20},{8,24},{12,28},{16,0},{20,4},{24,8},{28,12},{1,17},{... | collective-permute-start | bytes 393224 | tf_op jit(solution)/shard_map/ppermute | solution.py:42
  13.4 0.8 %collective-permute-done.3.refs_6_ = bf16[4,64,256]{2,1,0:T(8,128)(2,1)S(1)} collective-permute-done((bf16[4,64,256]{2,1,0:T(8,128)(2,1)S(1)}, bf16[4,64,256]{2,1,0:T(8,128)(2,1)S(1)}, u32[]{:S(2)}, u32[]{:S(2)}) %collective-permute-start.3) | collective-permute-done | bytes 131104 | tf_op jit(solution)/shard_map/ppermute | solution.py:42
  14.2 1.5 %collective-permute-start.14 = (bf16[4,64,256]{2,1,0:T(8,128)(2,1)S(1)}, bf16[4,64,256]{2,1,0:T(8,128)(2,1)S(1)}, u32[]{:S(2)}, u32[]{:S(2)}) collective-permute-start(bf16[4,64,256]{2,1,0:T(8,128)(2,1)S(1)} %get-tuple-element.50.refs_4_), channel_id=1, source_target_pairs={{0,24},{4,28},{8,16},{12,20},{16,8},{20,12},{24,0},{28,4},{1,25},{... | collective-permute-start | bytes 393224 | tf_op jit(solution)/shard_map/ppermute | solution.py:42
  15.7 4.7 %kerr.2 = (f32[4,64,256]{2,1,0:T(8,128)S(1)}, bf16[4,64,256]{2,1,0:T(8,128)(2,1)S(1)}, bf16[4,64,256]{2,1,0:T(8,128)(2,1)S(1)}, bf16[4,64,256]{2,1,0:T(8,128)(2,1)S(1)}) custom-call(bf16[2048,256]{1,0:T(8,128)(2,1)S(1)} %copy-done.1, bf16[2048,256]{1,0:T(8,128)(2,1)S(1)} %collective-permute-done.1.profiles.refs_1_, bf16[256,2048]{1,0:T(8,128)(2,1)S(1)} %turn.2.refs_2_, ...), custom_call_target="tpu_custom_call" | custom-call | flops 4294967296 | bytes 5373952 | tf_op jit(solution)/shard_map/kerr/pallas_call | solution.py:27
  20.4 1.6 %collective-permute-start.5 = (bf16[4,64,256]{2,1,0:T(8,128)(2,1)S(1)}, bf16[4,64,256]{2,1,0:T(8,128)(2,1)S(1)}, u32[]{:S(2)}, u32[]{:S(2)}) collective-permute-start(bf16[4,64,256]{2,1,0:T(8,128)(2,1)S(1)} %get-tuple-element.40), channel_id=1, source_target_pairs={{0,8},{4,12},{8,0},{12,4},{16,24},{20,28},{24,16},{28,20},{1,9},{5... | collective-permute-start | bytes 393224 | tf_op jit(solution)/shard_map/ppermute | solution.py:42
  22.0 0.5 collective-permute-start.6
  22.5 1.5 %collective-permute-start.7 = (bf16[4,64,256]{2,1,0:T(8,128)(2,1)S(1)}, bf16[4,64,256]{2,1,0:T(8,128)(2,1)S(1)}, u32[]{:S(2)}, u32[]{:S(2)}) collective-permute-start(bf16[4,64,256]{2,1,0:T(8,128)(2,1)S(1)} %get-tuple-element.42), channel_id=1, source_target_pairs={{0,24},{4,28},{8,16},{12,20},{16,8},{20,12},{24,0},{28,4},{1,25},{... | collective-permute-start | bytes 393224 | tf_op jit(solution)/shard_map/ppermute | solution.py:42
  24.0 4.7 %kerr.3 = (f32[4,64,256]{2,1,0:T(8,128)S(1)}, bf16[4,64,256]{2,1,0:T(8,128)(2,1)S(1)}, bf16[4,64,256]{2,1,0:T(8,128)(2,1)S(1)}, bf16[4,64,256]{2,1,0:T(8,128)(2,1)S(1)}) custom-call(bf16[2048,256]{1,0:T(8,128)(2,1)S(1)} %copy-done.1, bf16[2048,256]{1,0:T(8,128)(2,1)S(1)} %collective-permute-done.1.profiles.refs_1_, bf16[256,2048]{1,0:T(8,128)(2,1)S(1)} %turn.2.refs_2_, ...), custom_call_target="tpu_custom_call" | custom-call | flops 4294967296 | bytes 5373952 | tf_op jit(solution)/shard_map/kerr/pallas_call | solution.py:27
  28.8 1.6 %collective-permute-start.15 = (bf16[4,64,256]{2,1,0:T(8,128)(2,1)S(1)}, bf16[4,64,256]{2,1,0:T(8,128)(2,1)S(1)}, u32[]{:S(2)}, u32[]{:S(2)}) collective-permute-start(bf16[4,64,256]{2,1,0:T(8,128)(2,1)S(1)} %get-tuple-element.52), channel_id=1, source_target_pairs={{0,8},{4,12},{8,0},{12,4},{16,24},{20,28},{24,16},{28,20},{1,9},{5... | collective-permute-start | bytes 393224 | tf_op jit(solution)/shard_map/ppermute | solution.py:42
  30.3 0.5 collective-permute-start.16
  30.8 1.5 %collective-permute-start.17 = (bf16[4,64,256]{2,1,0:T(8,128)(2,1)S(1)}, bf16[4,64,256]{2,1,0:T(8,128)(2,1)S(1)}, u32[]{:S(2)}, u32[]{:S(2)}) collective-permute-start(bf16[4,64,256]{2,1,0:T(8,128)(2,1)S(1)} %get-tuple-element.54), channel_id=1, source_target_pairs={{0,24},{4,28},{8,16},{12,20},{16,8},{20,12},{24,0},{28,4},{1,25},{... | collective-permute-start | bytes 393224 | tf_op jit(solution)/shard_map/ppermute | solution.py:42
  32.4 1.6 %collective-permute-start.8 = (bf16[4,16,256]{2,1,0:T(8,128)(2,1)S(1)}, bf16[4,16,256]{2,1,0:T(8,128)(2,1)S(1)}, u32[]{:S(2)}, u32[]{:S(2)}) collective-permute-start(bf16[4,16,256]{2,1,0:T(8,128)(2,1)S(1)} %get-tuple-element.44), channel_id=1, source_target_pairs={{0,1},{1,0},{2,3},{3,2},{4,5},{5,4},{6,7},{7,6},{8,9},{9,8},{10,11... | collective-permute-start | bytes 98312 | tf_op jit(solution)/shard_map/ppermute | solution.py:46
  34.1 2.7 %collective-permute-start.9 = (bf16[4,16,256]{2,1,0:T(8,128)(2,1)S(1)}, bf16[4,16,256]{2,1,0:T(8,128)(2,1)S(1)}, u32[]{:S(2)}, u32[]{:S(2)}) collective-permute-start(bf16[4,16,256]{2,1,0:T(8,128)(2,1)S(1)} %get-tuple-element.45), channel_id=1, source_target_pairs={{0,2},{1,3},{2,0},{3,1},{4,6},{5,7},{6,4},{7,5},{8,10},{9,11},{10,... | collective-permute-start | bytes 98312 | tf_op jit(solution)/shard_map/ppermute | solution.py:46
  36.7 1.4 %collective-permute-start.10 = (bf16[4,16,256]{2,1,0:T(8,128)(2,1)S(1)}, bf16[4,16,256]{2,1,0:T(8,128)(2,1)S(1)}, u32[]{:S(2)}, u32[]{:S(2)}) collective-permute-start(bf16[4,16,256]{2,1,0:T(8,128)(2,1)S(1)} %get-tuple-element.46), channel_id=1, source_target_pairs={{0,3},{1,2},{2,1},{3,0},{4,7},{5,6},{6,5},{7,4},{8,11},{9,10},{10,... | collective-permute-start | bytes 98312 | tf_op jit(solution)/shard_map/ppermute | solution.py:46
  38.2 0.5 collective-permute-start.18
  38.7 2.6 %collective-permute-start.19 = (bf16[4,16,256]{2,1,0:T(8,128)(2,1)S(1)}, bf16[4,16,256]{2,1,0:T(8,128)(2,1)S(1)}, u32[]{:S(2)}, u32[]{:S(2)}) collective-permute-start(bf16[4,16,256]{2,1,0:T(8,128)(2,1)S(1)} %get-tuple-element.57), channel_id=1, source_target_pairs={{0,2},{1,3},{2,0},{3,1},{4,6},{5,7},{6,4},{7,5},{8,10},{9,11},{10,... | collective-permute-start | bytes 98312 | tf_op jit(solution)/shard_map/ppermute | solution.py:46
  41.3 1.3 %collective-permute-start.20 = (bf16[4,16,256]{2,1,0:T(8,128)(2,1)S(1)}, bf16[4,16,256]{2,1,0:T(8,128)(2,1)S(1)}, u32[]{:S(2)}, u32[]{:S(2)}) collective-permute-start(bf16[4,16,256]{2,1,0:T(8,128)(2,1)S(1)} %get-tuple-element.58), channel_id=1, source_target_pairs={{0,3},{1,2},{2,1},{3,0},{4,7},{5,6},{6,5},{7,4},{8,11},{9,10},{10,... | collective-permute-start | bytes 98312 | tf_op jit(solution)/shard_map/ppermute | solution.py:46
  43.8 3.4 %collective-permute-done.20.refs_7_ = bf16[4,16,256]{2,1,0:T(8,128)(2,1)S(1)} collective-permute-done((bf16[4,16,256]{2,1,0:T(8,128)(2,1)S(1)}, bf16[4,16,256]{2,1,0:T(8,128)(2,1)S(1)}, u32[]{:S(2)}, u32[]{:S(2)}) %collective-permute-start.20) | collective-permute-done | bytes 32800 | tf_op jit(solution)/shard_map/ppermute | solution.py:46
  47.3 1.8 %wave.1 = (f32[8,16,256]{2,1,0:T(8,128)S(1)}, bf16[8,16,256]{2,1,0:T(8,128)(2,1)S(1)}, bf16[8,16,256]{2,1,0:T(8,128)(2,1)S(1)}, bf16[8,16,256]{2,1,0:T(8,128)(2,1)S(1)}) custom-call(f32[4,16,256]{2,1,0:T(8,128)S(1)} %get-tuple-element.43.refs_0_, bf16[4,16,256]{2,1,0:T(8,128)(2,1)S(1)} %collective-permute-done.8.refs_1_, ...), custom_call_target="tpu_custom_call" | custom-call | flops 1000000000 | bytes 1318912 | tf_op jit(solution)/shard_map/wave/pallas_call | solution.py:27
  49.1 1.8 %collective-permute-start.23 = (bf16[8,16,256]{2,1,0:T(8,128)(2,1)S(1)}, bf16[8,16,256]{2,1,0:T(8,128)(2,1)S(1)}, u32[]{:S(2)}, u32[]{:S(2)}) collective-permute-start(bf16[8,16,256]{2,1,0:T(8,128)(2,1)S(1)} %get-tuple-element.61), channel_id=1, source_target_pairs={{0,2},{1,3},{2,0},{3,1},{4,6},{5,7},{6,4},{7,5},{8,10},{9,11},{10,... | collective-permute-start | bytes 196616 | tf_op jit(solution)/shard_map/ppermute | solution.py:46
  50.9 2.6 %collective-permute-start.24 = (bf16[8,16,256]{2,1,0:T(8,128)(2,1)S(1)}, bf16[8,16,256]{2,1,0:T(8,128)(2,1)S(1)}, u32[]{:S(2)}, u32[]{:S(2)}) collective-permute-start(bf16[8,16,256]{2,1,0:T(8,128)(2,1)S(1)} %get-tuple-element.62), channel_id=1, source_target_pairs={{0,3},{1,2},{2,1},{3,0},{4,7},{5,6},{6,5},{7,4},{8,11},{9,10},{10,... | collective-permute-start | bytes 196616 | tf_op jit(solution)/shard_map/ppermute | solution.py:46
  53.5 0.9 %collective-permute-done.23.refs_2_ = bf16[8,16,256]{2,1,0:T(8,128)(2,1)S(1)} collective-permute-done((bf16[8,16,256]{2,1,0:T(8,128)(2,1)S(1)}, bf16[8,16,256]{2,1,0:T(8,128)(2,1)S(1)}, u32[]{:S(2)}, u32[]{:S(2)}) %collective-permute-start.23) | collective-permute-done | bytes 65568 | tf_op jit(solution)/shard_map/ppermute | solution.py:46
  54.3 2.6 %collective-permute-done.24.refs_3_ = bf16[8,16,256]{2,1,0:T(8,128)(2,1)S(1)} collective-permute-done((bf16[8,16,256]{2,1,0:T(8,128)(2,1)S(1)}, bf16[8,16,256]{2,1,0:T(8,128)(2,1)S(1)}, u32[]{:S(2)}, u32[]{:S(2)}) %collective-permute-start.24) | collective-permute-done | bytes 65568 | tf_op jit(solution)/shard_map/ppermute | solution.py:46
  57.2 1.3 %collective-permute-done.25.other = bf16[8,32,256]{2,1,0:T(8,128)(2,1)S(1)} collective-permute-done((bf16[8,32,256]{2,1,0:T(8,128)(2,1)S(1)}, bf16[8,32,256]{2,1,0:T(8,128)(2,1)S(1)}, u32[]{:S(2)}, u32[]{:S(2)}) %collective-permute-start.25) | collective-permute-done | bytes 131104 | tf_op jit(solution)/shard_map/ppermute | solution.py:42
  58.5 1.0 %join.1 = f32[32,8,2,256]{3,2,1,0:T(2,128)} custom-call(f32[8,32,256]{2,1,0:T(8,128)S(1)} %get-tuple-element.63.own, bf16[8,32,256]{2,1,0:T(8,128)(2,1)S(1)} %collective-permute-done.25.other), custom_call_target="tpu_custom_call" | custom-call | bytes 917504 | tf_op jit(solution)/shard_map/join/pallas_call | solution.py:27
  (58 shorter events, 3.2 us)
Async XLA Ops:
  0.0 9.4 %collective-permute-start.1 = (bf16[2048,256]{1,0:T(8,128)(2,1)}, bf16[2048,256]{1,0:T(8,128)(2,1)S(1)}, u32[]{:S(2)}, u32[]{:S(2)}) collective-permute-start(bf16[2048,256]{1,0:T(8,128)(2,1)} %refs_0_.3), channel_id=1, source_target_pairs={{0,4},{4,0},{8,12},{12,8},{16,20},{20,16},{24,28},{28,24},{1,5},{5... | collective-permute-start | bytes 3145736 | tf_op jit(solution)/shard_map/ppermute | solution.py:42
  1.7 1.4 %collective-permute-start = (f32[4,32,256]{2,1,0:T(8,128)S(1)}, f32[4,32,256]{2,1,0:T(8,128)S(1)}, u32[]{:S(2)}, u32[]{:S(2)}) collective-permute-start(f32[4,32,256]{2,1,0:T(8,128)S(1)} %get-tuple-element.36), channel_id=1, source_target_pairs={{0,4},{4,0},{8,12},{12,8},{16,20},{20,16},{24,28},{28,24},{1,5},{5... | collective-permute-start | bytes 393224 | tf_op jit(solution)/shard_map/ppermute | solution.py:42
  1.8 7.4 %collective-permute-start.11 = (f32[4,32,256]{2,1,0:T(8,128)S(1)}, f32[4,32,256]{2,1,0:T(8,128)S(1)}, u32[]{:S(2)}, u32[]{:S(2)}) collective-permute-start(f32[4,32,256]{2,1,0:T(8,128)S(1)} %get-tuple-element.48), channel_id=1, source_target_pairs={{0,4},{4,0},{8,12},{12,8},{16,20},{20,16},{24,28},{28,24},{1,5},{5... | collective-permute-start | bytes 393224 | tf_op jit(solution)/shard_map/ppermute | solution.py:42
  3.2 6.1 %copy-start.9 = (f32[8,1024]{1,0:T(8,128)S(1)}, f32[8,1024]{1,0:T(8,128)}, u32[]{:S(2)}) copy-start(f32[8,1024]{1,0:T(8,128)} %param.11) | copy-start | bytes 98308
  3.2 8.6 %collective-permute-start.2 = (bf16[4,64,256]{2,1,0:T(8,128)(2,1)S(1)}, bf16[4,64,256]{2,1,0:T(8,128)(2,1)S(1)}, u32[]{:S(2)}, u32[]{:S(2)}) collective-permute-start(bf16[4,64,256]{2,1,0:T(8,128)(2,1)S(1)} %get-tuple-element.38.refs_4_), channel_id=1, source_target_pairs={{0,8},{4,12},{8,0},{12,4},{16,24},{20,28},{24,16},{28,20},{1,9},{5... | collective-permute-start | bytes 393224 | tf_op jit(solution)/shard_map/ppermute | solution.py:42
  6.1 8.1 %collective-permute-start.3 = (bf16[4,64,256]{2,1,0:T(8,128)(2,1)S(1)}, bf16[4,64,256]{2,1,0:T(8,128)(2,1)S(1)}, u32[]{:S(2)}, u32[]{:S(2)}) collective-permute-start(bf16[4,64,256]{2,1,0:T(8,128)(2,1)S(1)} %get-tuple-element.38.refs_4_), channel_id=1, source_target_pairs={{0,16},{4,20},{8,24},{12,28},{16,0},{20,4},{24,8},{28,12},{1,17},{... | collective-permute-start | bytes 393224 | tf_op jit(solution)/shard_map/ppermute | solution.py:42
  7.7 8.0 %collective-permute-start.4 = (bf16[4,64,256]{2,1,0:T(8,128)(2,1)S(1)}, bf16[4,64,256]{2,1,0:T(8,128)(2,1)S(1)}, u32[]{:S(2)}, u32[]{:S(2)}) collective-permute-start(bf16[4,64,256]{2,1,0:T(8,128)(2,1)S(1)} %get-tuple-element.38.refs_4_), channel_id=1, source_target_pairs={{0,24},{4,28},{8,16},{12,20},{16,8},{20,12},{24,0},{28,4},{1,25},{... | collective-permute-start | bytes 393224 | tf_op jit(solution)/shard_map/ppermute | solution.py:42
  9.3 24.8 %collective-permute-start.21 = (f32[8,1024]{1,0:T(8,128)S(1)}, f32[8,1024]{1,0:T(8,128)S(1)}, u32[]{:S(2)}, u32[]{:S(2)}) collective-permute-start(f32[8,1024]{1,0:T(8,128)S(1)} %copy-done.9), channel_id=1, source_target_pairs={{0,4},{4,0},{8,12},{12,8},{16,20},{20,16},{24,28},{28,24},{1,5},{5... | collective-permute-start | bytes 98312 | tf_op jit(solution)/shard_map/ppermute | solution.py:42
  9.4 6.3 %copy-start.1 = (bf16[2048,256]{1,0:T(8,128)(2,1)S(1)}, bf16[2048,256]{1,0:T(8,128)(2,1)}, u32[]{:S(2)}) copy-start(bf16[2048,256]{1,0:T(8,128)(2,1)} %refs_0_.3) | copy-start | bytes 3145732
  9.4 12.6 %collective-permute-start.12 = (bf16[4,64,256]{2,1,0:T(8,128)(2,1)S(1)}, bf16[4,64,256]{2,1,0:T(8,128)(2,1)S(1)}, u32[]{:S(2)}, u32[]{:S(2)}) collective-permute-start(bf16[4,64,256]{2,1,0:T(8,128)(2,1)S(1)} %get-tuple-element.50.refs_4_), channel_id=1, source_target_pairs={{0,8},{4,12},{8,0},{12,4},{16,24},{20,28},{24,16},{28,20},{1,9},{5... | collective-permute-start | bytes 393224 | tf_op jit(solution)/shard_map/ppermute | solution.py:42
  11.8 10.7 %collective-permute-start.13 = (bf16[4,64,256]{2,1,0:T(8,128)(2,1)S(1)}, bf16[4,64,256]{2,1,0:T(8,128)(2,1)S(1)}, u32[]{:S(2)}, u32[]{:S(2)}) collective-permute-start(bf16[4,64,256]{2,1,0:T(8,128)(2,1)S(1)} %get-tuple-element.50.refs_4_), channel_id=1, source_target_pairs={{0,16},{4,20},{8,24},{12,28},{16,0},{20,4},{24,8},{28,12},{1,17},{... | collective-permute-start | bytes 393224 | tf_op jit(solution)/shard_map/ppermute | solution.py:42
  14.2 9.8 %collective-permute-start.14 = (bf16[4,64,256]{2,1,0:T(8,128)(2,1)S(1)}, bf16[4,64,256]{2,1,0:T(8,128)(2,1)S(1)}, u32[]{:S(2)}, u32[]{:S(2)}) collective-permute-start(bf16[4,64,256]{2,1,0:T(8,128)(2,1)S(1)} %get-tuple-element.50.refs_4_), channel_id=1, source_target_pairs={{0,24},{4,28},{8,16},{12,20},{16,8},{20,12},{24,0},{28,4},{1,25},{... | collective-permute-start | bytes 393224 | tf_op jit(solution)/shard_map/ppermute | solution.py:42
  20.4 9.9 %collective-permute-start.5 = (bf16[4,64,256]{2,1,0:T(8,128)(2,1)S(1)}, bf16[4,64,256]{2,1,0:T(8,128)(2,1)S(1)}, u32[]{:S(2)}, u32[]{:S(2)}) collective-permute-start(bf16[4,64,256]{2,1,0:T(8,128)(2,1)S(1)} %get-tuple-element.40), channel_id=1, source_target_pairs={{0,8},{4,12},{8,0},{12,4},{16,24},{20,28},{24,16},{28,20},{1,9},{5... | collective-permute-start | bytes 393224 | tf_op jit(solution)/shard_map/ppermute | solution.py:42
  22.0 8.8 %collective-permute-start.6 = (bf16[4,64,256]{2,1,0:T(8,128)(2,1)S(1)}, bf16[4,64,256]{2,1,0:T(8,128)(2,1)S(1)}, u32[]{:S(2)}, u32[]{:S(2)}) collective-permute-start(bf16[4,64,256]{2,1,0:T(8,128)(2,1)S(1)} %get-tuple-element.41), channel_id=1, source_target_pairs={{0,16},{4,20},{8,24},{12,28},{16,0},{20,4},{24,8},{28,12},{1,17},{... | collective-permute-start | bytes 393224 | tf_op jit(solution)/shard_map/ppermute | solution.py:42
  22.5 9.8 %collective-permute-start.7 = (bf16[4,64,256]{2,1,0:T(8,128)(2,1)S(1)}, bf16[4,64,256]{2,1,0:T(8,128)(2,1)S(1)}, u32[]{:S(2)}, u32[]{:S(2)}) collective-permute-start(bf16[4,64,256]{2,1,0:T(8,128)(2,1)S(1)} %get-tuple-element.42), channel_id=1, source_target_pairs={{0,24},{4,28},{8,16},{12,20},{16,8},{20,12},{24,0},{28,4},{1,25},{... | collective-permute-start | bytes 393224 | tf_op jit(solution)/shard_map/ppermute | solution.py:42
  28.8 8.0 %collective-permute-start.15 = (bf16[4,64,256]{2,1,0:T(8,128)(2,1)S(1)}, bf16[4,64,256]{2,1,0:T(8,128)(2,1)S(1)}, u32[]{:S(2)}, u32[]{:S(2)}) collective-permute-start(bf16[4,64,256]{2,1,0:T(8,128)(2,1)S(1)} %get-tuple-element.52), channel_id=1, source_target_pairs={{0,8},{4,12},{8,0},{12,4},{16,24},{20,28},{24,16},{28,20},{1,9},{5... | collective-permute-start | bytes 393224 | tf_op jit(solution)/shard_map/ppermute | solution.py:42
  30.3 7.8 %collective-permute-start.16 = (bf16[4,64,256]{2,1,0:T(8,128)(2,1)S(1)}, bf16[4,64,256]{2,1,0:T(8,128)(2,1)S(1)}, u32[]{:S(2)}, u32[]{:S(2)}) collective-permute-start(bf16[4,64,256]{2,1,0:T(8,128)(2,1)S(1)} %get-tuple-element.53), channel_id=1, source_target_pairs={{0,16},{4,20},{8,24},{12,28},{16,0},{20,4},{24,8},{28,12},{1,17},{... | collective-permute-start | bytes 393224 | tf_op jit(solution)/shard_map/ppermute | solution.py:42
  30.8 7.3 %collective-permute-start.17 = (bf16[4,64,256]{2,1,0:T(8,128)(2,1)S(1)}, bf16[4,64,256]{2,1,0:T(8,128)(2,1)S(1)}, u32[]{:S(2)}, u32[]{:S(2)}) collective-permute-start(bf16[4,64,256]{2,1,0:T(8,128)(2,1)S(1)} %get-tuple-element.54), channel_id=1, source_target_pairs={{0,24},{4,28},{8,16},{12,20},{16,8},{20,12},{24,0},{28,4},{1,25},{... | collective-permute-start | bytes 393224 | tf_op jit(solution)/shard_map/ppermute | solution.py:42
  32.4 8.9 %collective-permute-start.8 = (bf16[4,16,256]{2,1,0:T(8,128)(2,1)S(1)}, bf16[4,16,256]{2,1,0:T(8,128)(2,1)S(1)}, u32[]{:S(2)}, u32[]{:S(2)}) collective-permute-start(bf16[4,16,256]{2,1,0:T(8,128)(2,1)S(1)} %get-tuple-element.44), channel_id=1, source_target_pairs={{0,1},{1,0},{2,3},{3,2},{4,5},{5,4},{6,7},{7,6},{8,9},{9,8},{10,11... | collective-permute-start | bytes 98312 | tf_op jit(solution)/shard_map/ppermute | solution.py:46
  34.1 9.7 %collective-permute-start.9 = (bf16[4,16,256]{2,1,0:T(8,128)(2,1)S(1)}, bf16[4,16,256]{2,1,0:T(8,128)(2,1)S(1)}, u32[]{:S(2)}, u32[]{:S(2)}) collective-permute-start(bf16[4,16,256]{2,1,0:T(8,128)(2,1)S(1)} %get-tuple-element.45), channel_id=1, source_target_pairs={{0,2},{1,3},{2,0},{3,1},{4,6},{5,7},{6,4},{7,5},{8,10},{9,11},{10,... | collective-permute-start | bytes 98312 | tf_op jit(solution)/shard_map/ppermute | solution.py:46
  36.7 7.0 %collective-permute-start.10 = (bf16[4,16,256]{2,1,0:T(8,128)(2,1)S(1)}, bf16[4,16,256]{2,1,0:T(8,128)(2,1)S(1)}, u32[]{:S(2)}, u32[]{:S(2)}) collective-permute-start(bf16[4,16,256]{2,1,0:T(8,128)(2,1)S(1)} %get-tuple-element.46), channel_id=1, source_target_pairs={{0,3},{1,2},{2,1},{3,0},{4,7},{5,6},{6,5},{7,4},{8,11},{9,10},{10,... | collective-permute-start | bytes 98312 | tf_op jit(solution)/shard_map/ppermute | solution.py:46
  38.2 5.6 %collective-permute-start.18 = (bf16[4,16,256]{2,1,0:T(8,128)(2,1)S(1)}, bf16[4,16,256]{2,1,0:T(8,128)(2,1)S(1)}, u32[]{:S(2)}, u32[]{:S(2)}) collective-permute-start(bf16[4,16,256]{2,1,0:T(8,128)(2,1)S(1)} %get-tuple-element.56), channel_id=1, source_target_pairs={{0,1},{1,0},{2,3},{3,2},{4,5},{5,4},{6,7},{7,6},{8,9},{9,8},{10,11... | collective-permute-start | bytes 98312 | tf_op jit(solution)/shard_map/ppermute | solution.py:46
  38.7 5.1 %collective-permute-start.19 = (bf16[4,16,256]{2,1,0:T(8,128)(2,1)S(1)}, bf16[4,16,256]{2,1,0:T(8,128)(2,1)S(1)}, u32[]{:S(2)}, u32[]{:S(2)}) collective-permute-start(bf16[4,16,256]{2,1,0:T(8,128)(2,1)S(1)} %get-tuple-element.57), channel_id=1, source_target_pairs={{0,2},{1,3},{2,0},{3,1},{4,6},{5,7},{6,4},{7,5},{8,10},{9,11},{10,... | collective-permute-start | bytes 98312 | tf_op jit(solution)/shard_map/ppermute | solution.py:46
  41.3 5.9 %collective-permute-start.20 = (bf16[4,16,256]{2,1,0:T(8,128)(2,1)S(1)}, bf16[4,16,256]{2,1,0:T(8,128)(2,1)S(1)}, u32[]{:S(2)}, u32[]{:S(2)}) collective-permute-start(bf16[4,16,256]{2,1,0:T(8,128)(2,1)S(1)} %get-tuple-element.58), channel_id=1, source_target_pairs={{0,3},{1,2},{2,1},{3,0},{4,7},{5,6},{6,5},{7,4},{8,11},{9,10},{10,... | collective-permute-start | bytes 98312 | tf_op jit(solution)/shard_map/ppermute | solution.py:46
  43.5 3.7 %copy-start.3 = (bf16[256,256]{1,0:T(8,128)(2,1)S(1)}, bf16[256,256]{1,0:T(8,128)(2,1)}, u32[]{:S(2)}) copy-start(bf16[256,256]{1,0:T(8,128)(2,1)} %constant.32.clone.refs_10_) | copy-start | bytes 393220
  43.5 3.7 %copy-start.4 = (bf16[256,256]{1,0:T(8,128)(2,1)S(1)}, bf16[256,256]{1,0:T(8,128)(2,1)}, u32[]{:S(2)}) copy-start(bf16[256,256]{1,0:T(8,128)(2,1)} %constant.33.clone.refs_11_) | copy-start | bytes 393220
  43.5 3.7 %copy-start.5 = (bf16[256,256]{1,0:T(8,128)(2,1)S(1)}, bf16[256,256]{1,0:T(8,128)(2,1)}, u32[]{:S(2)}) copy-start(bf16[256,256]{1,0:T(8,128)(2,1)} %constant.34.clone.refs_12_) | copy-start | bytes 393220
  43.5 3.7 %copy-start.6 = (bf16[256,256]{1,0:T(8,128)(2,1)S(1)}, bf16[256,256]{1,0:T(8,128)(2,1)}, u32[]{:S(2)}) copy-start(bf16[256,256]{1,0:T(8,128)(2,1)} %constant.35.clone.refs_13_) | copy-start | bytes 393220
  49.0 4.5 %collective-permute-start.22 = (bf16[8,16,256]{2,1,0:T(8,128)(2,1)S(1)}, bf16[8,16,256]{2,1,0:T(8,128)(2,1)S(1)}, u32[]{:S(2)}, u32[]{:S(2)}) collective-permute-start(bf16[8,16,256]{2,1,0:T(8,128)(2,1)S(1)} %get-tuple-element.60), channel_id=1, source_target_pairs={{0,1},{1,0},{2,3},{3,2},{4,5},{5,4},{6,7},{7,6},{8,9},{9,8},{10,11... | collective-permute-start | bytes 196616 | tf_op jit(solution)/shard_map/ppermute | solution.py:46
  49.1 5.2 %collective-permute-start.23 = (bf16[8,16,256]{2,1,0:T(8,128)(2,1)S(1)}, bf16[8,16,256]{2,1,0:T(8,128)(2,1)S(1)}, u32[]{:S(2)}, u32[]{:S(2)}) collective-permute-start(bf16[8,16,256]{2,1,0:T(8,128)(2,1)S(1)} %get-tuple-element.61), channel_id=1, source_target_pairs={{0,2},{1,3},{2,0},{3,1},{4,6},{5,7},{6,4},{7,5},{8,10},{9,11},{10,... | collective-permute-start | bytes 196616 | tf_op jit(solution)/shard_map/ppermute | solution.py:46
  50.9 6.1 %collective-permute-start.24 = (bf16[8,16,256]{2,1,0:T(8,128)(2,1)S(1)}, bf16[8,16,256]{2,1,0:T(8,128)(2,1)S(1)}, u32[]{:S(2)}, u32[]{:S(2)}) collective-permute-start(bf16[8,16,256]{2,1,0:T(8,128)(2,1)S(1)} %get-tuple-element.62), channel_id=1, source_target_pairs={{0,3},{1,2},{2,1},{3,0},{4,7},{5,6},{6,5},{7,4},{8,11},{9,10},{10,... | collective-permute-start | bytes 196616 | tf_op jit(solution)/shard_map/ppermute | solution.py:46
  57.1 1.4 %collective-permute-start.25 = (bf16[8,32,256]{2,1,0:T(8,128)(2,1)S(1)}, bf16[8,32,256]{2,1,0:T(8,128)(2,1)S(1)}, u32[]{:S(2)}, u32[]{:S(2)}) collective-permute-start(bf16[8,32,256]{2,1,0:T(8,128)(2,1)S(1)} %get-tuple-element.64), channel_id=1, source_target_pairs={{0,4},{4,0},{8,12},{12,8},{16,20},{20,16},{24,28},{28,24},{1,5},{5... | collective-permute-start | bytes 393224 | tf_op jit(solution)/shard_map/ppermute | solution.py:42
  (4 other events, 9.5 us)

commit v3 on v2

--- a/solution.py
+++ b/solution.py
@@ -9,6 +9,7 @@
 from jax.experimental.pallas import tpu as pltpu
 from jax.sharding import PartitionSpec as P
 
+
 BF16 = jnp.bfloat16
 F32 = jnp.float32
 CHUNKS = (1, 1)
@@ -19,7 +20,7 @@
     return math.prod(shape) * jnp.dtype(dtype).itemsize
 
 
-def call(kernel, name, outs, scratch=(), flops=0):
+def call(kernel, outs, scratch=(), flops=0):
     def run(*args):
         moved = sum(size_of(item.shape, item.dtype) for item in args)
         moved += sum(size_of(*out) for out in outs)
@@ -32,7 +33,6 @@
             scratch_shapes=[pltpu.VMEM(*item) for item in scratch],
             compiler_params=pltpu.CompilerParams(vmem_limit_bytes=moved + held + 3 * 2**20),
             cost_estimate=pl.CostEstimate(flops=flops, bytes_accessed=moved, transcendentals=0),
-            name=name,
         )(*args)
 
     return run
@@ -119,9 +119,14 @@
     lax.fori_loop(0, nb, one, 0)
 
 
-def step_kernel(nb, scale, times, full, *refs):
+def step_kernel(nb, scale, times, earlier, full, *refs):
+    carried, refs = refs[:earlier], refs[earlier:]
     chips = len(refs) - times - 1
     parts, outs, stepped = refs[:chips], refs[chips:-1], refs[-1]
+    ahead = 0
+    for block in carried:
+        outs[1][ahead : ahead + block.shape[0]] = block[...]
+        ahead += block.shape[0]
     z = lax.axis_index("tm")
     rows = full.shape[1]
     cut = rows // 2 // times
@@ -139,7 +144,8 @@
         for h in range(2):
             at = pl.multiple_of(h * (rows // 2) + (z ^ j) * cut, cut)
             for k in range(2 * nb):
-                outs[j][k, h * cut : (h + 1) * cut, :] = stepped[k, pl.ds(at, cut), :].astype(
+                to = k + (ahead if j == 1 else 0)
+                outs[j][to, h * cut : (h + 1) * cut, :] = stepped[k, pl.ds(at, cut), :].astype(
                     outs[j].dtype
                 )
 
@@ -163,11 +169,13 @@
 
 def wave_kernel(sizes, times, *refs):
     count = len(sizes)
-    blocks = refs[: times * count]
+    joint, refs = refs[0], refs[1:]
+    each = times - 1
+    blocks = refs[: each * count]
     phase_cos, phase_sin, cos_high, cos_low, sin_high, sin_low, twist_cos, twist_sin = refs[
-        times * count : times * count + 8
+        each * count : each * count + 8
     ]
-    outs = refs[times * count + 8 : -2]
+    outs = refs[each * count + 8 : -2]
     held, back = refs[-2:]
     z = lax.axis_index("tm")
     nb = sum(sizes)
@@ -176,11 +184,12 @@
     length = times * time
     start = 0
     for n, part in enumerate(sizes):
-        for j in range(times):
-            block = blocks[n * times + j]
+        own, *far = blocks[n * each : (n + 1) * each]
+        for j, block in enumerate([own, joint] + far):
             for c in range(2):
                 at = c * nb + start
-                held[z ^ j, at : at + part] = block[c * part : (c + 1) * part].astype(F32)
+                take = c * part + (2 * start if j == 1 else 0)
+                held[z ^ j, at : at + part] = block[take : take + part].astype(F32)
         start += part
     here = [
         (held[a, :nb].reshape(size, time), held[a, nb:].reshape(size, time)) for a in range(times)
@@ -265,7 +274,6 @@
 
     halves = call(
         functools.partial(split_kernel, starts, sizes),
-        "split",
         [((2 * nb, modes, time), F32) for nb in sizes for _ in range(2)],
     )(fields)
     others = [swap_pix(halves[2 * n + 1], 1, pix) for n in range(len(sizes))]
@@ -275,15 +283,15 @@
     fulls, gathers = [], []
     for n, nb in enumerate(sizes):
         full, modal = call(
-            modal_kernel, "modal", [((2 * nb, rows, time), F32), ((2 * nb, rows, time), BF16)]
+            modal_kernel, [((2 * nb, rows, time), F32), ((2 * nb, rows, time), BF16)]
         )(halves[2 * n], others[n])
         fulls.append(full)
         gathers.append([modal] + [swap_pix(modal, 2 * j, pix) for j in range(1, chips)])
 
-    turn = call(
-        functools.partial(turn_kernel, rows, chips), "turn", [((chips * rows, pixels), BF16)]
-    )
-    turned = turn(profiles)[0], turn(profiles_other)[0]
+    turn = call(functools.partial(turn_kernel, rows, chips), [((chips * rows, pixels), BF16)])
+    turned = []
+    for value in (profiles, profiles_other):
+        turned += turn(value)
 
     low = jnp.where(core == 0, phase, phase_other)
     high = jnp.where(core == 0, phase_other, phase)
@@ -291,29 +299,31 @@
     phase_cos, phase_sin = jnp.cos(angles), jnp.sin(angles)
     consts = tables(times, time)
 
-    waves = []
+    waves, near = [], []
     for n, nb in enumerate(sizes):
         block = (2 * nb, rows, time)
         parts = call(
             functools.partial(kerr_kernel, nb, chips, 512),
-            "kerr",
             [(block, F32)] + [(block, BF16)] * (chips - 1),
             [((chips * rows, 2 * time), BF16), ((2 * pixels, 2 * time), BF16)],
             flops=16 * pixels * chips * rows * nb * time,
         )(profiles, profiles_other, *turned, *gathers[n])
         sums = [parts[0]] + [swap_pix(parts[j], 2 * j, pix) for j in range(1, chips)]
         block = (2 * nb, cut, time)
+        last = n == len(sizes) - 1
+        joint = (2 * half, cut, time) if last else block
+        carried = near if last else []
         pieces = call(
-            functools.partial(step_kernel, nb, scale, times),
-            "step",
-            [(block, F32)] + [(block, BF16)] * (times - 1),
+            functools.partial(step_kernel, nb, scale, times, len(carried)),
+            [(block, F32), (joint, BF16)] + [(block, BF16)] * (times - 2),
             [((2 * nb, rows, time), F32)],
-        )(fulls[n], *sums)
-        waves += [pieces[0]] + [swap_tm(pieces[j], j, times) for j in range(1, times)]
+        )(fulls[n], *carried, *sums)
+        near.append(pieces[1])
+        waves += [pieces[0]] + [swap_tm(pieces[j], j, times) for j in range(2, times)]
+    waves = [swap_tm(near[-1], 1, times)] + waves
     block = (2 * half, cut, time)
     pieces = call(
         functools.partial(wave_kernel, sizes, times),
-        "wave",
         [(block, F32)] + [(block, BF16)] * (times - 1),
         [((times,) + block, F32)] * 2,
         flops=10**9,
@@ -322,11 +332,10 @@
     block = (2 * half, modes, time)
     own, other = call(
         functools.partial(part_kernel, times),
-        "part",
         [(block, F32), (block, BF16)],
         [((2 * half, cut, time), F32), (block, F32)],
     )(*pieces)
-    return call(join_kernel, "join", [(fields.shape, F32)])(own, swap_pix(other, 1, pix))[0]
+    return call(join_kernel, [(fields.shape, F32)])(own, swap_pix(other, 1, pix))[0]
 
 
 def split_length(length):

time: 59.7 us -> 66.3 us (1.11)
  waiting for transfers between devices: 9.98 us -> 18.9 us
  starting transfers between devices: 32.4 us -> 30.2 us
    ppermute x17, waiting for transfers between devices: 3.04 us -> 11.4 us  [swap_pix(): return lax.ppermute(value, 'pix', [(i, i ^ mask) for i in range(size)])]
    ppermute x9 -> x8, starting transfers between devices: 14.6 us -> 12.4 us  [swap_tm(): return lax.ppermute(value, 'tm', [(i, i ^ mask) for i in range(size)])]
    ppermute x9 -> x8, waiting for transfers between devices: 6.94 us -> 7.5 us  [swap_tm(): return lax.ppermute(value, 'tm', [(i, i ^ mask) for i in range(size)])]
  transfers between devices with their start and end apart: 26 -> 25, of which waited for: 6 -> 11; matrix products, arithmetic and copies ran while one was open for 2% -> 2% of each run, Pallas kernels for 18% -> 16%
where the time goes in v3:
time: 66.3 us; the launch traced here: 66.2 us
  starting transfers between devices  30.2 us (46%)
  waiting for transfers between devices  18.9 us (29%)
  Pallas kernels  13.5 us (20%)
  local copies, waits for them, and re-layouts  3.08 us (5%)
    ppermute x17, starting transfers between devices, swap_pix(): return lax.ppermute(value, 'pix', [(i, i ^ mask) for i in range(size)])  17.7 us
    pallas_call x12, Pallas kernels, run(): pl.pallas_call(kernel, out_shape=tuple((jax.ShapeDtypeStruct(*out) for ou...  13.5 us
    ppermute x8, starting transfers between devices, swap_tm(): return lax.ppermute(value, 'tm', [(i, i ^ mask) for i in range(size)])  12.4 us
    ppermute x17, waiting for transfers between devices, swap_pix(): return lax.ppermute(value, 'pix', [(i, i ^ mask) for i in range(size)])  11.4 us
    ppermute x8, waiting for transfers between devices, swap_tm(): return lax.ppermute(value, 'tm', [(i, i ^ mask) for i in range(size)])  7.5 us
    unnamed x20, local copies, waits for them, and re-layouts  2.31 us
  transfers between devices with their start and end apart: 25, of which 11 were waited for; matrix products, arithmetic and copies ran while one was open for 2% of the time, Pallas kernels for 16%

profile of v3, /device:TPU:0, one launch (start us, length us, event | category | flops | bytes accessed | tf_op | source)
XLA Modules:
  0.0 66.2 jit_solution(2144244281099460201)
XLA Ops:
  0.5 1.0 %copy-done.2 = f32[32,8,2,256]{3,2,1,0:T(2,128)S(1)} copy-done((f32[32,8,2,256]{3,2,1,0:T(2,128)S(1)}, f32[32,8,2,256]{3,2,1,0:T(2,128)}, u32[]{:S(2)}) %copy-start.2) | copy-done | bytes 524312
  2.3 0.9 %collective-permute-done.1.other = f32[4,32,256]{2,1,0:T(8,128)S(1)} collective-permute-done((f32[4,32,256]{2,1,0:T(8,128)S(1)}, f32[4,32,256]{2,1,0:T(8,128)S(1)}, u32[]{:S(2)}, u32[]{:S(2)}) %collective-permute-start.1) | collective-permute-done | bytes 131104 | tf_op jit(solution)/shard_map/ppermute | solution.py:42
  3.2 2.9 %collective-permute-start.3 = (bf16[4,64,256]{2,1,0:T(8,128)(2,1)S(1)}, bf16[4,64,256]{2,1,0:T(8,128)(2,1)S(1)}, u32[]{:S(2)}, u32[]{:S(2)}) collective-permute-start(bf16[4,64,256]{2,1,0:T(8,128)(2,1)S(1)} %get-tuple-element.41.refs_4_), channel_id=1, source_target_pairs={{0,8},{4,12},{8,0},{12,4},{16,24},{20,28},{24,16},{28,20},{1,9},{5... | collective-permute-start | bytes 393224 | tf_op jit(solution)/shard_map/ppermute | solution.py:42
  6.1 1.5 %collective-permute-start.4 = (bf16[4,64,256]{2,1,0:T(8,128)(2,1)S(1)}, bf16[4,64,256]{2,1,0:T(8,128)(2,1)S(1)}, u32[]{:S(2)}, u32[]{:S(2)}) collective-permute-start(bf16[4,64,256]{2,1,0:T(8,128)(2,1)S(1)} %get-tuple-element.41.refs_4_), channel_id=1, source_target_pairs={{0,16},{4,20},{8,24},{12,28},{16,0},{20,4},{24,8},{28,12},{1,17},{... | collective-permute-start | bytes 393224 | tf_op jit(solution)/shard_map/ppermute | solution.py:42
  7.7 1.2 %copy-done = bf16[2048,256]{1,0:T(8,128)(2,1)S(1)} copy-done((bf16[2048,256]{1,0:T(8,128)(2,1)S(1)}, bf16[2048,256]{1,0:T(8,128)(2,1)}, u32[]{:S(2)}) %copy-start) | copy-done | bytes 1048600
  9.4 2.0 %collective-permute-start.10 = (bf16[4,64,256]{2,1,0:T(8,128)(2,1)S(1)}, bf16[4,64,256]{2,1,0:T(8,128)(2,1)S(1)}, u32[]{:S(2)}, u32[]{:S(2)}) collective-permute-start(bf16[4,64,256]{2,1,0:T(8,128)(2,1)S(1)} %get-tuple-element.47.refs_4_), channel_id=1, source_target_pairs={{0,16},{4,20},{8,24},{12,28},{16,0},{20,4},{24,8},{28,12},{1,17},{... | collective-permute-start | bytes 393224 | tf_op jit(solution)/shard_map/ppermute | solution.py:42
  11.8 1.6 %collective-permute-start.11 = (bf16[4,64,256]{2,1,0:T(8,128)(2,1)S(1)}, bf16[4,64,256]{2,1,0:T(8,128)(2,1)S(1)}, u32[]{:S(2)}, u32[]{:S(2)}) collective-permute-start(bf16[4,64,256]{2,1,0:T(8,128)(2,1)S(1)} %get-tuple-element.47.refs_4_), channel_id=1, source_target_pairs={{0,24},{4,28},{8,16},{12,20},{16,8},{20,12},{24,0},{28,4},{1,25},{... | collective-permute-start | bytes 393224 | tf_op jit(solution)/shard_map/ppermute | solution.py:42
  13.5 3.4 %collective-permute-done.4.refs_6_ = bf16[4,64,256]{2,1,0:T(8,128)(2,1)S(1)} collective-permute-done((bf16[4,64,256]{2,1,0:T(8,128)(2,1)S(1)}, bf16[4,64,256]{2,1,0:T(8,128)(2,1)S(1)}, u32[]{:S(2)}, u32[]{:S(2)}) %collective-permute-start.4) | collective-permute-done | bytes 131104 | tf_op jit(solution)/shard_map/ppermute | solution.py:42
  16.9 4.8 %shard_map.96 = (f32[4,64,256]{2,1,0:T(8,128)S(1)}, bf16[4,64,256]{2,1,0:T(8,128)(2,1)S(1)}, bf16[4,64,256]{2,1,0:T(8,128)(2,1)S(1)}, bf16[4,64,256]{2,1,0:T(8,128)(2,1)S(1)}) custom-call(bf16[2048,256]{1,0:T(8,128)(2,1)S(1)} %copy-done.1, bf16[2048,256]{1,0:T(8,128)(2,1)S(1)} %collective-permute-done.2.profiles.refs_1_, ...), custom_call_target="tpu_custom_call" | custom-call | flops 4294967296 | bytes 5373952 | tf_op jit(solution)/shard_map/pallas_call | solution.py:28
  21.7 2.1 %collective-permute-start.6 = (bf16[4,64,256]{2,1,0:T(8,128)(2,1)S(1)}, bf16[4,64,256]{2,1,0:T(8,128)(2,1)S(1)}, u32[]{:S(2)}, u32[]{:S(2)}) collective-permute-start(bf16[4,64,256]{2,1,0:T(8,128)(2,1)S(1)} %get-tuple-element.43), channel_id=1, source_target_pairs={{0,8},{4,12},{8,0},{12,4},{16,24},{20,28},{24,16},{28,20},{1,9},{5... | collective-permute-start | bytes 393224 | tf_op jit(solution)/shard_map/ppermute | solution.py:42
  23.7 2.8 %collective-permute-start.7 = (bf16[4,64,256]{2,1,0:T(8,128)(2,1)S(1)}, bf16[4,64,256]{2,1,0:T(8,128)(2,1)S(1)}, u32[]{:S(2)}, u32[]{:S(2)}) collective-permute-start(bf16[4,64,256]{2,1,0:T(8,128)(2,1)S(1)} %get-tuple-element.44), channel_id=1, source_target_pairs={{0,16},{4,20},{8,24},{12,28},{16,0},{20,4},{24,8},{28,12},{1,17},{... | collective-permute-start | bytes 393224 | tf_op jit(solution)/shard_map/ppermute | solution.py:42
  26.5 4.8 %shard_map.98 = (f32[4,64,256]{2,1,0:T(8,128)S(1)}, bf16[4,64,256]{2,1,0:T(8,128)(2,1)S(1)}, bf16[4,64,256]{2,1,0:T(8,128)(2,1)S(1)}, bf16[4,64,256]{2,1,0:T(8,128)(2,1)S(1)}) custom-call(bf16[2048,256]{1,0:T(8,128)(2,1)S(1)} %copy-done.1, bf16[2048,256]{1,0:T(8,128)(2,1)S(1)} %collective-permute-done.2.profiles.refs_1_, ...), custom_call_target="tpu_custom_call" | custom-call | flops 4294967296 | bytes 5373952 | tf_op jit(solution)/shard_map/pallas_call | solution.py:28
  31.3 1.6 %collective-permute-start.12 = (bf16[4,64,256]{2,1,0:T(8,128)(2,1)S(1)}, bf16[4,64,256]{2,1,0:T(8,128)(2,1)S(1)}, u32[]{:S(2)}, u32[]{:S(2)}) collective-permute-start(bf16[4,64,256]{2,1,0:T(8,128)(2,1)S(1)} %get-tuple-element.49), channel_id=1, source_target_pairs={{0,8},{4,12},{8,0},{12,4},{16,24},{20,28},{24,16},{28,20},{1,9},{5... | collective-permute-start | bytes 393224 | tf_op jit(solution)/shard_map/ppermute | solution.py:42
  32.9 2.0 %collective-permute-start.13 = (bf16[4,64,256]{2,1,0:T(8,128)(2,1)S(1)}, bf16[4,64,256]{2,1,0:T(8,128)(2,1)S(1)}, u32[]{:S(2)}, u32[]{:S(2)}) collective-permute-start(bf16[4,64,256]{2,1,0:T(8,128)(2,1)S(1)} %get-tuple-element.50), channel_id=1, source_target_pairs={{0,16},{4,20},{8,24},{12,28},{16,0},{20,4},{24,8},{28,12},{1,17},{... | collective-permute-start | bytes 393224 | tf_op jit(solution)/shard_map/ppermute | solution.py:42
  35.0 1.3 %collective-permute-done.12.refs_2_ = bf16[4,64,256]{2,1,0:T(8,128)(2,1)S(1)} collective-permute-done((bf16[4,64,256]{2,1,0:T(8,128)(2,1)S(1)}, bf16[4,64,256]{2,1,0:T(8,128)(2,1)S(1)}, u32[]{:S(2)}, u32[]{:S(2)}) %collective-permute-start.12) | collective-permute-done | bytes 131104 | tf_op jit(solution)/shard_map/ppermute | solution.py:42
  36.3 2.4 %collective-permute-done.13.refs_3_ = bf16[4,64,256]{2,1,0:T(8,128)(2,1)S(1)} collective-permute-done((bf16[4,64,256]{2,1,0:T(8,128)(2,1)S(1)}, bf16[4,64,256]{2,1,0:T(8,128)(2,1)S(1)}, u32[]{:S(2)}, u32[]{:S(2)}) %collective-permute-start.13) | collective-permute-done | bytes 131104 | tf_op jit(solution)/shard_map/ppermute | solution.py:42
  38.7 1.9 %collective-permute-done.14.refs_4_ = bf16[4,64,256]{2,1,0:T(8,128)(2,1)S(1)} collective-permute-done((bf16[4,64,256]{2,1,0:T(8,128)(2,1)S(1)}, bf16[4,64,256]{2,1,0:T(8,128)(2,1)S(1)}, u32[]{:S(2)}, u32[]{:S(2)}) %collective-permute-start.14) | collective-permute-done | bytes 131104 | tf_op jit(solution)/shard_map/ppermute | solution.py:42
  40.8 1.6 %collective-permute-start.15 = (bf16[8,16,256]{2,1,0:T(8,128)(2,1)S(1)}, bf16[8,16,256]{2,1,0:T(8,128)(2,1)S(1)}, u32[]{:S(2)}, u32[]{:S(2)}) collective-permute-start(bf16[8,16,256]{2,1,0:T(8,128)(2,1)S(1)} %get-tuple-element.52), channel_id=1, source_target_pairs={{0,1},{1,0},{2,3},{3,2},{4,5},{5,4},{6,7},{7,6},{8,9},{9,8},{10,11... | collective-permute-start | bytes 196616 | tf_op jit(solution)/shard_map/ppermute | solution.py:46
  42.3 2.6 %collective-permute-start.18 = (bf16[4,16,256]{2,1,0:T(8,128)(2,1)S(1)}, bf16[4,16,256]{2,1,0:T(8,128)(2,1)S(1)}, u32[]{:S(2)}, u32[]{:S(2)}) collective-permute-start(bf16[4,16,256]{2,1,0:T(8,128)(2,1)S(1)} %get-tuple-element.57), channel_id=1, source_target_pairs={{0,2},{1,3},{2,0},{3,1},{4,6},{5,7},{6,4},{7,5},{8,10},{9,11},{10,... | collective-permute-start | bytes 98312 | tf_op jit(solution)/shard_map/ppermute | solution.py:46
  45.2 1.6 %collective-permute-start.16 = (bf16[4,16,256]{2,1,0:T(8,128)(2,1)S(1)}, bf16[4,16,256]{2,1,0:T(8,128)(2,1)S(1)}, u32[]{:S(2)}, u32[]{:S(2)}) collective-permute-start(bf16[4,16,256]{2,1,0:T(8,128)(2,1)S(1)} %get-tuple-element.54), channel_id=1, source_target_pairs={{0,2},{1,3},{2,0},{3,1},{4,6},{5,7},{6,4},{7,5},{8,10},{9,11},{10,... | collective-permute-start | bytes 98312 | tf_op jit(solution)/shard_map/ppermute | solution.py:46
  46.9 1.9 %collective-permute-start.17 = (bf16[4,16,256]{2,1,0:T(8,128)(2,1)S(1)}, bf16[4,16,256]{2,1,0:T(8,128)(2,1)S(1)}, u32[]{:S(2)}, u32[]{:S(2)}) collective-permute-start(bf16[4,16,256]{2,1,0:T(8,128)(2,1)S(1)} %get-tuple-element.55), channel_id=1, source_target_pairs={{0,3},{1,2},{2,1},{3,0},{4,7},{5,6},{6,5},{7,4},{8,11},{9,10},{10,... | collective-permute-start | bytes 98312 | tf_op jit(solution)/shard_map/ppermute | solution.py:46
  49.9 1.2 %collective-permute-done.19.refs_6_ = bf16[4,16,256]{2,1,0:T(8,128)(2,1)S(1)} collective-permute-done((bf16[4,16,256]{2,1,0:T(8,128)(2,1)S(1)}, bf16[4,16,256]{2,1,0:T(8,128)(2,1)S(1)}, u32[]{:S(2)}, u32[]{:S(2)}) %collective-permute-start.19) | collective-permute-done | bytes 32800 | tf_op jit(solution)/shard_map/ppermute | solution.py:46
  51.1 0.7 %collective-permute-done.16.refs_2_ = bf16[4,16,256]{2,1,0:T(8,128)(2,1)S(1)} collective-permute-done((bf16[4,16,256]{2,1,0:T(8,128)(2,1)S(1)}, bf16[4,16,256]{2,1,0:T(8,128)(2,1)S(1)}, u32[]{:S(2)}, u32[]{:S(2)}) %collective-permute-start.16) | collective-permute-done | bytes 32800 | tf_op jit(solution)/shard_map/ppermute | solution.py:46
  51.8 1.1 %collective-permute-done.17.refs_3_ = bf16[4,16,256]{2,1,0:T(8,128)(2,1)S(1)} collective-permute-done((bf16[4,16,256]{2,1,0:T(8,128)(2,1)S(1)}, bf16[4,16,256]{2,1,0:T(8,128)(2,1)S(1)}, u32[]{:S(2)}, u32[]{:S(2)}) %collective-permute-start.17) | collective-permute-done | bytes 32800 | tf_op jit(solution)/shard_map/ppermute | solution.py:46
  53.0 1.8 %shard_map.100 = (f32[8,16,256]{2,1,0:T(8,128)S(1)}, bf16[8,16,256]{2,1,0:T(8,128)(2,1)S(1)}, bf16[8,16,256]{2,1,0:T(8,128)(2,1)S(1)}, bf16[8,16,256]{2,1,0:T(8,128)(2,1)S(1)}) custom-call(bf16[8,16,256]{2,1,0:T(8,128)(2,1)S(1)} %collective-permute-done.15.refs_0_, f32[4,16,256]{2,1,0:T(8,128)S(1)} %get-tuple-element.53.refs_1_, ...), custom_call_target="tpu_custom_call" | custom-call | flops 1000000000 | bytes 1318912 | tf_op jit(solution)/shard_map/pallas_call | solution.py:28
  54.7 1.5 %collective-permute-start.21 = (bf16[8,16,256]{2,1,0:T(8,128)(2,1)S(1)}, bf16[8,16,256]{2,1,0:T(8,128)(2,1)S(1)}, u32[]{:S(2)}, u32[]{:S(2)}) collective-permute-start(bf16[8,16,256]{2,1,0:T(8,128)(2,1)S(1)} %get-tuple-element.60), channel_id=1, source_target_pairs={{0,1},{1,0},{2,3},{3,2},{4,5},{5,4},{6,7},{7,6},{8,9},{9,8},{10,11... | collective-permute-start | bytes 196616 | tf_op jit(solution)/shard_map/ppermute | solution.py:46
  56.2 1.3 %collective-permute-start.22 = (bf16[8,16,256]{2,1,0:T(8,128)(2,1)S(1)}, bf16[8,16,256]{2,1,0:T(8,128)(2,1)S(1)}, u32[]{:S(2)}, u32[]{:S(2)}) collective-permute-start(bf16[8,16,256]{2,1,0:T(8,128)(2,1)S(1)} %get-tuple-element.61), channel_id=1, source_target_pairs={{0,2},{1,3},{2,0},{3,1},{4,6},{5,7},{6,4},{7,5},{8,10},{9,11},{10,... | collective-permute-start | bytes 196616 | tf_op jit(solution)/shard_map/ppermute | solution.py:46
  57.6 1.6 %collective-permute-start.23 = (bf16[8,16,256]{2,1,0:T(8,128)(2,1)S(1)}, bf16[8,16,256]{2,1,0:T(8,128)(2,1)S(1)}, u32[]{:S(2)}, u32[]{:S(2)}) collective-permute-start(bf16[8,16,256]{2,1,0:T(8,128)(2,1)S(1)} %get-tuple-element.62), channel_id=1, source_target_pairs={{0,3},{1,2},{2,1},{3,0},{4,7},{5,6},{6,5},{7,4},{8,11},{9,10},{10,... | collective-permute-start | bytes 196616 | tf_op jit(solution)/shard_map/ppermute | solution.py:46
  59.2 2.9 %collective-permute-done.22.refs_2_ = bf16[8,16,256]{2,1,0:T(8,128)(2,1)S(1)} collective-permute-done((bf16[8,16,256]{2,1,0:T(8,128)(2,1)S(1)}, bf16[8,16,256]{2,1,0:T(8,128)(2,1)S(1)}, u32[]{:S(2)}, u32[]{:S(2)}) %collective-permute-start.22) | collective-permute-done | bytes 65568 | tf_op jit(solution)/shard_map/ppermute | solution.py:46
  62.1 1.5 %collective-permute-done.23.refs_3_ = bf16[8,16,256]{2,1,0:T(8,128)(2,1)S(1)} collective-permute-done((bf16[8,16,256]{2,1,0:T(8,128)(2,1)S(1)}, bf16[8,16,256]{2,1,0:T(8,128)(2,1)S(1)}, u32[]{:S(2)}, u32[]{:S(2)}) %collective-permute-start.23) | collective-permute-done | bytes 65568 | tf_op jit(solution)/shard_map/ppermute | solution.py:46
  63.8 1.3 %collective-permute-done.24.other = bf16[8,32,256]{2,1,0:T(8,128)(2,1)S(1)} collective-permute-done((bf16[8,32,256]{2,1,0:T(8,128)(2,1)S(1)}, bf16[8,32,256]{2,1,0:T(8,128)(2,1)S(1)}, u32[]{:S(2)}, u32[]{:S(2)}) %collective-permute-start.24) | collective-permute-done | bytes 131104 | tf_op jit(solution)/shard_map/ppermute | solution.py:42
  65.1 1.0 %shard_map.102 = f32[32,8,2,256]{3,2,1,0:T(2,128)} custom-call(f32[8,32,256]{2,1,0:T(8,128)S(1)} %get-tuple-element.63.own, bf16[8,32,256]{2,1,0:T(8,128)(2,1)S(1)} %collective-permute-done.24.other), custom_call_target="tpu_custom_call" | custom-call | bytes 917504 | tf_op jit(solution)/shard_map/pallas_call | solution.py:28
  (56 shorter events, 3.9 us)
Async XLA Ops:
  0.0 9.4 %collective-permute-start.2 = (bf16[2048,256]{1,0:T(8,128)(2,1)}, bf16[2048,256]{1,0:T(8,128)(2,1)S(1)}, u32[]{:S(2)}, u32[]{:S(2)}) collective-permute-start(bf16[2048,256]{1,0:T(8,128)(2,1)} %refs_0_.3), channel_id=1, source_target_pairs={{0,4},{4,0},{8,12},{12,8},{16,20},{20,16},{24,28},{28,24},{1,5},{5... | collective-permute-start | bytes 3145736 | tf_op jit(solution)/shard_map/ppermute | solution.py:42
  1.7 1.4 %collective-permute-start.1 = (f32[4,32,256]{2,1,0:T(8,128)S(1)}, f32[4,32,256]{2,1,0:T(8,128)S(1)}, u32[]{:S(2)}, u32[]{:S(2)}) collective-permute-start(f32[4,32,256]{2,1,0:T(8,128)S(1)} %get-tuple-element.39), channel_id=1, source_target_pairs={{0,4},{4,0},{8,12},{12,8},{16,20},{20,16},{24,28},{28,24},{1,5},{5... | collective-permute-start | bytes 393224 | tf_op jit(solution)/shard_map/ppermute | solution.py:42
  1.8 7.4 %collective-permute-start = (f32[4,32,256]{2,1,0:T(8,128)S(1)}, f32[4,32,256]{2,1,0:T(8,128)S(1)}, u32[]{:S(2)}, u32[]{:S(2)}) collective-permute-start(f32[4,32,256]{2,1,0:T(8,128)S(1)} %get-tuple-element.36), channel_id=1, source_target_pairs={{0,4},{4,0},{8,12},{12,8},{16,20},{20,16},{24,28},{28,24},{1,5},{5... | collective-permute-start | bytes 393224 | tf_op jit(solution)/shard_map/ppermute | solution.py:42
  3.2 6.1 %copy-start.9 = (f32[8,1024]{1,0:T(8,128)S(1)}, f32[8,1024]{1,0:T(8,128)}, u32[]{:S(2)}) copy-start(f32[8,1024]{1,0:T(8,128)} %param.11) | copy-start | bytes 98308
  3.2 8.6 %collective-permute-start.3 = (bf16[4,64,256]{2,1,0:T(8,128)(2,1)S(1)}, bf16[4,64,256]{2,1,0:T(8,128)(2,1)S(1)}, u32[]{:S(2)}, u32[]{:S(2)}) collective-permute-start(bf16[4,64,256]{2,1,0:T(8,128)(2,1)S(1)} %get-tuple-element.41.refs_4_), channel_id=1, source_target_pairs={{0,8},{4,12},{8,0},{12,4},{16,24},{20,28},{24,16},{28,20},{1,9},{5... | collective-permute-start | bytes 393224 | tf_op jit(solution)/shard_map/ppermute | solution.py:42
  6.1 10.7 %collective-permute-start.4 = (bf16[4,64,256]{2,1,0:T(8,128)(2,1)S(1)}, bf16[4,64,256]{2,1,0:T(8,128)(2,1)S(1)}, u32[]{:S(2)}, u32[]{:S(2)}) collective-permute-start(bf16[4,64,256]{2,1,0:T(8,128)(2,1)S(1)} %get-tuple-element.41.refs_4_), channel_id=1, source_target_pairs={{0,16},{4,20},{8,24},{12,28},{16,0},{20,4},{24,8},{28,12},{1,17},{... | collective-permute-start | bytes 393224 | tf_op jit(solution)/shard_map/ppermute | solution.py:42
  7.7 9.2 %collective-permute-start.5 = (bf16[4,64,256]{2,1,0:T(8,128)(2,1)S(1)}, bf16[4,64,256]{2,1,0:T(8,128)(2,1)S(1)}, u32[]{:S(2)}, u32[]{:S(2)}) collective-permute-start(bf16[4,64,256]{2,1,0:T(8,128)(2,1)S(1)} %get-tuple-element.41.refs_4_), channel_id=1, source_target_pairs={{0,24},{4,28},{8,16},{12,20},{16,8},{20,12},{24,0},{28,4},{1,25},{... | collective-permute-start | bytes 393224 | tf_op jit(solution)/shard_map/ppermute | solution.py:42
  9.3 23.6 %collective-permute-start.20 = (f32[8,1024]{1,0:T(8,128)S(1)}, f32[8,1024]{1,0:T(8,128)S(1)}, u32[]{:S(2)}, u32[]{:S(2)}) collective-permute-start(f32[8,1024]{1,0:T(8,128)S(1)} %copy-done.9), channel_id=1, source_target_pairs={{0,4},{4,0},{8,12},{12,8},{16,20},{20,16},{24,28},{28,24},{1,5},{5... | collective-permute-start | bytes 98312 | tf_op jit(solution)/shard_map/ppermute | solution.py:42
  9.4 7.5 %copy-start.1 = (bf16[2048,256]{1,0:T(8,128)(2,1)S(1)}, bf16[2048,256]{1,0:T(8,128)(2,1)}, u32[]{:S(2)}) copy-start(bf16[2048,256]{1,0:T(8,128)(2,1)} %refs_0_.3) | copy-start | bytes 3145732
  9.4 14.3 %collective-permute-start.10 = (bf16[4,64,256]{2,1,0:T(8,128)(2,1)S(1)}, bf16[4,64,256]{2,1,0:T(8,128)(2,1)S(1)}, u32[]{:S(2)}, u32[]{:S(2)}) collective-permute-start(bf16[4,64,256]{2,1,0:T(8,128)(2,1)S(1)} %get-tuple-element.47.refs_4_), channel_id=1, source_target_pairs={{0,16},{4,20},{8,24},{12,28},{16,0},{20,4},{24,8},{28,12},{1,17},{... | collective-permute-start | bytes 393224 | tf_op jit(solution)/shard_map/ppermute | solution.py:42
  11.8 14.7 %collective-permute-start.11 = (bf16[4,64,256]{2,1,0:T(8,128)(2,1)S(1)}, bf16[4,64,256]{2,1,0:T(8,128)(2,1)S(1)}, u32[]{:S(2)}, u32[]{:S(2)}) collective-permute-start(bf16[4,64,256]{2,1,0:T(8,128)(2,1)S(1)} %get-tuple-element.47.refs_4_), channel_id=1, source_target_pairs={{0,24},{4,28},{8,16},{12,20},{16,8},{20,12},{24,0},{28,4},{1,25},{... | collective-permute-start | bytes 393224 | tf_op jit(solution)/shard_map/ppermute | solution.py:42
  16.9 9.6 %collective-permute-start.9 = (bf16[4,64,256]{2,1,0:T(8,128)(2,1)S(1)}, bf16[4,64,256]{2,1,0:T(8,128)(2,1)S(1)}, u32[]{:S(2)}, u32[]{:S(2)}) collective-permute-start(bf16[4,64,256]{2,1,0:T(8,128)(2,1)S(1)} %get-tuple-element.47.refs_4_), channel_id=1, source_target_pairs={{0,8},{4,12},{8,0},{12,4},{16,24},{20,28},{24,16},{28,20},{1,9},{5... | collective-permute-start | bytes 393224 | tf_op jit(solution)/shard_map/ppermute | solution.py:42
  21.7 13.2 %collective-permute-start.6 = (bf16[4,64,256]{2,1,0:T(8,128)(2,1)S(1)}, bf16[4,64,256]{2,1,0:T(8,128)(2,1)S(1)}, u32[]{:S(2)}, u32[]{:S(2)}) collective-permute-start(bf16[4,64,256]{2,1,0:T(8,128)(2,1)S(1)} %get-tuple-element.43), channel_id=1, source_target_pairs={{0,8},{4,12},{8,0},{12,4},{16,24},{20,28},{24,16},{28,20},{1,9},{5... | collective-permute-start | bytes 393224 | tf_op jit(solution)/shard_map/ppermute | solution.py:42
  23.7 11.1 %collective-permute-start.7 = (bf16[4,64,256]{2,1,0:T(8,128)(2,1)S(1)}, bf16[4,64,256]{2,1,0:T(8,128)(2,1)S(1)}, u32[]{:S(2)}, u32[]{:S(2)}) collective-permute-start(bf16[4,64,256]{2,1,0:T(8,128)(2,1)S(1)} %get-tuple-element.44), channel_id=1, source_target_pairs={{0,16},{4,20},{8,24},{12,28},{16,0},{20,4},{24,8},{28,12},{1,17},{... | collective-permute-start | bytes 393224 | tf_op jit(solution)/shard_map/ppermute | solution.py:42
  26.5 8.3 %collective-permute-start.8 = (bf16[4,64,256]{2,1,0:T(8,128)(2,1)S(1)}, bf16[4,64,256]{2,1,0:T(8,128)(2,1)S(1)}, u32[]{:S(2)}, u32[]{:S(2)}) collective-permute-start(bf16[4,64,256]{2,1,0:T(8,128)(2,1)S(1)} %get-tuple-element.45), channel_id=1, source_target_pairs={{0,24},{4,28},{8,16},{12,20},{16,8},{20,12},{24,0},{28,4},{1,25},{... | collective-permute-start | bytes 393224 | tf_op jit(solution)/shard_map/ppermute | solution.py:42
  31.3 5.0 %collective-permute-start.12 = (bf16[4,64,256]{2,1,0:T(8,128)(2,1)S(1)}, bf16[4,64,256]{2,1,0:T(8,128)(2,1)S(1)}, u32[]{:S(2)}, u32[]{:S(2)}) collective-permute-start(bf16[4,64,256]{2,1,0:T(8,128)(2,1)S(1)} %get-tuple-element.49), channel_id=1, source_target_pairs={{0,8},{4,12},{8,0},{12,4},{16,24},{20,28},{24,16},{28,20},{1,9},{5... | collective-permute-start | bytes 393224 | tf_op jit(solution)/shard_map/ppermute | solution.py:42
  32.9 5.9 %collective-permute-start.13 = (bf16[4,64,256]{2,1,0:T(8,128)(2,1)S(1)}, bf16[4,64,256]{2,1,0:T(8,128)(2,1)S(1)}, u32[]{:S(2)}, u32[]{:S(2)}) collective-permute-start(bf16[4,64,256]{2,1,0:T(8,128)(2,1)S(1)} %get-tuple-element.50), channel_id=1, source_target_pairs={{0,16},{4,20},{8,24},{12,28},{16,0},{20,4},{24,8},{28,12},{1,17},{... | collective-permute-start | bytes 393224 | tf_op jit(solution)/shard_map/ppermute | solution.py:42
  34.8 5.9 %collective-permute-start.14 = (bf16[4,64,256]{2,1,0:T(8,128)(2,1)S(1)}, bf16[4,64,256]{2,1,0:T(8,128)(2,1)S(1)}, u32[]{:S(2)}, u32[]{:S(2)}) collective-permute-start(bf16[4,64,256]{2,1,0:T(8,128)(2,1)S(1)} %get-tuple-element.51), channel_id=1, source_target_pairs={{0,24},{4,28},{8,16},{12,20},{16,8},{20,12},{24,0},{28,4},{1,25},{... | collective-permute-start | bytes 393224 | tf_op jit(solution)/shard_map/ppermute | solution.py:42
  40.8 12.1 %collective-permute-start.15 = (bf16[8,16,256]{2,1,0:T(8,128)(2,1)S(1)}, bf16[8,16,256]{2,1,0:T(8,128)(2,1)S(1)}, u32[]{:S(2)}, u32[]{:S(2)}) collective-permute-start(bf16[8,16,256]{2,1,0:T(8,128)(2,1)S(1)} %get-tuple-element.52), channel_id=1, source_target_pairs={{0,1},{1,0},{2,3},{3,2},{4,5},{5,4},{6,7},{7,6},{8,9},{9,8},{10,11... | collective-permute-start | bytes 196616 | tf_op jit(solution)/shard_map/ppermute | solution.py:46
  42.3 7.5 %collective-permute-start.18 = (bf16[4,16,256]{2,1,0:T(8,128)(2,1)S(1)}, bf16[4,16,256]{2,1,0:T(8,128)(2,1)S(1)}, u32[]{:S(2)}, u32[]{:S(2)}) collective-permute-start(bf16[4,16,256]{2,1,0:T(8,128)(2,1)S(1)} %get-tuple-element.57), channel_id=1, source_target_pairs={{0,2},{1,3},{2,0},{3,1},{4,6},{5,7},{6,4},{7,5},{8,10},{9,11},{10,... | collective-permute-start | bytes 98312 | tf_op jit(solution)/shard_map/ppermute | solution.py:46
  44.9 6.2 %collective-permute-start.19 = (bf16[4,16,256]{2,1,0:T(8,128)(2,1)S(1)}, bf16[4,16,256]{2,1,0:T(8,128)(2,1)S(1)}, u32[]{:S(2)}, u32[]{:S(2)}) collective-permute-start(bf16[4,16,256]{2,1,0:T(8,128)(2,1)S(1)} %get-tuple-element.58), channel_id=1, source_target_pairs={{0,3},{1,2},{2,1},{3,0},{4,7},{5,6},{6,5},{7,4},{8,11},{9,10},{10,... | collective-permute-start | bytes 98312 | tf_op jit(solution)/shard_map/ppermute | solution.py:46
  45.2 6.6 %collective-permute-start.16 = (bf16[4,16,256]{2,1,0:T(8,128)(2,1)S(1)}, bf16[4,16,256]{2,1,0:T(8,128)(2,1)S(1)}, u32[]{:S(2)}, u32[]{:S(2)}) collective-permute-start(bf16[4,16,256]{2,1,0:T(8,128)(2,1)S(1)} %get-tuple-element.54), channel_id=1, source_target_pairs={{0,2},{1,3},{2,0},{3,1},{4,6},{5,7},{6,4},{7,5},{8,10},{9,11},{10,... | collective-permute-start | bytes 98312 | tf_op jit(solution)/shard_map/ppermute | solution.py:46
  46.9 6.1 %collective-permute-start.17 = (bf16[4,16,256]{2,1,0:T(8,128)(2,1)S(1)}, bf16[4,16,256]{2,1,0:T(8,128)(2,1)S(1)}, u32[]{:S(2)}, u32[]{:S(2)}) collective-permute-start(bf16[4,16,256]{2,1,0:T(8,128)(2,1)S(1)} %get-tuple-element.55), channel_id=1, source_target_pairs={{0,3},{1,2},{2,1},{3,0},{4,7},{5,6},{6,5},{7,4},{8,11},{9,10},{10,... | collective-permute-start | bytes 98312 | tf_op jit(solution)/shard_map/ppermute | solution.py:46
  49.6 3.3 %copy-start.3 = (bf16[256,256]{1,0:T(8,128)(2,1)S(1)}, bf16[256,256]{1,0:T(8,128)(2,1)}, u32[]{:S(2)}) copy-start(bf16[256,256]{1,0:T(8,128)(2,1)} %constant.32.clone.refs_9_) | copy-start | bytes 393220
  49.6 3.3 %copy-start.4 = (bf16[256,256]{1,0:T(8,128)(2,1)S(1)}, bf16[256,256]{1,0:T(8,128)(2,1)}, u32[]{:S(2)}) copy-start(bf16[256,256]{1,0:T(8,128)(2,1)} %constant.33.clone.refs_10_) | copy-start | bytes 393220
  49.6 3.3 %copy-start.5 = (bf16[256,256]{1,0:T(8,128)(2,1)S(1)}, bf16[256,256]{1,0:T(8,128)(2,1)}, u32[]{:S(2)}) copy-start(bf16[256,256]{1,0:T(8,128)(2,1)} %constant.34.clone.refs_11_) | copy-start | bytes 393220
  49.7 3.3 %copy-start.6 = (bf16[256,256]{1,0:T(8,128)(2,1)S(1)}, bf16[256,256]{1,0:T(8,128)(2,1)}, u32[]{:S(2)}) copy-start(bf16[256,256]{1,0:T(8,128)(2,1)} %constant.35.clone.refs_12_) | copy-start | bytes 393220
  49.7 3.3 %copy-start.8 = (f32[4,256]{1,0:T(4,128)S(1)}, f32[4,256]{1,0:T(4,128)}, u32[]{:S(2)}) copy-start(f32[4,256]{1,0:T(4,128)} %constant.37.clone.refs_14_) | copy-start | bytes 12292
  54.7 4.5 %collective-permute-start.21 = (bf16[8,16,256]{2,1,0:T(8,128)(2,1)S(1)}, bf16[8,16,256]{2,1,0:T(8,128)(2,1)S(1)}, u32[]{:S(2)}, u32[]{:S(2)}) collective-permute-start(bf16[8,16,256]{2,1,0:T(8,128)(2,1)S(1)} %get-tuple-element.60), channel_id=1, source_target_pairs={{0,1},{1,0},{2,3},{3,2},{4,5},{5,4},{6,7},{7,6},{8,9},{9,8},{10,11... | collective-permute-start | bytes 196616 | tf_op jit(solution)/shard_map/ppermute | solution.py:46
  56.2 5.9 %collective-permute-start.22 = (bf16[8,16,256]{2,1,0:T(8,128)(2,1)S(1)}, bf16[8,16,256]{2,1,0:T(8,128)(2,1)S(1)}, u32[]{:S(2)}, u32[]{:S(2)}) collective-permute-start(bf16[8,16,256]{2,1,0:T(8,128)(2,1)S(1)} %get-tuple-element.61), channel_id=1, source_target_pairs={{0,2},{1,3},{2,0},{3,1},{4,6},{5,7},{6,4},{7,5},{8,10},{9,11},{10,... | collective-permute-start | bytes 196616 | tf_op jit(solution)/shard_map/ppermute | solution.py:46
  57.6 6.1 %collective-permute-start.23 = (bf16[8,16,256]{2,1,0:T(8,128)(2,1)S(1)}, bf16[8,16,256]{2,1,0:T(8,128)(2,1)S(1)}, u32[]{:S(2)}, u32[]{:S(2)}) collective-permute-start(bf16[8,16,256]{2,1,0:T(8,128)(2,1)S(1)} %get-tuple-element.62), channel_id=1, source_target_pairs={{0,3},{1,2},{2,1},{3,0},{4,7},{5,6},{6,5},{7,4},{8,11},{9,10},{10,... | collective-permute-start | bytes 196616 | tf_op jit(solution)/shard_map/ppermute | solution.py:46
  63.7 1.4 %collective-permute-start.24 = (bf16[8,32,256]{2,1,0:T(8,128)(2,1)S(1)}, bf16[8,32,256]{2,1,0:T(8,128)(2,1)S(1)}, u32[]{:S(2)}, u32[]{:S(2)}) collective-permute-start(bf16[8,32,256]{2,1,0:T(8,128)(2,1)S(1)} %get-tuple-element.64), channel_id=1, source_target_pairs={{0,4},{4,0},{8,12},{12,8},{16,20},{20,16},{24,28},{28,24},{1,5},{5... | collective-permute-start | bytes 393224 | tf_op jit(solution)/shard_map/ppermute | solution.py:42
  (3 other events, 5.4 us)

commit v4 on v3

--- a/solution.py
+++ b/solution.py
@@ -38,8 +38,19 @@
     return run
 
 
+def turned_mask(mask, core):
+    if isinstance(core, int):
+        return {1: 2, 2: 1}.get(mask, mask) if core else mask
+    return mask ^ 3 * core if mask in (1, 2) else mask
+
+
 def swap_pix(value, mask, size):
     return lax.ppermute(value, "pix", [(i, i ^ mask) for i in range(size)])
+
+
+def swap_chip(value, mask, size):
+    pairs = [(i, i ^ 2 * turned_mask(mask, i % 2)) for i in range(size)]
+    return lax.ppermute(value, "pix", pairs)
 
 
 def swap_tm(value, mask, size):
@@ -72,12 +83,14 @@
 
 
 def turn_kernel(rows, chips, profiles, turned):
-    chip = lax.axis_index("pix") // 2
+    chip, core = lax.axis_index("pix") // 2, lax.axis_index("pix") % 2
     step = 256
     for i in range(profiles.shape[0] // step):
         block = profiles[i * step : (i + 1) * step, :].T
         for j in range(chips):
-            place = pl.multiple_of((chip ^ j) * rows, rows)
+            mask = chip ^ j
+            mask = jnp.where((mask == 1) | (mask == 2), mask ^ 3 * core, mask)
+            place = pl.multiple_of(mask * rows, rows)
             turned[pl.ds(place, rows), i * step : (i + 1) * step] = block[j * rows : (j + 1) * rows]
 
 
@@ -86,13 +99,13 @@
     blocks = refs[4 : 4 + chips]
     outs = refs[4 + chips : 4 + 2 * chips]
     gathered, cubed = refs[4 + 2 * chips :]
-    chip = lax.axis_index("pix") // 2
+    chip, core = lax.axis_index("pix") // 2, lax.axis_index("pix") % 2
     rows, time = blocks[0].shape[1:]
     pixels = profiles[0].shape[0]
 
     def one(b, carry):
         for j in range(chips):
-            place = pl.multiple_of((chip ^ j) * rows, rows)
+            place = pl.multiple_of((chip ^ turned_mask(j, core)) * rows, rows)
             for c in range(2):
                 gathered[pl.ds(place, rows), c * time : (c + 1) * time] = blocks[j][c * nb + b]
         modal = gathered[...]
@@ -286,7 +299,7 @@
             modal_kernel, [((2 * nb, rows, time), F32), ((2 * nb, rows, time), BF16)]
         )(halves[2 * n], others[n])
         fulls.append(full)
-        gathers.append([modal] + [swap_pix(modal, 2 * j, pix) for j in range(1, chips)])
+        gathers.append([modal] + [swap_chip(modal, j, pix) for j in range(1, chips)])
 
     turn = call(functools.partial(turn_kernel, rows, chips), [((chips * rows, pixels), BF16)])
     turned = []
@@ -308,7 +321,7 @@
             [((chips * rows, 2 * time), BF16), ((2 * pixels, 2 * time), BF16)],
             flops=16 * pixels * chips * rows * nb * time,
         )(profiles, profiles_other, *turned, *gathers[n])
-        sums = [parts[0]] + [swap_pix(parts[j], 2 * j, pix) for j in range(1, chips)]
+        sums = [parts[0]] + [swap_chip(parts[j], j, pix) for j in range(1, chips)]
         block = (2 * nb, cut, time)
         last = n == len(sizes) - 1
         joint = (2 * half, cut, time) if last else block

time: 66.3 us -> 61.5 us (0.928)
  waiting for transfers between devices: 18.9 us -> 15.1 us
  starting transfers between devices: 30.2 us -> 29.2 us
    ppermute x17 -> x5, starting transfers between devices: 17.7 us -> 1.21 us  [swap_pix(): return lax.ppermute(value, 'pix', [(i, i ^ mask) for i in range(size)])]
    ppermute x0 -> x12, starting transfers between devices: none -> 15.5 us  [swap_chip(): return lax.ppermute(value, 'pix', pairs)]
    ppermute x17 -> x5, waiting for transfers between devices: 11.4 us -> 2.2 us  [swap_pix(): return lax.ppermute(value, 'pix', [(i, i ^ mask) for i in range(size)])]
    ppermute x0 -> x12, waiting for transfers between devices: none -> 6.01 us  [swap_chip(): return lax.ppermute(value, 'pix', pairs)]
  transfers between devices with their start and end apart: 25 -> 25, of which waited for: 11 -> 10; matrix products, arithmetic and copies ran while one was open for 2% -> 2% of each run, Pallas kernels for 16% -> 17%
where the time goes in v4:
time: 61.5 us; the launch traced here: 61.3 us
  starting transfers between devices  29.2 us (47%)
  waiting for transfers between devices  15.1 us (25%)
  Pallas kernels  13.5 us (22%)
  local copies, waits for them, and re-layouts  3.08 us (5%)
    ppermute x12, starting transfers between devices, swap_chip(): return lax.ppermute(value, 'pix', pairs)  15.5 us
    pallas_call x12, Pallas kernels, run(): pl.pallas_call(kernel, out_shape=tuple((jax.ShapeDtypeStruct(*out) for ou...  13.5 us
    ppermute x8, starting transfers between devices, swap_tm(): return lax.ppermute(value, 'tm', [(i, i ^ mask) for i in range(size)])  12.5 us
    ppermute x8, waiting for transfers between devices, swap_tm(): return lax.ppermute(value, 'tm', [(i, i ^ mask) for i in range(size)])  6.86 us
    ppermute x12, waiting for transfers between devices, swap_chip(): return lax.ppermute(value, 'pix', pairs)  6.01 us
    unnamed x20, local copies, waits for them, and re-layouts  2.31 us
    ppermute x5, waiting for transfers between devices, swap_pix(): return lax.ppermute(value, 'pix', [(i, i ^ mask) for i in range(size)])  2.2 us
  transfers between devices with their start and end apart: 25, of which 10 were waited for; matrix products, arithmetic and copies ran while one was open for 2% of the time, Pallas kernels for 17%

profile of v4, /device:TPU:0, one launch (start us, length us, event | category | flops | bytes accessed | tf_op | source)
XLA Modules:
  0.0 61.3 jit_solution(18109670323991987903)
XLA Ops:
  0.0 0.5 collective-permute-start.2
  0.5 1.0 %copy-done.2 = f32[32,8,2,256]{3,2,1,0:T(2,128)S(1)} copy-done((f32[32,8,2,256]{3,2,1,0:T(2,128)S(1)}, f32[32,8,2,256]{3,2,1,0:T(2,128)}, u32[]{:S(2)}) %copy-start.2) | copy-done | bytes 524312
  1.8 0.5 collective-permute-start
  2.3 0.9 %collective-permute-done.1.other = f32[4,32,256]{2,1,0:T(8,128)S(1)} collective-permute-done((f32[4,32,256]{2,1,0:T(8,128)S(1)}, f32[4,32,256]{2,1,0:T(8,128)S(1)}, u32[]{:S(2)}, u32[]{:S(2)}) %collective-permute-start.1) | collective-permute-done | bytes 131104 | tf_op jit(solution)/shard_map/ppermute | solution.py:48
  3.2 2.9 %collective-permute-start.3 = (bf16[4,64,256]{2,1,0:T(8,128)(2,1)S(1)}, bf16[4,64,256]{2,1,0:T(8,128)(2,1)S(1)}, u32[]{:S(2)}, u32[]{:S(2)}) collective-permute-start(bf16[4,64,256]{2,1,0:T(8,128)(2,1)S(1)} %get-tuple-element.41.refs_4_), channel_id=1, source_target_pairs={{0,8},{4,20},{8,0},{12,28},{16,24},{20,4},{24,16},{28,12},{1,9},{5... | collective-permute-start | bytes 393224 | tf_op jit(solution)/shard_map/ppermute | solution.py:53
  6.1 1.5 %collective-permute-start.4 = (bf16[4,64,256]{2,1,0:T(8,128)(2,1)S(1)}, bf16[4,64,256]{2,1,0:T(8,128)(2,1)S(1)}, u32[]{:S(2)}, u32[]{:S(2)}) collective-permute-start(bf16[4,64,256]{2,1,0:T(8,128)(2,1)S(1)} %get-tuple-element.41.refs_4_), channel_id=1, source_target_pairs={{0,16},{4,12},{8,24},{12,4},{16,0},{20,28},{24,8},{28,20},{1,17},{... | collective-permute-start | bytes 393224 | tf_op jit(solution)/shard_map/ppermute | solution.py:53
  7.7 1.2 %copy-done = bf16[2048,256]{1,0:T(8,128)(2,1)S(1)} copy-done((bf16[2048,256]{1,0:T(8,128)(2,1)S(1)}, bf16[2048,256]{1,0:T(8,128)(2,1)}, u32[]{:S(2)}) %copy-start) | copy-done | bytes 1048600
  9.4 2.0 %collective-permute-start.10 = (bf16[4,64,256]{2,1,0:T(8,128)(2,1)S(1)}, bf16[4,64,256]{2,1,0:T(8,128)(2,1)S(1)}, u32[]{:S(2)}, u32[]{:S(2)}) collective-permute-start(bf16[4,64,256]{2,1,0:T(8,128)(2,1)S(1)} %get-tuple-element.47.refs_4_), channel_id=1, source_target_pairs={{0,16},{4,12},{8,24},{12,4},{16,0},{20,28},{24,8},{28,20},{1,17},{... | collective-permute-start | bytes 393224 | tf_op jit(solution)/shard_map/ppermute | solution.py:53
  11.8 1.6 %collective-permute-start.11 = (bf16[4,64,256]{2,1,0:T(8,128)(2,1)S(1)}, bf16[4,64,256]{2,1,0:T(8,128)(2,1)S(1)}, u32[]{:S(2)}, u32[]{:S(2)}) collective-permute-start(bf16[4,64,256]{2,1,0:T(8,128)(2,1)S(1)} %get-tuple-element.47.refs_4_), channel_id=1, source_target_pairs={{0,24},{4,28},{8,16},{12,20},{16,8},{20,12},{24,0},{28,4},{1,25},{... | collective-permute-start | bytes 393224 | tf_op jit(solution)/shard_map/ppermute | solution.py:53
  14.1 4.7 %shard_map.96 = (f32[4,64,256]{2,1,0:T(8,128)S(1)}, bf16[4,64,256]{2,1,0:T(8,128)(2,1)S(1)}, bf16[4,64,256]{2,1,0:T(8,128)(2,1)S(1)}, bf16[4,64,256]{2,1,0:T(8,128)(2,1)S(1)}) custom-call(bf16[2048,256]{1,0:T(8,128)(2,1)S(1)} %copy-done.1, bf16[2048,256]{1,0:T(8,128)(2,1)S(1)} %collective-permute-done.2.profiles.refs_1_, ...), custom_call_target="tpu_custom_call" | custom-call | flops 4294967296 | bytes 5373952 | tf_op jit(solution)/shard_map/pallas_call | solution.py:28
  18.9 1.8 %collective-permute-start.6 = (bf16[4,64,256]{2,1,0:T(8,128)(2,1)S(1)}, bf16[4,64,256]{2,1,0:T(8,128)(2,1)S(1)}, u32[]{:S(2)}, u32[]{:S(2)}) collective-permute-start(bf16[4,64,256]{2,1,0:T(8,128)(2,1)S(1)} %get-tuple-element.43), channel_id=1, source_target_pairs={{0,8},{4,20},{8,0},{12,28},{16,24},{20,4},{24,16},{28,12},{1,9},{5... | collective-permute-start | bytes 393224 | tf_op jit(solution)/shard_map/ppermute | solution.py:53
  20.7 1.6 %collective-permute-start.7 = (bf16[4,64,256]{2,1,0:T(8,128)(2,1)S(1)}, bf16[4,64,256]{2,1,0:T(8,128)(2,1)S(1)}, u32[]{:S(2)}, u32[]{:S(2)}) collective-permute-start(bf16[4,64,256]{2,1,0:T(8,128)(2,1)S(1)} %get-tuple-element.44), channel_id=1, source_target_pairs={{0,16},{4,12},{8,24},{12,4},{16,0},{20,28},{24,8},{28,20},{1,17},{... | collective-permute-start | bytes 393224 | tf_op jit(solution)/shard_map/ppermute | solution.py:53
  22.4 4.7 %shard_map.98 = (f32[4,64,256]{2,1,0:T(8,128)S(1)}, bf16[4,64,256]{2,1,0:T(8,128)(2,1)S(1)}, bf16[4,64,256]{2,1,0:T(8,128)(2,1)S(1)}, bf16[4,64,256]{2,1,0:T(8,128)(2,1)S(1)}) custom-call(bf16[2048,256]{1,0:T(8,128)(2,1)S(1)} %copy-done.1, bf16[2048,256]{1,0:T(8,128)(2,1)S(1)} %collective-permute-done.2.profiles.refs_1_, ...), custom_call_target="tpu_custom_call" | custom-call | flops 4294967296 | bytes 5373952 | tf_op jit(solution)/shard_map/pallas_call | solution.py:28
  27.2 1.8 %collective-permute-start.12 = (bf16[4,64,256]{2,1,0:T(8,128)(2,1)S(1)}, bf16[4,64,256]{2,1,0:T(8,128)(2,1)S(1)}, u32[]{:S(2)}, u32[]{:S(2)}) collective-permute-start(bf16[4,64,256]{2,1,0:T(8,128)(2,1)S(1)} %get-tuple-element.49), channel_id=1, source_target_pairs={{0,8},{4,20},{8,0},{12,28},{16,24},{20,4},{24,16},{28,12},{1,9},{5... | collective-permute-start | bytes 393224 | tf_op jit(solution)/shard_map/ppermute | solution.py:53
  29.0 1.6 %collective-permute-start.13 = (bf16[4,64,256]{2,1,0:T(8,128)(2,1)S(1)}, bf16[4,64,256]{2,1,0:T(8,128)(2,1)S(1)}, u32[]{:S(2)}, u32[]{:S(2)}) collective-permute-start(bf16[4,64,256]{2,1,0:T(8,128)(2,1)S(1)} %get-tuple-element.50), channel_id=1, source_target_pairs={{0,16},{4,12},{8,24},{12,4},{16,0},{20,28},{24,8},{28,20},{1,17},{... | collective-permute-start | bytes 393224 | tf_op jit(solution)/shard_map/ppermute | solution.py:53
  30.9 2.7 %collective-permute-done.12.refs_2_ = bf16[4,64,256]{2,1,0:T(8,128)(2,1)S(1)} collective-permute-done((bf16[4,64,256]{2,1,0:T(8,128)(2,1)S(1)}, bf16[4,64,256]{2,1,0:T(8,128)(2,1)S(1)}, u32[]{:S(2)}, u32[]{:S(2)}) %collective-permute-start.12) | collective-permute-done | bytes 131104 | tf_op jit(solution)/shard_map/ppermute | solution.py:53
  33.6 1.6 %collective-permute-done.13.refs_3_ = bf16[4,64,256]{2,1,0:T(8,128)(2,1)S(1)} collective-permute-done((bf16[4,64,256]{2,1,0:T(8,128)(2,1)S(1)}, bf16[4,64,256]{2,1,0:T(8,128)(2,1)S(1)}, u32[]{:S(2)}, u32[]{:S(2)}) %collective-permute-start.13) | collective-permute-done | bytes 131104 | tf_op jit(solution)/shard_map/ppermute | solution.py:53
  35.2 1.3 %collective-permute-done.14.refs_4_ = bf16[4,64,256]{2,1,0:T(8,128)(2,1)S(1)} collective-permute-done((bf16[4,64,256]{2,1,0:T(8,128)(2,1)S(1)}, bf16[4,64,256]{2,1,0:T(8,128)(2,1)S(1)}, u32[]{:S(2)}, u32[]{:S(2)}) %collective-permute-start.14) | collective-permute-done | bytes 131104 | tf_op jit(solution)/shard_map/ppermute | solution.py:53
  36.6 1.6 %collective-permute-start.15 = (bf16[8,16,256]{2,1,0:T(8,128)(2,1)S(1)}, bf16[8,16,256]{2,1,0:T(8,128)(2,1)S(1)}, u32[]{:S(2)}, u32[]{:S(2)}) collective-permute-start(bf16[8,16,256]{2,1,0:T(8,128)(2,1)S(1)} %get-tuple-element.52), channel_id=1, source_target_pairs={{0,1},{1,0},{2,3},{3,2},{4,5},{5,4},{6,7},{7,6},{8,9},{9,8},{10,11... | collective-permute-start | bytes 196616 | tf_op jit(solution)/shard_map/ppermute | solution.py:57
  38.2 2.6 %collective-permute-start.18 = (bf16[4,16,256]{2,1,0:T(8,128)(2,1)S(1)}, bf16[4,16,256]{2,1,0:T(8,128)(2,1)S(1)}, u32[]{:S(2)}, u32[]{:S(2)}) collective-permute-start(bf16[4,16,256]{2,1,0:T(8,128)(2,1)S(1)} %get-tuple-element.57), channel_id=1, source_target_pairs={{0,2},{1,3},{2,0},{3,1},{4,6},{5,7},{6,4},{7,5},{8,10},{9,11},{10,... | collective-permute-start | bytes 98312 | tf_op jit(solution)/shard_map/ppermute | solution.py:57
  41.0 1.6 %collective-permute-start.16 = (bf16[4,16,256]{2,1,0:T(8,128)(2,1)S(1)}, bf16[4,16,256]{2,1,0:T(8,128)(2,1)S(1)}, u32[]{:S(2)}, u32[]{:S(2)}) collective-permute-start(bf16[4,16,256]{2,1,0:T(8,128)(2,1)S(1)} %get-tuple-element.54), channel_id=1, source_target_pairs={{0,2},{1,3},{2,0},{3,1},{4,6},{5,7},{6,4},{7,5},{8,10},{9,11},{10,... | collective-permute-start | bytes 98312 | tf_op jit(solution)/shard_map/ppermute | solution.py:57
  42.7 1.9 %collective-permute-start.17 = (bf16[4,16,256]{2,1,0:T(8,128)(2,1)S(1)}, bf16[4,16,256]{2,1,0:T(8,128)(2,1)S(1)}, u32[]{:S(2)}, u32[]{:S(2)}) collective-permute-start(bf16[4,16,256]{2,1,0:T(8,128)(2,1)S(1)} %get-tuple-element.55), channel_id=1, source_target_pairs={{0,3},{1,2},{2,1},{3,0},{4,7},{5,6},{6,5},{7,4},{8,11},{9,10},{10,... | collective-permute-start | bytes 98312 | tf_op jit(solution)/shard_map/ppermute | solution.py:57
  45.7 0.8 %collective-permute-done.19.refs_6_ = bf16[4,16,256]{2,1,0:T(8,128)(2,1)S(1)} collective-permute-done((bf16[4,16,256]{2,1,0:T(8,128)(2,1)S(1)}, bf16[4,16,256]{2,1,0:T(8,128)(2,1)S(1)}, u32[]{:S(2)}, u32[]{:S(2)}) %collective-permute-start.19) | collective-permute-done | bytes 32800 | tf_op jit(solution)/shard_map/ppermute | solution.py:57
  46.5 1.9 %collective-permute-done.17.refs_3_ = bf16[4,16,256]{2,1,0:T(8,128)(2,1)S(1)} collective-permute-done((bf16[4,16,256]{2,1,0:T(8,128)(2,1)S(1)}, bf16[4,16,256]{2,1,0:T(8,128)(2,1)S(1)}, u32[]{:S(2)}, u32[]{:S(2)}) %collective-permute-start.17) | collective-permute-done | bytes 32800 | tf_op jit(solution)/shard_map/ppermute | solution.py:57
  48.5 1.8 %shard_map.100 = (f32[8,16,256]{2,1,0:T(8,128)S(1)}, bf16[8,16,256]{2,1,0:T(8,128)(2,1)S(1)}, bf16[8,16,256]{2,1,0:T(8,128)(2,1)S(1)}, bf16[8,16,256]{2,1,0:T(8,128)(2,1)S(1)}) custom-call(bf16[8,16,256]{2,1,0:T(8,128)(2,1)S(1)} %collective-permute-done.15.refs_0_, f32[4,16,256]{2,1,0:T(8,128)S(1)} %get-tuple-element.53.refs_1_, ...), custom_call_target="tpu_custom_call" | custom-call | flops 1000000000 | bytes 1318912 | tf_op jit(solution)/shard_map/pallas_call | solution.py:28
  50.2 1.0 %collective-permute-start.21 = (bf16[8,16,256]{2,1,0:T(8,128)(2,1)S(1)}, bf16[8,16,256]{2,1,0:T(8,128)(2,1)S(1)}, u32[]{:S(2)}, u32[]{:S(2)}) collective-permute-start(bf16[8,16,256]{2,1,0:T(8,128)(2,1)S(1)} %get-tuple-element.60), channel_id=1, source_target_pairs={{0,1},{1,0},{2,3},{3,2},{4,5},{5,4},{6,7},{7,6},{8,9},{9,8},{10,11... | collective-permute-start | bytes 196616 | tf_op jit(solution)/shard_map/ppermute | solution.py:57
  51.2 1.6 %collective-permute-start.22 = (bf16[8,16,256]{2,1,0:T(8,128)(2,1)S(1)}, bf16[8,16,256]{2,1,0:T(8,128)(2,1)S(1)}, u32[]{:S(2)}, u32[]{:S(2)}) collective-permute-start(bf16[8,16,256]{2,1,0:T(8,128)(2,1)S(1)} %get-tuple-element.61), channel_id=1, source_target_pairs={{0,2},{1,3},{2,0},{3,1},{4,6},{5,7},{6,4},{7,5},{8,10},{9,11},{10,... | collective-permute-start | bytes 196616 | tf_op jit(solution)/shard_map/ppermute | solution.py:57
  52.7 1.9 %collective-permute-start.23 = (bf16[8,16,256]{2,1,0:T(8,128)(2,1)S(1)}, bf16[8,16,256]{2,1,0:T(8,128)(2,1)S(1)}, u32[]{:S(2)}, u32[]{:S(2)}) collective-permute-start(bf16[8,16,256]{2,1,0:T(8,128)(2,1)S(1)} %get-tuple-element.62), channel_id=1, source_target_pairs={{0,3},{1,2},{2,1},{3,0},{4,7},{5,6},{6,5},{7,4},{8,11},{9,10},{10,... | collective-permute-start | bytes 196616 | tf_op jit(solution)/shard_map/ppermute | solution.py:57
  54.7 2.4 %collective-permute-done.22.refs_2_ = bf16[8,16,256]{2,1,0:T(8,128)(2,1)S(1)} collective-permute-done((bf16[8,16,256]{2,1,0:T(8,128)(2,1)S(1)}, bf16[8,16,256]{2,1,0:T(8,128)(2,1)S(1)}, u32[]{:S(2)}, u32[]{:S(2)}) %collective-permute-start.22) | collective-permute-done | bytes 65568 | tf_op jit(solution)/shard_map/ppermute | solution.py:57
  57.0 1.8 %collective-permute-done.23.refs_3_ = bf16[8,16,256]{2,1,0:T(8,128)(2,1)S(1)} collective-permute-done((bf16[8,16,256]{2,1,0:T(8,128)(2,1)S(1)}, bf16[8,16,256]{2,1,0:T(8,128)(2,1)S(1)}, u32[]{:S(2)}, u32[]{:S(2)}) %collective-permute-start.23) | collective-permute-done | bytes 65568 | tf_op jit(solution)/shard_map/ppermute | solution.py:57
  59.0 1.3 %collective-permute-done.24.other = bf16[8,32,256]{2,1,0:T(8,128)(2,1)S(1)} collective-permute-done((bf16[8,32,256]{2,1,0:T(8,128)(2,1)S(1)}, bf16[8,32,256]{2,1,0:T(8,128)(2,1)S(1)}, u32[]{:S(2)}, u32[]{:S(2)}) %collective-permute-start.24) | collective-permute-done | bytes 131104 | tf_op jit(solution)/shard_map/ppermute | solution.py:48
  60.3 1.0 %shard_map.102 = f32[32,8,2,256]{3,2,1,0:T(2,128)} custom-call(f32[8,32,256]{2,1,0:T(8,128)S(1)} %get-tuple-element.63.own, bf16[8,32,256]{2,1,0:T(8,128)(2,1)S(1)} %collective-permute-done.24.other), custom_call_target="tpu_custom_call" | custom-call | bytes 917504 | tf_op jit(solution)/shard_map/pallas_call | solution.py:28
  (56 shorter events, 3.8 us)
Async XLA Ops:
  0.0 9.4 %collective-permute-start.2 = (bf16[2048,256]{1,0:T(8,128)(2,1)}, bf16[2048,256]{1,0:T(8,128)(2,1)S(1)}, u32[]{:S(2)}, u32[]{:S(2)}) collective-permute-start(bf16[2048,256]{1,0:T(8,128)(2,1)} %refs_0_.3), channel_id=1, source_target_pairs={{0,4},{4,0},{8,12},{12,8},{16,20},{20,16},{24,28},{28,24},{1,5},{5... | collective-permute-start | bytes 3145736 | tf_op jit(solution)/shard_map/ppermute | solution.py:48
  1.7 1.4 %collective-permute-start.1 = (f32[4,32,256]{2,1,0:T(8,128)S(1)}, f32[4,32,256]{2,1,0:T(8,128)S(1)}, u32[]{:S(2)}, u32[]{:S(2)}) collective-permute-start(f32[4,32,256]{2,1,0:T(8,128)S(1)} %get-tuple-element.39), channel_id=1, source_target_pairs={{0,4},{4,0},{8,12},{12,8},{16,20},{20,16},{24,28},{28,24},{1,5},{5... | collective-permute-start | bytes 393224 | tf_op jit(solution)/shard_map/ppermute | solution.py:48
  1.8 7.4 %collective-permute-start = (f32[4,32,256]{2,1,0:T(8,128)S(1)}, f32[4,32,256]{2,1,0:T(8,128)S(1)}, u32[]{:S(2)}, u32[]{:S(2)}) collective-permute-start(f32[4,32,256]{2,1,0:T(8,128)S(1)} %get-tuple-element.36), channel_id=1, source_target_pairs={{0,4},{4,0},{8,12},{12,8},{16,20},{20,16},{24,28},{28,24},{1,5},{5... | collective-permute-start | bytes 393224 | tf_op jit(solution)/shard_map/ppermute | solution.py:48
  3.2 6.1 %copy-start.9 = (f32[8,1024]{1,0:T(8,128)S(1)}, f32[8,1024]{1,0:T(8,128)}, u32[]{:S(2)}) copy-start(f32[8,1024]{1,0:T(8,128)} %param.11) | copy-start | bytes 98308
  3.2 8.6 %collective-permute-start.3 = (bf16[4,64,256]{2,1,0:T(8,128)(2,1)S(1)}, bf16[4,64,256]{2,1,0:T(8,128)(2,1)S(1)}, u32[]{:S(2)}, u32[]{:S(2)}) collective-permute-start(bf16[4,64,256]{2,1,0:T(8,128)(2,1)S(1)} %get-tuple-element.41.refs_4_), channel_id=1, source_target_pairs={{0,8},{4,20},{8,0},{12,28},{16,24},{20,4},{24,16},{28,12},{1,9},{5... | collective-permute-start | bytes 393224 | tf_op jit(solution)/shard_map/ppermute | solution.py:53
  6.1 7.3 %collective-permute-start.4 = (bf16[4,64,256]{2,1,0:T(8,128)(2,1)S(1)}, bf16[4,64,256]{2,1,0:T(8,128)(2,1)S(1)}, u32[]{:S(2)}, u32[]{:S(2)}) collective-permute-start(bf16[4,64,256]{2,1,0:T(8,128)(2,1)S(1)} %get-tuple-element.41.refs_4_), channel_id=1, source_target_pairs={{0,16},{4,12},{8,24},{12,4},{16,0},{20,28},{24,8},{28,20},{1,17},{... | collective-permute-start | bytes 393224 | tf_op jit(solution)/shard_map/ppermute | solution.py:53
  7.7 6.5 %collective-permute-start.5 = (bf16[4,64,256]{2,1,0:T(8,128)(2,1)S(1)}, bf16[4,64,256]{2,1,0:T(8,128)(2,1)S(1)}, u32[]{:S(2)}, u32[]{:S(2)}) collective-permute-start(bf16[4,64,256]{2,1,0:T(8,128)(2,1)S(1)} %get-tuple-element.41.refs_4_), channel_id=1, source_target_pairs={{0,24},{4,28},{8,16},{12,20},{16,8},{20,12},{24,0},{28,4},{1,25},{... | collective-permute-start | bytes 393224 | tf_op jit(solution)/shard_map/ppermute | solution.py:53
  9.3 19.7 %collective-permute-start.20 = (f32[8,1024]{1,0:T(8,128)S(1)}, f32[8,1024]{1,0:T(8,128)S(1)}, u32[]{:S(2)}, u32[]{:S(2)}) collective-permute-start(f32[8,1024]{1,0:T(8,128)S(1)} %copy-done.9), channel_id=1, source_target_pairs={{0,4},{4,0},{8,12},{12,8},{16,20},{20,16},{24,28},{28,24},{1,5},{5... | collective-permute-start | bytes 98312 | tf_op jit(solution)/shard_map/ppermute | solution.py:48
  9.4 4.7 %copy-start.1 = (bf16[2048,256]{1,0:T(8,128)(2,1)S(1)}, bf16[2048,256]{1,0:T(8,128)(2,1)}, u32[]{:S(2)}) copy-start(bf16[2048,256]{1,0:T(8,128)(2,1)} %refs_0_.3) | copy-start | bytes 3145732
  9.4 11.2 %collective-permute-start.10 = (bf16[4,64,256]{2,1,0:T(8,128)(2,1)S(1)}, bf16[4,64,256]{2,1,0:T(8,128)(2,1)S(1)}, u32[]{:S(2)}, u32[]{:S(2)}) collective-permute-start(bf16[4,64,256]{2,1,0:T(8,128)(2,1)S(1)} %get-tuple-element.47.refs_4_), channel_id=1, source_target_pairs={{0,16},{4,12},{8,24},{12,4},{16,0},{20,28},{24,8},{28,20},{1,17},{... | collective-permute-start | bytes 393224 | tf_op jit(solution)/shard_map/ppermute | solution.py:53
  11.8 10.5 %collective-permute-start.11 = (bf16[4,64,256]{2,1,0:T(8,128)(2,1)S(1)}, bf16[4,64,256]{2,1,0:T(8,128)(2,1)S(1)}, u32[]{:S(2)}, u32[]{:S(2)}) collective-permute-start(bf16[4,64,256]{2,1,0:T(8,128)(2,1)S(1)} %get-tuple-element.47.refs_4_), channel_id=1, source_target_pairs={{0,24},{4,28},{8,16},{12,20},{16,8},{20,12},{24,0},{28,4},{1,25},{... | collective-permute-start | bytes 393224 | tf_op jit(solution)/shard_map/ppermute | solution.py:53
  13.5 9.0 %collective-permute-start.9 = (bf16[4,64,256]{2,1,0:T(8,128)(2,1)S(1)}, bf16[4,64,256]{2,1,0:T(8,128)(2,1)S(1)}, u32[]{:S(2)}, u32[]{:S(2)}) collective-permute-start(bf16[4,64,256]{2,1,0:T(8,128)(2,1)S(1)} %get-tuple-element.47.refs_4_), channel_id=1, source_target_pairs={{0,8},{4,20},{8,0},{12,28},{16,24},{20,4},{24,16},{28,12},{1,9},{5... | collective-permute-start | bytes 393224 | tf_op jit(solution)/shard_map/ppermute | solution.py:53
  18.9 11.7 %collective-permute-start.6 = (bf16[4,64,256]{2,1,0:T(8,128)(2,1)S(1)}, bf16[4,64,256]{2,1,0:T(8,128)(2,1)S(1)}, u32[]{:S(2)}, u32[]{:S(2)}) collective-permute-start(bf16[4,64,256]{2,1,0:T(8,128)(2,1)S(1)} %get-tuple-element.43), channel_id=1, source_target_pairs={{0,8},{4,20},{8,0},{12,28},{16,24},{20,4},{24,16},{28,12},{1,9},{5... | collective-permute-start | bytes 393224 | tf_op jit(solution)/shard_map/ppermute | solution.py:53
  20.7 10.1 %collective-permute-start.7 = (bf16[4,64,256]{2,1,0:T(8,128)(2,1)S(1)}, bf16[4,64,256]{2,1,0:T(8,128)(2,1)S(1)}, u32[]{:S(2)}, u32[]{:S(2)}) collective-permute-start(bf16[4,64,256]{2,1,0:T(8,128)(2,1)S(1)} %get-tuple-element.44), channel_id=1, source_target_pairs={{0,16},{4,12},{8,24},{12,4},{16,0},{20,28},{24,8},{28,20},{1,17},{... | collective-permute-start | bytes 393224 | tf_op jit(solution)/shard_map/ppermute | solution.py:53
  22.3 8.5 %collective-permute-start.8 = (bf16[4,64,256]{2,1,0:T(8,128)(2,1)S(1)}, bf16[4,64,256]{2,1,0:T(8,128)(2,1)S(1)}, u32[]{:S(2)}, u32[]{:S(2)}) collective-permute-start(bf16[4,64,256]{2,1,0:T(8,128)(2,1)S(1)} %get-tuple-element.45), channel_id=1, source_target_pairs={{0,24},{4,28},{8,16},{12,20},{16,8},{20,12},{24,0},{28,4},{1,25},{... | collective-permute-start | bytes 393224 | tf_op jit(solution)/shard_map/ppermute | solution.py:53
  27.2 6.4 %collective-permute-start.12 = (bf16[4,64,256]{2,1,0:T(8,128)(2,1)S(1)}, bf16[4,64,256]{2,1,0:T(8,128)(2,1)S(1)}, u32[]{:S(2)}, u32[]{:S(2)}) collective-permute-start(bf16[4,64,256]{2,1,0:T(8,128)(2,1)S(1)} %get-tuple-element.49), channel_id=1, source_target_pairs={{0,8},{4,20},{8,0},{12,28},{16,24},{20,4},{24,16},{28,12},{1,9},{5... | collective-permute-start | bytes 393224 | tf_op jit(solution)/shard_map/ppermute | solution.py:53
  29.0 6.2 %collective-permute-start.13 = (bf16[4,64,256]{2,1,0:T(8,128)(2,1)S(1)}, bf16[4,64,256]{2,1,0:T(8,128)(2,1)S(1)}, u32[]{:S(2)}, u32[]{:S(2)}) collective-permute-start(bf16[4,64,256]{2,1,0:T(8,128)(2,1)S(1)} %get-tuple-element.50), channel_id=1, source_target_pairs={{0,16},{4,12},{8,24},{12,4},{16,0},{20,28},{24,8},{28,20},{1,17},{... | collective-permute-start | bytes 393224 | tf_op jit(solution)/shard_map/ppermute | solution.py:53
  30.6 5.9 %collective-permute-start.14 = (bf16[4,64,256]{2,1,0:T(8,128)(2,1)S(1)}, bf16[4,64,256]{2,1,0:T(8,128)(2,1)S(1)}, u32[]{:S(2)}, u32[]{:S(2)}) collective-permute-start(bf16[4,64,256]{2,1,0:T(8,128)(2,1)S(1)} %get-tuple-element.51), channel_id=1, source_target_pairs={{0,24},{4,28},{8,16},{12,20},{16,8},{20,12},{24,0},{28,4},{1,25},{... | collective-permute-start | bytes 393224 | tf_op jit(solution)/shard_map/ppermute | solution.py:53
  36.6 11.8 %collective-permute-start.15 = (bf16[8,16,256]{2,1,0:T(8,128)(2,1)S(1)}, bf16[8,16,256]{2,1,0:T(8,128)(2,1)S(1)}, u32[]{:S(2)}, u32[]{:S(2)}) collective-permute-start(bf16[8,16,256]{2,1,0:T(8,128)(2,1)S(1)} %get-tuple-element.52), channel_id=1, source_target_pairs={{0,1},{1,0},{2,3},{3,2},{4,5},{5,4},{6,7},{7,6},{8,9},{9,8},{10,11... | collective-permute-start | bytes 196616 | tf_op jit(solution)/shard_map/ppermute | solution.py:57
  38.2 7.5 %collective-permute-start.18 = (bf16[4,16,256]{2,1,0:T(8,128)(2,1)S(1)}, bf16[4,16,256]{2,1,0:T(8,128)(2,1)S(1)}, u32[]{:S(2)}, u32[]{:S(2)}) collective-permute-start(bf16[4,16,256]{2,1,0:T(8,128)(2,1)S(1)} %get-tuple-element.57), channel_id=1, source_target_pairs={{0,2},{1,3},{2,0},{3,1},{4,6},{5,7},{6,4},{7,5},{8,10},{9,11},{10,... | collective-permute-start | bytes 98312 | tf_op jit(solution)/shard_map/ppermute | solution.py:57
  40.8 5.7 %collective-permute-start.19 = (bf16[4,16,256]{2,1,0:T(8,128)(2,1)S(1)}, bf16[4,16,256]{2,1,0:T(8,128)(2,1)S(1)}, u32[]{:S(2)}, u32[]{:S(2)}) collective-permute-start(bf16[4,16,256]{2,1,0:T(8,128)(2,1)S(1)} %get-tuple-element.58), channel_id=1, source_target_pairs={{0,3},{1,2},{2,1},{3,0},{4,7},{5,6},{6,5},{7,4},{8,11},{9,10},{10,... | collective-permute-start | bytes 98312 | tf_op jit(solution)/shard_map/ppermute | solution.py:57
  41.0 5.4 %collective-permute-start.16 = (bf16[4,16,256]{2,1,0:T(8,128)(2,1)S(1)}, bf16[4,16,256]{2,1,0:T(8,128)(2,1)S(1)}, u32[]{:S(2)}, u32[]{:S(2)}) collective-permute-start(bf16[4,16,256]{2,1,0:T(8,128)(2,1)S(1)} %get-tuple-element.54), channel_id=1, source_target_pairs={{0,2},{1,3},{2,0},{3,1},{4,6},{5,7},{6,4},{7,5},{8,10},{9,11},{10,... | collective-permute-start | bytes 98312 | tf_op jit(solution)/shard_map/ppermute | solution.py:57
  42.7 5.7 %collective-permute-start.17 = (bf16[4,16,256]{2,1,0:T(8,128)(2,1)S(1)}, bf16[4,16,256]{2,1,0:T(8,128)(2,1)S(1)}, u32[]{:S(2)}, u32[]{:S(2)}) collective-permute-start(bf16[4,16,256]{2,1,0:T(8,128)(2,1)S(1)} %get-tuple-element.55), channel_id=1, source_target_pairs={{0,3},{1,2},{2,1},{3,0},{4,7},{5,6},{6,5},{7,4},{8,11},{9,10},{10,... | collective-permute-start | bytes 98312 | tf_op jit(solution)/shard_map/ppermute | solution.py:57
  45.4 3.0 %copy-start.3 = (bf16[256,256]{1,0:T(8,128)(2,1)S(1)}, bf16[256,256]{1,0:T(8,128)(2,1)}, u32[]{:S(2)}) copy-start(bf16[256,256]{1,0:T(8,128)(2,1)} %constant.32.clone.refs_9_) | copy-start | bytes 393220
  45.4 3.0 %copy-start.4 = (bf16[256,256]{1,0:T(8,128)(2,1)S(1)}, bf16[256,256]{1,0:T(8,128)(2,1)}, u32[]{:S(2)}) copy-start(bf16[256,256]{1,0:T(8,128)(2,1)} %constant.33.clone.refs_10_) | copy-start | bytes 393220
  45.5 3.0 %copy-start.5 = (bf16[256,256]{1,0:T(8,128)(2,1)S(1)}, bf16[256,256]{1,0:T(8,128)(2,1)}, u32[]{:S(2)}) copy-start(bf16[256,256]{1,0:T(8,128)(2,1)} %constant.34.clone.refs_11_) | copy-start | bytes 393220
  45.5 3.0 %copy-start.6 = (bf16[256,256]{1,0:T(8,128)(2,1)S(1)}, bf16[256,256]{1,0:T(8,128)(2,1)}, u32[]{:S(2)}) copy-start(bf16[256,256]{1,0:T(8,128)(2,1)} %constant.35.clone.refs_12_) | copy-start | bytes 393220
  45.5 3.0 %copy-start.8 = (f32[4,256]{1,0:T(4,128)S(1)}, f32[4,256]{1,0:T(4,128)}, u32[]{:S(2)}) copy-start(f32[4,256]{1,0:T(4,128)} %constant.37.clone.refs_14_) | copy-start | bytes 12292
  50.2 4.5 %collective-permute-start.21 = (bf16[8,16,256]{2,1,0:T(8,128)(2,1)S(1)}, bf16[8,16,256]{2,1,0:T(8,128)(2,1)S(1)}, u32[]{:S(2)}, u32[]{:S(2)}) collective-permute-start(bf16[8,16,256]{2,1,0:T(8,128)(2,1)S(1)} %get-tuple-element.60), channel_id=1, source_target_pairs={{0,1},{1,0},{2,3},{3,2},{4,5},{5,4},{6,7},{7,6},{8,9},{9,8},{10,11... | collective-permute-start | bytes 196616 | tf_op jit(solution)/shard_map/ppermute | solution.py:57
  51.2 5.9 %collective-permute-start.22 = (bf16[8,16,256]{2,1,0:T(8,128)(2,1)S(1)}, bf16[8,16,256]{2,1,0:T(8,128)(2,1)S(1)}, u32[]{:S(2)}, u32[]{:S(2)}) collective-permute-start(bf16[8,16,256]{2,1,0:T(8,128)(2,1)S(1)} %get-tuple-element.61), channel_id=1, source_target_pairs={{0,2},{1,3},{2,0},{3,1},{4,6},{5,7},{6,4},{7,5},{8,10},{9,11},{10,... | collective-permute-start | bytes 196616 | tf_op jit(solution)/shard_map/ppermute | solution.py:57
  52.7 6.1 %collective-permute-start.23 = (bf16[8,16,256]{2,1,0:T(8,128)(2,1)S(1)}, bf16[8,16,256]{2,1,0:T(8,128)(2,1)S(1)}, u32[]{:S(2)}, u32[]{:S(2)}) collective-permute-start(bf16[8,16,256]{2,1,0:T(8,128)(2,1)S(1)} %get-tuple-element.62), channel_id=1, source_target_pairs={{0,3},{1,2},{2,1},{3,0},{4,7},{5,6},{6,5},{7,4},{8,11},{9,10},{10,... | collective-permute-start | bytes 196616 | tf_op jit(solution)/shard_map/ppermute | solution.py:57
  58.9 1.4 %collective-permute-start.24 = (bf16[8,32,256]{2,1,0:T(8,128)(2,1)S(1)}, bf16[8,32,256]{2,1,0:T(8,128)(2,1)S(1)}, u32[]{:S(2)}, u32[]{:S(2)}) collective-permute-start(bf16[8,32,256]{2,1,0:T(8,128)(2,1)S(1)} %get-tuple-element.64), channel_id=1, source_target_pairs={{0,4},{4,0},{8,12},{12,8},{16,20},{20,16},{24,28},{28,24},{1,5},{5... | collective-permute-start | bytes 393224 | tf_op jit(solution)/shard_map/ppermute | solution.py:48
  (3 other events, 5.0 us)

commit v5 on v4

--- a/solution.py
+++ b/solution.py
@@ -252,13 +252,35 @@
     other[...] = sent[...].astype(other.dtype)
 
 
-def join_kernel(own, other, out):
+def join_kernel(mine, part, *refs):
+    out, held, sem = refs[-3:]
     half = out.shape[1] // 2
     core = lax.axis_index("pix") % 2
     for c in range(2):
         for b in range(half):
-            out[:, core * half + b, c, :] = own[c * half + b]
-            out[:, (1 - core) * half + b, c, :] = other[c * half + b].astype(F32)
+            held[:, b, c, :] = part[c * half + b].astype(F32)
+    which = core if mine else 1 - core
+    copy = pltpu.make_async_copy(held, out.at[:, pl.ds(which * half, half)], sem)
+    copy.start()
+    copy.wait()
+
+
+def join(part, shape, before=None):
+    half = (shape[0], shape[1] // 2) + tuple(shape[2:])
+    anywhere = pl.BlockSpec(memory_space=pl.ANY)
+    args = (part,) if before is None else (part, before)
+    moved = size_of(part.shape, part.dtype) + size_of(half, F32)
+    return pl.pallas_call(
+        functools.partial(join_kernel, before is None),
+        out_shape=jax.ShapeDtypeStruct(shape, F32),
+        in_specs=[VMEM] + [anywhere] * (len(args) - 1),
+        out_specs=anywhere,
+        scratch_shapes=[pltpu.VMEM(half, F32), pltpu.SemaphoreType.DMA],
+        input_output_aliases={} if before is None else {1: 0},
+        compiler_params=pltpu.CompilerParams(vmem_limit_bytes=2 * moved + 2**20),
+        cost_estimate=pl.CostEstimate(flops=0, bytes_accessed=moved, transcendentals=0),
+        name="join",
+    )(*args)
 
 
 def tables(times, time):
@@ -348,7 +370,9 @@
         [(block, F32), (block, BF16)],
         [((2 * half, cut, time), F32), (block, F32)],
     )(*pieces)
-    return call(join_kernel, [(fields.shape, F32)])(own, swap_pix(other, 1, pix))[0]
+    other = swap_pix(other, 1, pix)
+    result = join(own, fields.shape)
+    return join(other, fields.shape, result)
 
 
 def split_length(length):

time: 61.5 us -> 61.3 us (level)
  waiting for transfers between devices: 15.1 us -> 14.3 us
    pallas_call x0 -> x2, Pallas kernels: none -> 1.59 us  [join(): pl.pallas_call(functools.partial(join_kernel, before is None), out_shape=...]
    pallas_call x12 -> x11, Pallas kernels: 13.5 us -> 12.5 us  [run(): pl.pallas_call(kernel, out_shape=tuple((jax.ShapeDtypeStruct(*out) for ou...]
    ppermute x5, waiting for transfers between devices: 2.2 us -> 1.39 us  [swap_pix(): return lax.ppermute(value, 'pix', [(i, i ^ mask) for i in range(size)])]
  transfers between devices with their start and end apart: 25 -> 25, of which waited for: 10 -> 10; matrix products, arithmetic and copies ran while one was open for 2% -> 2% of each run, Pallas kernels for 17% -> 19%
where the time goes in v5:
time: 61.3 us; the launch traced here: 61.1 us
  starting transfers between devices  29.2 us (48%)
  waiting for transfers between devices  14.3 us (23%)
  Pallas kernels  14.1 us (23%)
  local copies, waits for them, and re-layouts  3.08 us (5%)
    ppermute x12, starting transfers between devices, swap_chip(): return lax.ppermute(value, 'pix', pairs)  15.5 us
    pallas_call x11, Pallas kernels, run(): pl.pallas_call(kernel, out_shape=tuple((jax.ShapeDtypeStruct(*out) for ou...  12.5 us
    ppermute x8, starting transfers between devices, swap_tm(): return lax.ppermute(value, 'tm', [(i, i ^ mask) for i in range(size)])  12.5 us
    ppermute x8, waiting for transfers between devices, swap_tm(): return lax.ppermute(value, 'tm', [(i, i ^ mask) for i in range(size)])  6.86 us
    ppermute x12, waiting for transfers between devices, swap_chip(): return lax.ppermute(value, 'pix', pairs)  6.01 us
    unnamed x20, local copies, waits for them, and re-layouts  2.31 us
    pallas_call x2, Pallas kernels, join(): pl.pallas_call(functools.partial(join_kernel, before is None), out_shape=...  1.59 us
    ppermute x5, waiting for transfers between devices, swap_pix(): return lax.ppermute(value, 'pix', [(i, i ^ mask) for i in range(size)])  1.39 us
  transfers between devices with their start and end apart: 25, of which 10 were waited for; matrix products, arithmetic and copies ran while one was open for 2% of the time, Pallas kernels for 19%

profile of v5, /device:TPU:0, one launch (start us, length us, event | category | flops | bytes accessed | tf_op | source)
XLA Modules:
  0.0 61.1 jit_solution(6510644374163173714)
XLA Ops:
  0.0 0.5 collective-permute-start.2
  0.5 1.0 %copy-done.2 = f32[32,8,2,256]{3,2,1,0:T(2,128)S(1)} copy-done((f32[32,8,2,256]{3,2,1,0:T(2,128)S(1)}, f32[32,8,2,256]{3,2,1,0:T(2,128)}, u32[]{:S(2)}) %copy-start.2) | copy-done | bytes 524312
  2.3 0.9 %collective-permute-done.1.other = f32[4,32,256]{2,1,0:T(8,128)S(1)} collective-permute-done((f32[4,32,256]{2,1,0:T(8,128)S(1)}, f32[4,32,256]{2,1,0:T(8,128)S(1)}, u32[]{:S(2)}, u32[]{:S(2)}) %collective-permute-start.1) | collective-permute-done | bytes 131104 | tf_op jit(solution)/shard_map/ppermute | solution.py:48
  3.2 2.9 %collective-permute-start.3 = (bf16[4,64,256]{2,1,0:T(8,128)(2,1)S(1)}, bf16[4,64,256]{2,1,0:T(8,128)(2,1)S(1)}, u32[]{:S(2)}, u32[]{:S(2)}) collective-permute-start(bf16[4,64,256]{2,1,0:T(8,128)(2,1)S(1)} %get-tuple-element.41.refs_4_), channel_id=1, source_target_pairs={{0,8},{4,20},{8,0},{12,28},{16,24},{20,4},{24,16},{28,12},{1,9},{5... | collective-permute-start | bytes 393224 | tf_op jit(solution)/shard_map/ppermute | solution.py:53
  6.1 1.5 %collective-permute-start.4 = (bf16[4,64,256]{2,1,0:T(8,128)(2,1)S(1)}, bf16[4,64,256]{2,1,0:T(8,128)(2,1)S(1)}, u32[]{:S(2)}, u32[]{:S(2)}) collective-permute-start(bf16[4,64,256]{2,1,0:T(8,128)(2,1)S(1)} %get-tuple-element.41.refs_4_), channel_id=1, source_target_pairs={{0,16},{4,12},{8,24},{12,4},{16,0},{20,28},{24,8},{28,20},{1,17},{... | collective-permute-start | bytes 393224 | tf_op jit(solution)/shard_map/ppermute | solution.py:53
  7.7 1.2 %copy-done = bf16[2048,256]{1,0:T(8,128)(2,1)S(1)} copy-done((bf16[2048,256]{1,0:T(8,128)(2,1)S(1)}, bf16[2048,256]{1,0:T(8,128)(2,1)}, u32[]{:S(2)}) %copy-start) | copy-done | bytes 1048600
  9.4 2.0 %collective-permute-start.10 = (bf16[4,64,256]{2,1,0:T(8,128)(2,1)S(1)}, bf16[4,64,256]{2,1,0:T(8,128)(2,1)S(1)}, u32[]{:S(2)}, u32[]{:S(2)}) collective-permute-start(bf16[4,64,256]{2,1,0:T(8,128)(2,1)S(1)} %get-tuple-element.47.refs_4_), channel_id=1, source_target_pairs={{0,16},{4,12},{8,24},{12,4},{16,0},{20,28},{24,8},{28,20},{1,17},{... | collective-permute-start | bytes 393224 | tf_op jit(solution)/shard_map/ppermute | solution.py:53
  11.8 1.6 %collective-permute-start.11 = (bf16[4,64,256]{2,1,0:T(8,128)(2,1)S(1)}, bf16[4,64,256]{2,1,0:T(8,128)(2,1)S(1)}, u32[]{:S(2)}, u32[]{:S(2)}) collective-permute-start(bf16[4,64,256]{2,1,0:T(8,128)(2,1)S(1)} %get-tuple-element.47.refs_4_), channel_id=1, source_target_pairs={{0,24},{4,28},{8,16},{12,20},{16,8},{20,12},{24,0},{28,4},{1,25},{... | collective-permute-start | bytes 393224 | tf_op jit(solution)/shard_map/ppermute | solution.py:53
  14.1 4.7 %shard_map.96 = (f32[4,64,256]{2,1,0:T(8,128)S(1)}, bf16[4,64,256]{2,1,0:T(8,128)(2,1)S(1)}, bf16[4,64,256]{2,1,0:T(8,128)(2,1)S(1)}, bf16[4,64,256]{2,1,0:T(8,128)(2,1)S(1)}) custom-call(bf16[2048,256]{1,0:T(8,128)(2,1)S(1)} %copy-done.1, bf16[2048,256]{1,0:T(8,128)(2,1)S(1)} %collective-permute-done.2.profiles.refs_1_, ...), custom_call_target="tpu_custom_call" | custom-call | flops 4294967296 | bytes 5373952 | tf_op jit(solution)/shard_map/pallas_call | solution.py:28
  18.9 1.8 %collective-permute-start.6 = (bf16[4,64,256]{2,1,0:T(8,128)(2,1)S(1)}, bf16[4,64,256]{2,1,0:T(8,128)(2,1)S(1)}, u32[]{:S(2)}, u32[]{:S(2)}) collective-permute-start(bf16[4,64,256]{2,1,0:T(8,128)(2,1)S(1)} %get-tuple-element.43), channel_id=1, source_target_pairs={{0,8},{4,20},{8,0},{12,28},{16,24},{20,4},{24,16},{28,12},{1,9},{5... | collective-permute-start | bytes 393224 | tf_op jit(solution)/shard_map/ppermute | solution.py:53
  20.7 1.6 %collective-permute-start.7 = (bf16[4,64,256]{2,1,0:T(8,128)(2,1)S(1)}, bf16[4,64,256]{2,1,0:T(8,128)(2,1)S(1)}, u32[]{:S(2)}, u32[]{:S(2)}) collective-permute-start(bf16[4,64,256]{2,1,0:T(8,128)(2,1)S(1)} %get-tuple-element.44), channel_id=1, source_target_pairs={{0,16},{4,12},{8,24},{12,4},{16,0},{20,28},{24,8},{28,20},{1,17},{... | collective-permute-start | bytes 393224 | tf_op jit(solution)/shard_map/ppermute | solution.py:53
  22.4 4.7 %shard_map.98 = (f32[4,64,256]{2,1,0:T(8,128)S(1)}, bf16[4,64,256]{2,1,0:T(8,128)(2,1)S(1)}, bf16[4,64,256]{2,1,0:T(8,128)(2,1)S(1)}, bf16[4,64,256]{2,1,0:T(8,128)(2,1)S(1)}) custom-call(bf16[2048,256]{1,0:T(8,128)(2,1)S(1)} %copy-done.1, bf16[2048,256]{1,0:T(8,128)(2,1)S(1)} %collective-permute-done.2.profiles.refs_1_, ...), custom_call_target="tpu_custom_call" | custom-call | flops 4294967296 | bytes 5373952 | tf_op jit(solution)/shard_map/pallas_call | solution.py:28
  27.2 1.8 %collective-permute-start.12 = (bf16[4,64,256]{2,1,0:T(8,128)(2,1)S(1)}, bf16[4,64,256]{2,1,0:T(8,128)(2,1)S(1)}, u32[]{:S(2)}, u32[]{:S(2)}) collective-permute-start(bf16[4,64,256]{2,1,0:T(8,128)(2,1)S(1)} %get-tuple-element.49), channel_id=1, source_target_pairs={{0,8},{4,20},{8,0},{12,28},{16,24},{20,4},{24,16},{28,12},{1,9},{5... | collective-permute-start | bytes 393224 | tf_op jit(solution)/shard_map/ppermute | solution.py:53
  29.0 1.6 %collective-permute-start.13 = (bf16[4,64,256]{2,1,0:T(8,128)(2,1)S(1)}, bf16[4,64,256]{2,1,0:T(8,128)(2,1)S(1)}, u32[]{:S(2)}, u32[]{:S(2)}) collective-permute-start(bf16[4,64,256]{2,1,0:T(8,128)(2,1)S(1)} %get-tuple-element.50), channel_id=1, source_target_pairs={{0,16},{4,12},{8,24},{12,4},{16,0},{20,28},{24,8},{28,20},{1,17},{... | collective-permute-start | bytes 393224 | tf_op jit(solution)/shard_map/ppermute | solution.py:53
  30.9 2.7 %collective-permute-done.12.refs_2_ = bf16[4,64,256]{2,1,0:T(8,128)(2,1)S(1)} collective-permute-done((bf16[4,64,256]{2,1,0:T(8,128)(2,1)S(1)}, bf16[4,64,256]{2,1,0:T(8,128)(2,1)S(1)}, u32[]{:S(2)}, u32[]{:S(2)}) %collective-permute-start.12) | collective-permute-done | bytes 131104 | tf_op jit(solution)/shard_map/ppermute | solution.py:53
  33.6 1.6 %collective-permute-done.13.refs_3_ = bf16[4,64,256]{2,1,0:T(8,128)(2,1)S(1)} collective-permute-done((bf16[4,64,256]{2,1,0:T(8,128)(2,1)S(1)}, bf16[4,64,256]{2,1,0:T(8,128)(2,1)S(1)}, u32[]{:S(2)}, u32[]{:S(2)}) %collective-permute-start.13) | collective-permute-done | bytes 131104 | tf_op jit(solution)/shard_map/ppermute | solution.py:53
  35.2 1.3 %collective-permute-done.14.refs_4_ = bf16[4,64,256]{2,1,0:T(8,128)(2,1)S(1)} collective-permute-done((bf16[4,64,256]{2,1,0:T(8,128)(2,1)S(1)}, bf16[4,64,256]{2,1,0:T(8,128)(2,1)S(1)}, u32[]{:S(2)}, u32[]{:S(2)}) %collective-permute-start.14) | collective-permute-done | bytes 131104 | tf_op jit(solution)/shard_map/ppermute | solution.py:53
  36.6 1.6 %collective-permute-start.15 = (bf16[8,16,256]{2,1,0:T(8,128)(2,1)S(1)}, bf16[8,16,256]{2,1,0:T(8,128)(2,1)S(1)}, u32[]{:S(2)}, u32[]{:S(2)}) collective-permute-start(bf16[8,16,256]{2,1,0:T(8,128)(2,1)S(1)} %get-tuple-element.52), channel_id=1, source_target_pairs={{0,1},{1,0},{2,3},{3,2},{4,5},{5,4},{6,7},{7,6},{8,9},{9,8},{10,11... | collective-permute-start | bytes 196616 | tf_op jit(solution)/shard_map/ppermute | solution.py:57
  38.2 2.6 %collective-permute-start.18 = (bf16[4,16,256]{2,1,0:T(8,128)(2,1)S(1)}, bf16[4,16,256]{2,1,0:T(8,128)(2,1)S(1)}, u32[]{:S(2)}, u32[]{:S(2)}) collective-permute-start(bf16[4,16,256]{2,1,0:T(8,128)(2,1)S(1)} %get-tuple-element.57), channel_id=1, source_target_pairs={{0,2},{1,3},{2,0},{3,1},{4,6},{5,7},{6,4},{7,5},{8,10},{9,11},{10,... | collective-permute-start | bytes 98312 | tf_op jit(solution)/shard_map/ppermute | solution.py:57
  41.0 1.6 %collective-permute-start.16 = (bf16[4,16,256]{2,1,0:T(8,128)(2,1)S(1)}, bf16[4,16,256]{2,1,0:T(8,128)(2,1)S(1)}, u32[]{:S(2)}, u32[]{:S(2)}) collective-permute-start(bf16[4,16,256]{2,1,0:T(8,128)(2,1)S(1)} %get-tuple-element.54), channel_id=1, source_target_pairs={{0,2},{1,3},{2,0},{3,1},{4,6},{5,7},{6,4},{7,5},{8,10},{9,11},{10,... | collective-permute-start | bytes 98312 | tf_op jit(solution)/shard_map/ppermute | solution.py:57
  42.7 1.9 %collective-permute-start.17 = (bf16[4,16,256]{2,1,0:T(8,128)(2,1)S(1)}, bf16[4,16,256]{2,1,0:T(8,128)(2,1)S(1)}, u32[]{:S(2)}, u32[]{:S(2)}) collective-permute-start(bf16[4,16,256]{2,1,0:T(8,128)(2,1)S(1)} %get-tuple-element.55), channel_id=1, source_target_pairs={{0,3},{1,2},{2,1},{3,0},{4,7},{5,6},{6,5},{7,4},{8,11},{9,10},{10,... | collective-permute-start | bytes 98312 | tf_op jit(solution)/shard_map/ppermute | solution.py:57
  45.7 0.8 %collective-permute-done.19.refs_6_ = bf16[4,16,256]{2,1,0:T(8,128)(2,1)S(1)} collective-permute-done((bf16[4,16,256]{2,1,0:T(8,128)(2,1)S(1)}, bf16[4,16,256]{2,1,0:T(8,128)(2,1)S(1)}, u32[]{:S(2)}, u32[]{:S(2)}) %collective-permute-start.19) | collective-permute-done | bytes 32800 | tf_op jit(solution)/shard_map/ppermute | solution.py:57
  46.5 1.9 %collective-permute-done.17.refs_3_ = bf16[4,16,256]{2,1,0:T(8,128)(2,1)S(1)} collective-permute-done((bf16[4,16,256]{2,1,0:T(8,128)(2,1)S(1)}, bf16[4,16,256]{2,1,0:T(8,128)(2,1)S(1)}, u32[]{:S(2)}, u32[]{:S(2)}) %collective-permute-start.17) | collective-permute-done | bytes 32800 | tf_op jit(solution)/shard_map/ppermute | solution.py:57
  48.5 1.8 %shard_map.100 = (f32[8,16,256]{2,1,0:T(8,128)S(1)}, bf16[8,16,256]{2,1,0:T(8,128)(2,1)S(1)}, bf16[8,16,256]{2,1,0:T(8,128)(2,1)S(1)}, bf16[8,16,256]{2,1,0:T(8,128)(2,1)S(1)}) custom-call(bf16[8,16,256]{2,1,0:T(8,128)(2,1)S(1)} %collective-permute-done.15.refs_0_, f32[4,16,256]{2,1,0:T(8,128)S(1)} %get-tuple-element.53.refs_1_, ...), custom_call_target="tpu_custom_call" | custom-call | flops 1000000000 | bytes 1318912 | tf_op jit(solution)/shard_map/pallas_call | solution.py:28
  50.2 1.0 %collective-permute-start.21 = (bf16[8,16,256]{2,1,0:T(8,128)(2,1)S(1)}, bf16[8,16,256]{2,1,0:T(8,128)(2,1)S(1)}, u32[]{:S(2)}, u32[]{:S(2)}) collective-permute-start(bf16[8,16,256]{2,1,0:T(8,128)(2,1)S(1)} %get-tuple-element.60), channel_id=1, source_target_pairs={{0,1},{1,0},{2,3},{3,2},{4,5},{5,4},{6,7},{7,6},{8,9},{9,8},{10,11... | collective-permute-start | bytes 196616 | tf_op jit(solution)/shard_map/ppermute | solution.py:57
  51.2 1.6 %collective-permute-start.22 = (bf16[8,16,256]{2,1,0:T(8,128)(2,1)S(1)}, bf16[8,16,256]{2,1,0:T(8,128)(2,1)S(1)}, u32[]{:S(2)}, u32[]{:S(2)}) collective-permute-start(bf16[8,16,256]{2,1,0:T(8,128)(2,1)S(1)} %get-tuple-element.61), channel_id=1, source_target_pairs={{0,2},{1,3},{2,0},{3,1},{4,6},{5,7},{6,4},{7,5},{8,10},{9,11},{10,... | collective-permute-start | bytes 196616 | tf_op jit(solution)/shard_map/ppermute | solution.py:57
  52.7 1.9 %collective-permute-start.23 = (bf16[8,16,256]{2,1,0:T(8,128)(2,1)S(1)}, bf16[8,16,256]{2,1,0:T(8,128)(2,1)S(1)}, u32[]{:S(2)}, u32[]{:S(2)}) collective-permute-start(bf16[8,16,256]{2,1,0:T(8,128)(2,1)S(1)} %get-tuple-element.62), channel_id=1, source_target_pairs={{0,3},{1,2},{2,1},{3,0},{4,7},{5,6},{6,5},{7,4},{8,11},{9,10},{10,... | collective-permute-start | bytes 196616 | tf_op jit(solution)/shard_map/ppermute | solution.py:57
  54.7 2.4 %collective-permute-done.22.refs_2_ = bf16[8,16,256]{2,1,0:T(8,128)(2,1)S(1)} collective-permute-done((bf16[8,16,256]{2,1,0:T(8,128)(2,1)S(1)}, bf16[8,16,256]{2,1,0:T(8,128)(2,1)S(1)}, u32[]{:S(2)}, u32[]{:S(2)}) %collective-permute-start.22) | collective-permute-done | bytes 65568 | tf_op jit(solution)/shard_map/ppermute | solution.py:57
  57.0 1.8 %collective-permute-done.23.refs_3_ = bf16[8,16,256]{2,1,0:T(8,128)(2,1)S(1)} collective-permute-done((bf16[8,16,256]{2,1,0:T(8,128)(2,1)S(1)}, bf16[8,16,256]{2,1,0:T(8,128)(2,1)S(1)}, u32[]{:S(2)}, u32[]{:S(2)}) %collective-permute-start.23) | collective-permute-done | bytes 65568 | tf_op jit(solution)/shard_map/ppermute | solution.py:57
  59.0 0.8 %join.2.refs_0_ = f32[32,8,2,256]{3,2,1,0:T(2,128)} custom-call(f32[8,32,256]{2,1,0:T(8,128)S(1)} %get-tuple-element.64.part), custom_call_target="tpu_custom_call" | custom-call | bytes 524288 | tf_op jit(solution)/shard_map/join/pallas_call | solution.py:273
  59.8 0.5 collective-permute-done.24.part
  60.3 0.8 %join.3 = f32[32,8,2,256]{3,2,1,0:T(2,128)} custom-call(bf16[8,32,256]{2,1,0:T(8,128)(2,1)S(1)} %collective-permute-done.24.part, f32[32,8,2,256]{3,2,1,0:T(2,128)} %join.2.refs_0_), custom_call_target="tpu_custom_call", output_to_operand_aliasing={{}: (1, {})} | custom-call | bytes 393216 | tf_op jit(solution)/shard_map/join/pallas_call | solution.py:273
  (57 shorter events, 4.3 us)
Async XLA Ops:
  0.0 9.4 %collective-permute-start.2 = (bf16[2048,256]{1,0:T(8,128)(2,1)}, bf16[2048,256]{1,0:T(8,128)(2,1)S(1)}, u32[]{:S(2)}, u32[]{:S(2)}) collective-permute-start(bf16[2048,256]{1,0:T(8,128)(2,1)} %refs_0_.3), channel_id=1, source_target_pairs={{0,4},{4,0},{8,12},{12,8},{16,20},{20,16},{24,28},{28,24},{1,5},{5... | collective-permute-start | bytes 3145736 | tf_op jit(solution)/shard_map/ppermute | solution.py:48
  1.7 1.4 %collective-permute-start.1 = (f32[4,32,256]{2,1,0:T(8,128)S(1)}, f32[4,32,256]{2,1,0:T(8,128)S(1)}, u32[]{:S(2)}, u32[]{:S(2)}) collective-permute-start(f32[4,32,256]{2,1,0:T(8,128)S(1)} %get-tuple-element.39), channel_id=1, source_target_pairs={{0,4},{4,0},{8,12},{12,8},{16,20},{20,16},{24,28},{28,24},{1,5},{5... | collective-permute-start | bytes 393224 | tf_op jit(solution)/shard_map/ppermute | solution.py:48
  1.8 7.4 %collective-permute-start = (f32[4,32,256]{2,1,0:T(8,128)S(1)}, f32[4,32,256]{2,1,0:T(8,128)S(1)}, u32[]{:S(2)}, u32[]{:S(2)}) collective-permute-start(f32[4,32,256]{2,1,0:T(8,128)S(1)} %get-tuple-element.36), channel_id=1, source_target_pairs={{0,4},{4,0},{8,12},{12,8},{16,20},{20,16},{24,28},{28,24},{1,5},{5... | collective-permute-start | bytes 393224 | tf_op jit(solution)/shard_map/ppermute | solution.py:48
  3.2 6.1 %copy-start.9 = (f32[8,1024]{1,0:T(8,128)S(1)}, f32[8,1024]{1,0:T(8,128)}, u32[]{:S(2)}) copy-start(f32[8,1024]{1,0:T(8,128)} %param.11) | copy-start | bytes 98308
  3.2 8.6 %collective-permute-start.3 = (bf16[4,64,256]{2,1,0:T(8,128)(2,1)S(1)}, bf16[4,64,256]{2,1,0:T(8,128)(2,1)S(1)}, u32[]{:S(2)}, u32[]{:S(2)}) collective-permute-start(bf16[4,64,256]{2,1,0:T(8,128)(2,1)S(1)} %get-tuple-element.41.refs_4_), channel_id=1, source_target_pairs={{0,8},{4,20},{8,0},{12,28},{16,24},{20,4},{24,16},{28,12},{1,9},{5... | collective-permute-start | bytes 393224 | tf_op jit(solution)/shard_map/ppermute | solution.py:53
  6.1 7.3 %collective-permute-start.4 = (bf16[4,64,256]{2,1,0:T(8,128)(2,1)S(1)}, bf16[4,64,256]{2,1,0:T(8,128)(2,1)S(1)}, u32[]{:S(2)}, u32[]{:S(2)}) collective-permute-start(bf16[4,64,256]{2,1,0:T(8,128)(2,1)S(1)} %get-tuple-element.41.refs_4_), channel_id=1, source_target_pairs={{0,16},{4,12},{8,24},{12,4},{16,0},{20,28},{24,8},{28,20},{1,17},{... | collective-permute-start | bytes 393224 | tf_op jit(solution)/shard_map/ppermute | solution.py:53
  7.7 6.5 %collective-permute-start.5 = (bf16[4,64,256]{2,1,0:T(8,128)(2,1)S(1)}, bf16[4,64,256]{2,1,0:T(8,128)(2,1)S(1)}, u32[]{:S(2)}, u32[]{:S(2)}) collective-permute-start(bf16[4,64,256]{2,1,0:T(8,128)(2,1)S(1)} %get-tuple-element.41.refs_4_), channel_id=1, source_target_pairs={{0,24},{4,28},{8,16},{12,20},{16,8},{20,12},{24,0},{28,4},{1,25},{... | collective-permute-start | bytes 393224 | tf_op jit(solution)/shard_map/ppermute | solution.py:53
  9.3 19.7 %collective-permute-start.20 = (f32[8,1024]{1,0:T(8,128)S(1)}, f32[8,1024]{1,0:T(8,128)S(1)}, u32[]{:S(2)}, u32[]{:S(2)}) collective-permute-start(f32[8,1024]{1,0:T(8,128)S(1)} %copy-done.9), channel_id=1, source_target_pairs={{0,4},{4,0},{8,12},{12,8},{16,20},{20,16},{24,28},{28,24},{1,5},{5... | collective-permute-start | bytes 98312 | tf_op jit(solution)/shard_map/ppermute | solution.py:48
  9.4 4.7 %copy-start.1 = (bf16[2048,256]{1,0:T(8,128)(2,1)S(1)}, bf16[2048,256]{1,0:T(8,128)(2,1)}, u32[]{:S(2)}) copy-start(bf16[2048,256]{1,0:T(8,128)(2,1)} %refs_0_.3) | copy-start | bytes 3145732
  9.4 11.2 %collective-permute-start.10 = (bf16[4,64,256]{2,1,0:T(8,128)(2,1)S(1)}, bf16[4,64,256]{2,1,0:T(8,128)(2,1)S(1)}, u32[]{:S(2)}, u32[]{:S(2)}) collective-permute-start(bf16[4,64,256]{2,1,0:T(8,128)(2,1)S(1)} %get-tuple-element.47.refs_4_), channel_id=1, source_target_pairs={{0,16},{4,12},{8,24},{12,4},{16,0},{20,28},{24,8},{28,20},{1,17},{... | collective-permute-start | bytes 393224 | tf_op jit(solution)/shard_map/ppermute | solution.py:53
  11.8 10.5 %collective-permute-start.11 = (bf16[4,64,256]{2,1,0:T(8,128)(2,1)S(1)}, bf16[4,64,256]{2,1,0:T(8,128)(2,1)S(1)}, u32[]{:S(2)}, u32[]{:S(2)}) collective-permute-start(bf16[4,64,256]{2,1,0:T(8,128)(2,1)S(1)} %get-tuple-element.47.refs_4_), channel_id=1, source_target_pairs={{0,24},{4,28},{8,16},{12,20},{16,8},{20,12},{24,0},{28,4},{1,25},{... | collective-permute-start | bytes 393224 | tf_op jit(solution)/shard_map/ppermute | solution.py:53
  13.5 9.0 %collective-permute-start.9 = (bf16[4,64,256]{2,1,0:T(8,128)(2,1)S(1)}, bf16[4,64,256]{2,1,0:T(8,128)(2,1)S(1)}, u32[]{:S(2)}, u32[]{:S(2)}) collective-permute-start(bf16[4,64,256]{2,1,0:T(8,128)(2,1)S(1)} %get-tuple-element.47.refs_4_), channel_id=1, source_target_pairs={{0,8},{4,20},{8,0},{12,28},{16,24},{20,4},{24,16},{28,12},{1,9},{5... | collective-permute-start | bytes 393224 | tf_op jit(solution)/shard_map/ppermute | solution.py:53
  18.9 11.7 %collective-permute-start.6 = (bf16[4,64,256]{2,1,0:T(8,128)(2,1)S(1)}, bf16[4,64,256]{2,1,0:T(8,128)(2,1)S(1)}, u32[]{:S(2)}, u32[]{:S(2)}) collective-permute-start(bf16[4,64,256]{2,1,0:T(8,128)(2,1)S(1)} %get-tuple-element.43), channel_id=1, source_target_pairs={{0,8},{4,20},{8,0},{12,28},{16,24},{20,4},{24,16},{28,12},{1,9},{5... | collective-permute-start | bytes 393224 | tf_op jit(solution)/shard_map/ppermute | solution.py:53
  20.7 10.1 %collective-permute-start.7 = (bf16[4,64,256]{2,1,0:T(8,128)(2,1)S(1)}, bf16[4,64,256]{2,1,0:T(8,128)(2,1)S(1)}, u32[]{:S(2)}, u32[]{:S(2)}) collective-permute-start(bf16[4,64,256]{2,1,0:T(8,128)(2,1)S(1)} %get-tuple-element.44), channel_id=1, source_target_pairs={{0,16},{4,12},{8,24},{12,4},{16,0},{20,28},{24,8},{28,20},{1,17},{... | collective-permute-start | bytes 393224 | tf_op jit(solution)/shard_map/ppermute | solution.py:53
  22.3 8.5 %collective-permute-start.8 = (bf16[4,64,256]{2,1,0:T(8,128)(2,1)S(1)}, bf16[4,64,256]{2,1,0:T(8,128)(2,1)S(1)}, u32[]{:S(2)}, u32[]{:S(2)}) collective-permute-start(bf16[4,64,256]{2,1,0:T(8,128)(2,1)S(1)} %get-tuple-element.45), channel_id=1, source_target_pairs={{0,24},{4,28},{8,16},{12,20},{16,8},{20,12},{24,0},{28,4},{1,25},{... | collective-permute-start | bytes 393224 | tf_op jit(solution)/shard_map/ppermute | solution.py:53
  27.2 6.4 %collective-permute-start.12 = (bf16[4,64,256]{2,1,0:T(8,128)(2,1)S(1)}, bf16[4,64,256]{2,1,0:T(8,128)(2,1)S(1)}, u32[]{:S(2)}, u32[]{:S(2)}) collective-permute-start(bf16[4,64,256]{2,1,0:T(8,128)(2,1)S(1)} %get-tuple-element.49), channel_id=1, source_target_pairs={{0,8},{4,20},{8,0},{12,28},{16,24},{20,4},{24,16},{28,12},{1,9},{5... | collective-permute-start | bytes 393224 | tf_op jit(solution)/shard_map/ppermute | solution.py:53
  29.0 6.2 %collective-permute-start.13 = (bf16[4,64,256]{2,1,0:T(8,128)(2,1)S(1)}, bf16[4,64,256]{2,1,0:T(8,128)(2,1)S(1)}, u32[]{:S(2)}, u32[]{:S(2)}) collective-permute-start(bf16[4,64,256]{2,1,0:T(8,128)(2,1)S(1)} %get-tuple-element.50), channel_id=1, source_target_pairs={{0,16},{4,12},{8,24},{12,4},{16,0},{20,28},{24,8},{28,20},{1,17},{... | collective-permute-start | bytes 393224 | tf_op jit(solution)/shard_map/ppermute | solution.py:53
  30.6 5.9 %collective-permute-start.14 = (bf16[4,64,256]{2,1,0:T(8,128)(2,1)S(1)}, bf16[4,64,256]{2,1,0:T(8,128)(2,1)S(1)}, u32[]{:S(2)}, u32[]{:S(2)}) collective-permute-start(bf16[4,64,256]{2,1,0:T(8,128)(2,1)S(1)} %get-tuple-element.51), channel_id=1, source_target_pairs={{0,24},{4,28},{8,16},{12,20},{16,8},{20,12},{24,0},{28,4},{1,25},{... | collective-permute-start | bytes 393224 | tf_op jit(solution)/shard_map/ppermute | solution.py:53
  36.6 11.8 %collective-permute-start.15 = (bf16[8,16,256]{2,1,0:T(8,128)(2,1)S(1)}, bf16[8,16,256]{2,1,0:T(8,128)(2,1)S(1)}, u32[]{:S(2)}, u32[]{:S(2)}) collective-permute-start(bf16[8,16,256]{2,1,0:T(8,128)(2,1)S(1)} %get-tuple-element.52), channel_id=1, source_target_pairs={{0,1},{1,0},{2,3},{3,2},{4,5},{5,4},{6,7},{7,6},{8,9},{9,8},{10,11... | collective-permute-start | bytes 196616 | tf_op jit(solution)/shard_map/ppermute | solution.py:57
  38.2 7.5 %collective-permute-start.18 = (bf16[4,16,256]{2,1,0:T(8,128)(2,1)S(1)}, bf16[4,16,256]{2,1,0:T(8,128)(2,1)S(1)}, u32[]{:S(2)}, u32[]{:S(2)}) collective-permute-start(bf16[4,16,256]{2,1,0:T(8,128)(2,1)S(1)} %get-tuple-element.57), channel_id=1, source_target_pairs={{0,2},{1,3},{2,0},{3,1},{4,6},{5,7},{6,4},{7,5},{8,10},{9,11},{10,... | collective-permute-start | bytes 98312 | tf_op jit(solution)/shard_map/ppermute | solution.py:57
  40.8 5.7 %collective-permute-start.19 = (bf16[4,16,256]{2,1,0:T(8,128)(2,1)S(1)}, bf16[4,16,256]{2,1,0:T(8,128)(2,1)S(1)}, u32[]{:S(2)}, u32[]{:S(2)}) collective-permute-start(bf16[4,16,256]{2,1,0:T(8,128)(2,1)S(1)} %get-tuple-element.58), channel_id=1, source_target_pairs={{0,3},{1,2},{2,1},{3,0},{4,7},{5,6},{6,5},{7,4},{8,11},{9,10},{10,... | collective-permute-start | bytes 98312 | tf_op jit(solution)/shard_map/ppermute | solution.py:57
  41.0 5.4 %collective-permute-start.16 = (bf16[4,16,256]{2,1,0:T(8,128)(2,1)S(1)}, bf16[4,16,256]{2,1,0:T(8,128)(2,1)S(1)}, u32[]{:S(2)}, u32[]{:S(2)}) collective-permute-start(bf16[4,16,256]{2,1,0:T(8,128)(2,1)S(1)} %get-tuple-element.54), channel_id=1, source_target_pairs={{0,2},{1,3},{2,0},{3,1},{4,6},{5,7},{6,4},{7,5},{8,10},{9,11},{10,... | collective-permute-start | bytes 98312 | tf_op jit(solution)/shard_map/ppermute | solution.py:57
  42.7 5.7 %collective-permute-start.17 = (bf16[4,16,256]{2,1,0:T(8,128)(2,1)S(1)}, bf16[4,16,256]{2,1,0:T(8,128)(2,1)S(1)}, u32[]{:S(2)}, u32[]{:S(2)}) collective-permute-start(bf16[4,16,256]{2,1,0:T(8,128)(2,1)S(1)} %get-tuple-element.55), channel_id=1, source_target_pairs={{0,3},{1,2},{2,1},{3,0},{4,7},{5,6},{6,5},{7,4},{8,11},{9,10},{10,... | collective-permute-start | bytes 98312 | tf_op jit(solution)/shard_map/ppermute | solution.py:57
  45.4 3.0 %copy-start.3 = (bf16[256,256]{1,0:T(8,128)(2,1)S(1)}, bf16[256,256]{1,0:T(8,128)(2,1)}, u32[]{:S(2)}) copy-start(bf16[256,256]{1,0:T(8,128)(2,1)} %constant.32.clone.refs_9_) | copy-start | bytes 393220
  45.4 3.0 %copy-start.4 = (bf16[256,256]{1,0:T(8,128)(2,1)S(1)}, bf16[256,256]{1,0:T(8,128)(2,1)}, u32[]{:S(2)}) copy-start(bf16[256,256]{1,0:T(8,128)(2,1)} %constant.33.clone.refs_10_) | copy-start | bytes 393220
  45.5 3.0 %copy-start.5 = (bf16[256,256]{1,0:T(8,128)(2,1)S(1)}, bf16[256,256]{1,0:T(8,128)(2,1)}, u32[]{:S(2)}) copy-start(bf16[256,256]{1,0:T(8,128)(2,1)} %constant.34.clone.refs_11_) | copy-start | bytes 393220
  45.5 3.0 %copy-start.6 = (bf16[256,256]{1,0:T(8,128)(2,1)S(1)}, bf16[256,256]{1,0:T(8,128)(2,1)}, u32[]{:S(2)}) copy-start(bf16[256,256]{1,0:T(8,128)(2,1)} %constant.35.clone.refs_12_) | copy-start | bytes 393220
  45.5 3.0 %copy-start.8 = (f32[4,256]{1,0:T(4,128)S(1)}, f32[4,256]{1,0:T(4,128)}, u32[]{:S(2)}) copy-start(f32[4,256]{1,0:T(4,128)} %constant.37.clone.refs_14_) | copy-start | bytes 12292
  50.2 4.5 %collective-permute-start.21 = (bf16[8,16,256]{2,1,0:T(8,128)(2,1)S(1)}, bf16[8,16,256]{2,1,0:T(8,128)(2,1)S(1)}, u32[]{:S(2)}, u32[]{:S(2)}) collective-permute-start(bf16[8,16,256]{2,1,0:T(8,128)(2,1)S(1)} %get-tuple-element.60), channel_id=1, source_target_pairs={{0,1},{1,0},{2,3},{3,2},{4,5},{5,4},{6,7},{7,6},{8,9},{9,8},{10,11... | collective-permute-start | bytes 196616 | tf_op jit(solution)/shard_map/ppermute | solution.py:57
  51.2 5.9 %collective-permute-start.22 = (bf16[8,16,256]{2,1,0:T(8,128)(2,1)S(1)}, bf16[8,16,256]{2,1,0:T(8,128)(2,1)S(1)}, u32[]{:S(2)}, u32[]{:S(2)}) collective-permute-start(bf16[8,16,256]{2,1,0:T(8,128)(2,1)S(1)} %get-tuple-element.61), channel_id=1, source_target_pairs={{0,2},{1,3},{2,0},{3,1},{4,6},{5,7},{6,4},{7,5},{8,10},{9,11},{10,... | collective-permute-start | bytes 196616 | tf_op jit(solution)/shard_map/ppermute | solution.py:57
  52.7 6.1 %collective-permute-start.23 = (bf16[8,16,256]{2,1,0:T(8,128)(2,1)S(1)}, bf16[8,16,256]{2,1,0:T(8,128)(2,1)S(1)}, u32[]{:S(2)}, u32[]{:S(2)}) collective-permute-start(bf16[8,16,256]{2,1,0:T(8,128)(2,1)S(1)} %get-tuple-element.62), channel_id=1, source_target_pairs={{0,3},{1,2},{2,1},{3,0},{4,7},{5,6},{6,5},{7,4},{8,11},{9,10},{10,... | collective-permute-start | bytes 196616 | tf_op jit(solution)/shard_map/ppermute | solution.py:57
  58.9 1.4 %collective-permute-start.24 = (bf16[8,32,256]{2,1,0:T(8,128)(2,1)S(1)}, bf16[8,32,256]{2,1,0:T(8,128)(2,1)S(1)}, u32[]{:S(2)}, u32[]{:S(2)}) collective-permute-start(bf16[8,32,256]{2,1,0:T(8,128)(2,1)S(1)} %get-tuple-element.63), channel_id=1, source_target_pairs={{0,4},{4,0},{8,12},{12,8},{16,20},{20,16},{24,28},{28,24},{1,5},{5... | collective-permute-start | bytes 393224 | tf_op jit(solution)/shard_map/ppermute | solution.py:48
  (3 other events, 5.0 us)

commit v6 on v5

--- a/solution.py
+++ b/solution.py
@@ -185,10 +185,11 @@
     joint, refs = refs[0], refs[1:]
     each = times - 1
     blocks = refs[: each * count]
-    phase_cos, phase_sin, cos_high, cos_low, sin_high, sin_low, twist_cos, twist_sin = refs[
-        each * count : each * count + 8
+    phase_cos, phase_sin, cos_high, cos_low, less_high, less_low = refs[
+        each * count : each * count + 6
     ]
-    outs = refs[each * count + 8 : -2]
+    more_high, more_low, twist_cos, twist_sin = refs[each * count + 6 : each * count + 10]
+    outs = refs[each * count + 10 : -2]
     held, back = refs[-2:]
     z = lax.axis_index("tm")
     nb = sum(sizes)
@@ -214,16 +215,19 @@
         real.append(re * tc + im * ts)
         imag.append(im * tc - re * ts)
     real, imag = jnp.concatenate(real, axis=0), jnp.concatenate(imag, axis=0)
-    ch, cl, sh, sl = cos_high[...], cos_low[...], sin_high[...], sin_low[...]
-    freq_re = product(real, ch, cl) + product(imag, sh, sl)
-    freq_im = product(imag, ch, cl) - product(real, sh, sl)
+    ch, cl, dh, dl = cos_high[...], cos_low[...], less_high[...], less_low[...]
+    eh, el = more_high[...], more_low[...]
+    both = product(real + imag, ch, cl)
+    freq_re = both - product(imag, dh, dl)
+    freq_im = both - product(real, eh, el)
     shape = (times, nb, rows, time)
     pc = jnp.broadcast_to(phase_cos[...][:, None], shape).reshape(times * size, time)
     ps = jnp.broadcast_to(phase_sin[...][:, None], shape).reshape(times * size, time)
     spun_re = freq_re * pc - freq_im * ps
     spun_im = freq_re * ps + freq_im * pc
-    back_re = product(spun_re, ch, cl) - product(spun_im, sh, sl)
-    back_im = product(spun_im, ch, cl) + product(spun_re, sh, sl)
+    both = product(spun_re + spun_im, ch, cl)
+    back_re = both - product(spun_im, eh, el)
+    back_im = both - product(spun_re, dh, dl)
     terms = []
     for s in range(times):
         tc, ts = twist_cos[s : s + 1, :] / length, twist_sin[s : s + 1, :] / length
@@ -289,7 +293,8 @@
     length = times * time
     twist = 2.0 * np.pi / length * (np.arange(times)[:, None] * index[None, :] % length)
     out = []
-    for table in (np.cos(angle), np.sin(angle)):
+    cos, sin = np.cos(angle), np.sin(angle)
+    for table in (cos, cos - sin, cos + sin):
         high = table.astype(np.float32).astype(jnp.bfloat16)
         low = (table - high.astype(np.float64)).astype(np.float32).astype(jnp.bfloat16)
         out += [jnp.asarray(high), jnp.asarray(low)]

time: 61.3 us -> 61 us (level)
    unnamed x20 -> x24, local copies, waits for them, and re-layouts: 2.31 us -> 2.32 us
where the time goes in v6:
time: 61 us; the launch traced here: 60.8 us
  starting transfers between devices  29.2 us (48%)
  waiting for transfers between devices  14.3 us (23%)
  Pallas kernels  13.7 us (22%)
  local copies, waits for them, and re-layouts  3.08 us (5%)
    ppermute x12, starting transfers between devices, swap_chip(): return lax.ppermute(value, 'pix', pairs)  15.5 us
    ppermute x8, starting transfers between devices, swap_tm(): return lax.ppermute(value, 'tm', [(i, i ^ mask) for i in range(size)])  12.5 us
    pallas_call x11, Pallas kernels, run(): pl.pallas_call(kernel, out_shape=tuple((jax.ShapeDtypeStruct(*out) for ou...  12.1 us
    ppermute x8, waiting for transfers between devices, swap_tm(): return lax.ppermute(value, 'tm', [(i, i ^ mask) for i in range(size)])  6.86 us
    ppermute x12, waiting for transfers between devices, swap_chip(): return lax.ppermute(value, 'pix', pairs)  6.01 us
    unnamed x24, local copies, waits for them, and re-layouts  2.32 us
    pallas_call x2, Pallas kernels, join(): pl.pallas_call(functools.partial(join_kernel, before is None), out_shape=...  1.59 us
    ppermute x5, waiting for transfers between devices, swap_pix(): return lax.ppermute(value, 'pix', [(i, i ^ mask) for i in range(size)])  1.39 us
  transfers between devices with their start and end apart: 25, of which 10 were waited for; matrix products, arithmetic and copies ran while one was open for 2% of the time, Pallas kernels for 19%

profile of v6, /device:TPU:0, one launch (start us, length us, event | category | flops | bytes accessed | tf_op | source)
XLA Modules:
  0.0 60.8 jit_solution(4601279342683215133)
XLA Ops:
  0.0 0.5 collective-permute-start.2
  0.5 1.0 %copy-done.2 = f32[32,8,2,256]{3,2,1,0:T(2,128)S(1)} copy-done((f32[32,8,2,256]{3,2,1,0:T(2,128)S(1)}, f32[32,8,2,256]{3,2,1,0:T(2,128)}, u32[]{:S(2)}) %copy-start.2) | copy-done | bytes 524312
  2.3 0.9 %collective-permute-done.1.other = f32[4,32,256]{2,1,0:T(8,128)S(1)} collective-permute-done((f32[4,32,256]{2,1,0:T(8,128)S(1)}, f32[4,32,256]{2,1,0:T(8,128)S(1)}, u32[]{:S(2)}, u32[]{:S(2)}) %collective-permute-start.1) | collective-permute-done | bytes 131104 | tf_op jit(solution)/shard_map/ppermute | solution.py:48
  3.2 2.9 %collective-permute-start.3 = (bf16[4,64,256]{2,1,0:T(8,128)(2,1)S(1)}, bf16[4,64,256]{2,1,0:T(8,128)(2,1)S(1)}, u32[]{:S(2)}, u32[]{:S(2)}) collective-permute-start(bf16[4,64,256]{2,1,0:T(8,128)(2,1)S(1)} %get-tuple-element.41.refs_4_), channel_id=1, source_target_pairs={{0,8},{4,20},{8,0},{12,28},{16,24},{20,4},{24,16},{28,12},{1,9},{5... | collective-permute-start | bytes 393224 | tf_op jit(solution)/shard_map/ppermute | solution.py:53
  6.1 1.5 %collective-permute-start.4 = (bf16[4,64,256]{2,1,0:T(8,128)(2,1)S(1)}, bf16[4,64,256]{2,1,0:T(8,128)(2,1)S(1)}, u32[]{:S(2)}, u32[]{:S(2)}) collective-permute-start(bf16[4,64,256]{2,1,0:T(8,128)(2,1)S(1)} %get-tuple-element.41.refs_4_), channel_id=1, source_target_pairs={{0,16},{4,12},{8,24},{12,4},{16,0},{20,28},{24,8},{28,20},{1,17},{... | collective-permute-start | bytes 393224 | tf_op jit(solution)/shard_map/ppermute | solution.py:53
  7.7 1.2 %copy-done = bf16[2048,256]{1,0:T(8,128)(2,1)S(1)} copy-done((bf16[2048,256]{1,0:T(8,128)(2,1)S(1)}, bf16[2048,256]{1,0:T(8,128)(2,1)}, u32[]{:S(2)}) %copy-start) | copy-done | bytes 1048600
  9.4 2.0 %collective-permute-start.10 = (bf16[4,64,256]{2,1,0:T(8,128)(2,1)S(1)}, bf16[4,64,256]{2,1,0:T(8,128)(2,1)S(1)}, u32[]{:S(2)}, u32[]{:S(2)}) collective-permute-start(bf16[4,64,256]{2,1,0:T(8,128)(2,1)S(1)} %get-tuple-element.47.refs_4_), channel_id=1, source_target_pairs={{0,16},{4,12},{8,24},{12,4},{16,0},{20,28},{24,8},{28,20},{1,17},{... | collective-permute-start | bytes 393224 | tf_op jit(solution)/shard_map/ppermute | solution.py:53
  11.8 1.6 %collective-permute-start.11 = (bf16[4,64,256]{2,1,0:T(8,128)(2,1)S(1)}, bf16[4,64,256]{2,1,0:T(8,128)(2,1)S(1)}, u32[]{:S(2)}, u32[]{:S(2)}) collective-permute-start(bf16[4,64,256]{2,1,0:T(8,128)(2,1)S(1)} %get-tuple-element.47.refs_4_), channel_id=1, source_target_pairs={{0,24},{4,28},{8,16},{12,20},{16,8},{20,12},{24,0},{28,4},{1,25},{... | collective-permute-start | bytes 393224 | tf_op jit(solution)/shard_map/ppermute | solution.py:53
  14.1 4.7 %shard_map.114 = (f32[4,64,256]{2,1,0:T(8,128)S(1)}, bf16[4,64,256]{2,1,0:T(8,128)(2,1)S(1)}, bf16[4,64,256]{2,1,0:T(8,128)(2,1)S(1)}, bf16[4,64,256]{2,1,0:T(8,128)(2,1)S(1)}) custom-call(bf16[2048,256]{1,0:T(8,128)(2,1)S(1)} %copy-done.1, bf16[2048,256]{1,0:T(8,128)(2,1)S(1)} %collective-permute-done.2.profiles.refs_1_, ...), custom_call_target="tpu_custom_call" | custom-call | flops 4294967296 | bytes 5373952 | tf_op jit(solution)/shard_map/pallas_call | solution.py:28
  18.9 1.8 %collective-permute-start.6 = (bf16[4,64,256]{2,1,0:T(8,128)(2,1)S(1)}, bf16[4,64,256]{2,1,0:T(8,128)(2,1)S(1)}, u32[]{:S(2)}, u32[]{:S(2)}) collective-permute-start(bf16[4,64,256]{2,1,0:T(8,128)(2,1)S(1)} %get-tuple-element.43), channel_id=1, source_target_pairs={{0,8},{4,20},{8,0},{12,28},{16,24},{20,4},{24,16},{28,12},{1,9},{5... | collective-permute-start | bytes 393224 | tf_op jit(solution)/shard_map/ppermute | solution.py:53
  20.7 1.6 %collective-permute-start.7 = (bf16[4,64,256]{2,1,0:T(8,128)(2,1)S(1)}, bf16[4,64,256]{2,1,0:T(8,128)(2,1)S(1)}, u32[]{:S(2)}, u32[]{:S(2)}) collective-permute-start(bf16[4,64,256]{2,1,0:T(8,128)(2,1)S(1)} %get-tuple-element.44), channel_id=1, source_target_pairs={{0,16},{4,12},{8,24},{12,4},{16,0},{20,28},{24,8},{28,20},{1,17},{... | collective-permute-start | bytes 393224 | tf_op jit(solution)/shard_map/ppermute | solution.py:53
  22.4 4.7 %shard_map.116 = (f32[4,64,256]{2,1,0:T(8,128)S(1)}, bf16[4,64,256]{2,1,0:T(8,128)(2,1)S(1)}, bf16[4,64,256]{2,1,0:T(8,128)(2,1)S(1)}, bf16[4,64,256]{2,1,0:T(8,128)(2,1)S(1)}) custom-call(bf16[2048,256]{1,0:T(8,128)(2,1)S(1)} %copy-done.1, bf16[2048,256]{1,0:T(8,128)(2,1)S(1)} %collective-permute-done.2.profiles.refs_1_, ...), custom_call_target="tpu_custom_call" | custom-call | flops 4294967296 | bytes 5373952 | tf_op jit(solution)/shard_map/pallas_call | solution.py:28
  27.2 1.8 %collective-permute-start.12 = (bf16[4,64,256]{2,1,0:T(8,128)(2,1)S(1)}, bf16[4,64,256]{2,1,0:T(8,128)(2,1)S(1)}, u32[]{:S(2)}, u32[]{:S(2)}) collective-permute-start(bf16[4,64,256]{2,1,0:T(8,128)(2,1)S(1)} %get-tuple-element.49), channel_id=1, source_target_pairs={{0,8},{4,20},{8,0},{12,28},{16,24},{20,4},{24,16},{28,12},{1,9},{5... | collective-permute-start | bytes 393224 | tf_op jit(solution)/shard_map/ppermute | solution.py:53
  29.0 1.6 %collective-permute-start.13 = (bf16[4,64,256]{2,1,0:T(8,128)(2,1)S(1)}, bf16[4,64,256]{2,1,0:T(8,128)(2,1)S(1)}, u32[]{:S(2)}, u32[]{:S(2)}) collective-permute-start(bf16[4,64,256]{2,1,0:T(8,128)(2,1)S(1)} %get-tuple-element.50), channel_id=1, source_target_pairs={{0,16},{4,12},{8,24},{12,4},{16,0},{20,28},{24,8},{28,20},{1,17},{... | collective-permute-start | bytes 393224 | tf_op jit(solution)/shard_map/ppermute | solution.py:53
  30.9 2.7 %collective-permute-done.12.refs_2_ = bf16[4,64,256]{2,1,0:T(8,128)(2,1)S(1)} collective-permute-done((bf16[4,64,256]{2,1,0:T(8,128)(2,1)S(1)}, bf16[4,64,256]{2,1,0:T(8,128)(2,1)S(1)}, u32[]{:S(2)}, u32[]{:S(2)}) %collective-permute-start.12) | collective-permute-done | bytes 131104 | tf_op jit(solution)/shard_map/ppermute | solution.py:53
  33.6 1.6 %collective-permute-done.13.refs_3_ = bf16[4,64,256]{2,1,0:T(8,128)(2,1)S(1)} collective-permute-done((bf16[4,64,256]{2,1,0:T(8,128)(2,1)S(1)}, bf16[4,64,256]{2,1,0:T(8,128)(2,1)S(1)}, u32[]{:S(2)}, u32[]{:S(2)}) %collective-permute-start.13) | collective-permute-done | bytes 131104 | tf_op jit(solution)/shard_map/ppermute | solution.py:53
  35.2 1.3 %collective-permute-done.14.refs_4_ = bf16[4,64,256]{2,1,0:T(8,128)(2,1)S(1)} collective-permute-done((bf16[4,64,256]{2,1,0:T(8,128)(2,1)S(1)}, bf16[4,64,256]{2,1,0:T(8,128)(2,1)S(1)}, u32[]{:S(2)}, u32[]{:S(2)}) %collective-permute-start.14) | collective-permute-done | bytes 131104 | tf_op jit(solution)/shard_map/ppermute | solution.py:53
  36.6 1.6 %collective-permute-start.15 = (bf16[8,16,256]{2,1,0:T(8,128)(2,1)S(1)}, bf16[8,16,256]{2,1,0:T(8,128)(2,1)S(1)}, u32[]{:S(2)}, u32[]{:S(2)}) collective-permute-start(bf16[8,16,256]{2,1,0:T(8,128)(2,1)S(1)} %get-tuple-element.52), channel_id=1, source_target_pairs={{0,1},{1,0},{2,3},{3,2},{4,5},{5,4},{6,7},{7,6},{8,9},{9,8},{10,11... | collective-permute-start | bytes 196616 | tf_op jit(solution)/shard_map/ppermute | solution.py:57
  38.2 2.6 %collective-permute-start.18 = (bf16[4,16,256]{2,1,0:T(8,128)(2,1)S(1)}, bf16[4,16,256]{2,1,0:T(8,128)(2,1)S(1)}, u32[]{:S(2)}, u32[]{:S(2)}) collective-permute-start(bf16[4,16,256]{2,1,0:T(8,128)(2,1)S(1)} %get-tuple-element.57), channel_id=1, source_target_pairs={{0,2},{1,3},{2,0},{3,1},{4,6},{5,7},{6,4},{7,5},{8,10},{9,11},{10,... | collective-permute-start | bytes 98312 | tf_op jit(solution)/shard_map/ppermute | solution.py:57
  41.0 1.6 %collective-permute-start.16 = (bf16[4,16,256]{2,1,0:T(8,128)(2,1)S(1)}, bf16[4,16,256]{2,1,0:T(8,128)(2,1)S(1)}, u32[]{:S(2)}, u32[]{:S(2)}) collective-permute-start(bf16[4,16,256]{2,1,0:T(8,128)(2,1)S(1)} %get-tuple-element.54), channel_id=1, source_target_pairs={{0,2},{1,3},{2,0},{3,1},{4,6},{5,7},{6,4},{7,5},{8,10},{9,11},{10,... | collective-permute-start | bytes 98312 | tf_op jit(solution)/shard_map/ppermute | solution.py:57
  42.7 1.9 %collective-permute-start.17 = (bf16[4,16,256]{2,1,0:T(8,128)(2,1)S(1)}, bf16[4,16,256]{2,1,0:T(8,128)(2,1)S(1)}, u32[]{:S(2)}, u32[]{:S(2)}) collective-permute-start(bf16[4,16,256]{2,1,0:T(8,128)(2,1)S(1)} %get-tuple-element.55), channel_id=1, source_target_pairs={{0,3},{1,2},{2,1},{3,0},{4,7},{5,6},{6,5},{7,4},{8,11},{9,10},{10,... | collective-permute-start | bytes 98312 | tf_op jit(solution)/shard_map/ppermute | solution.py:57
  45.7 0.8 %collective-permute-done.19.refs_6_ = bf16[4,16,256]{2,1,0:T(8,128)(2,1)S(1)} collective-permute-done((bf16[4,16,256]{2,1,0:T(8,128)(2,1)S(1)}, bf16[4,16,256]{2,1,0:T(8,128)(2,1)S(1)}, u32[]{:S(2)}, u32[]{:S(2)}) %collective-permute-start.19) | collective-permute-done | bytes 32800 | tf_op jit(solution)/shard_map/ppermute | solution.py:57
  46.5 1.9 %collective-permute-done.17.refs_3_ = bf16[4,16,256]{2,1,0:T(8,128)(2,1)S(1)} collective-permute-done((bf16[4,16,256]{2,1,0:T(8,128)(2,1)S(1)}, bf16[4,16,256]{2,1,0:T(8,128)(2,1)S(1)}, u32[]{:S(2)}, u32[]{:S(2)}) %collective-permute-start.17) | collective-permute-done | bytes 32800 | tf_op jit(solution)/shard_map/ppermute | solution.py:57
  48.5 1.4 %shard_map.118 = (f32[8,16,256]{2,1,0:T(8,128)S(1)}, bf16[8,16,256]{2,1,0:T(8,128)(2,1)S(1)}, bf16[8,16,256]{2,1,0:T(8,128)(2,1)S(1)}, bf16[8,16,256]{2,1,0:T(8,128)(2,1)S(1)}) custom-call(bf16[8,16,256]{2,1,0:T(8,128)(2,1)S(1)} %collective-permute-done.15.refs_0_, f32[4,16,256]{2,1,0:T(8,128)S(1)} %get-tuple-element.53.refs_1_, ...), custom_call_target="tpu_custom_call" | custom-call | flops 1000000000 | bytes 1581056 | tf_op jit(solution)/shard_map/pallas_call | solution.py:28
  49.9 1.0 %collective-permute-start.21 = (bf16[8,16,256]{2,1,0:T(8,128)(2,1)S(1)}, bf16[8,16,256]{2,1,0:T(8,128)(2,1)S(1)}, u32[]{:S(2)}, u32[]{:S(2)}) collective-permute-start(bf16[8,16,256]{2,1,0:T(8,128)(2,1)S(1)} %get-tuple-element.60), channel_id=1, source_target_pairs={{0,1},{1,0},{2,3},{3,2},{4,5},{5,4},{6,7},{7,6},{8,9},{9,8},{10,11... | collective-permute-start | bytes 196616 | tf_op jit(solution)/shard_map/ppermute | solution.py:57
  50.8 1.6 %collective-permute-start.22 = (bf16[8,16,256]{2,1,0:T(8,128)(2,1)S(1)}, bf16[8,16,256]{2,1,0:T(8,128)(2,1)S(1)}, u32[]{:S(2)}, u32[]{:S(2)}) collective-permute-start(bf16[8,16,256]{2,1,0:T(8,128)(2,1)S(1)} %get-tuple-element.61), channel_id=1, source_target_pairs={{0,2},{1,3},{2,0},{3,1},{4,6},{5,7},{6,4},{7,5},{8,10},{9,11},{10,... | collective-permute-start | bytes 196616 | tf_op jit(solution)/shard_map/ppermute | solution.py:57
  52.4 1.9 %collective-permute-start.23 = (bf16[8,16,256]{2,1,0:T(8,128)(2,1)S(1)}, bf16[8,16,256]{2,1,0:T(8,128)(2,1)S(1)}, u32[]{:S(2)}, u32[]{:S(2)}) collective-permute-start(bf16[8,16,256]{2,1,0:T(8,128)(2,1)S(1)} %get-tuple-element.62), channel_id=1, source_target_pairs={{0,3},{1,2},{2,1},{3,0},{4,7},{5,6},{6,5},{7,4},{8,11},{9,10},{10,... | collective-permute-start | bytes 196616 | tf_op jit(solution)/shard_map/ppermute | solution.py:57
  54.3 2.4 %collective-permute-done.22.refs_2_ = bf16[8,16,256]{2,1,0:T(8,128)(2,1)S(1)} collective-permute-done((bf16[8,16,256]{2,1,0:T(8,128)(2,1)S(1)}, bf16[8,16,256]{2,1,0:T(8,128)(2,1)S(1)}, u32[]{:S(2)}, u32[]{:S(2)}) %collective-permute-start.22) | collective-permute-done | bytes 65568 | tf_op jit(solution)/shard_map/ppermute | solution.py:57
  56.7 1.8 %collective-permute-done.23.refs_3_ = bf16[8,16,256]{2,1,0:T(8,128)(2,1)S(1)} collective-permute-done((bf16[8,16,256]{2,1,0:T(8,128)(2,1)S(1)}, bf16[8,16,256]{2,1,0:T(8,128)(2,1)S(1)}, u32[]{:S(2)}, u32[]{:S(2)}) %collective-permute-start.23) | collective-permute-done | bytes 65568 | tf_op jit(solution)/shard_map/ppermute | solution.py:57
  58.6 0.8 %join.2.refs_0_ = f32[32,8,2,256]{3,2,1,0:T(2,128)} custom-call(f32[8,32,256]{2,1,0:T(8,128)S(1)} %get-tuple-element.64.part), custom_call_target="tpu_custom_call" | custom-call | bytes 524288 | tf_op jit(solution)/shard_map/join/pallas_call | solution.py:277
  59.4 0.5 collective-permute-done.24.part
  60.0 0.8 %join.3 = f32[32,8,2,256]{3,2,1,0:T(2,128)} custom-call(bf16[8,32,256]{2,1,0:T(8,128)(2,1)S(1)} %collective-permute-done.24.part, f32[32,8,2,256]{3,2,1,0:T(2,128)} %join.2.refs_0_), custom_call_target="tpu_custom_call", output_to_operand_aliasing={{}: (1, {})} | custom-call | bytes 393216 | tf_op jit(solution)/shard_map/join/pallas_call | solution.py:277
  (61 shorter events, 4.3 us)
Async XLA Ops:
  0.0 9.4 %collective-permute-start.2 = (bf16[2048,256]{1,0:T(8,128)(2,1)}, bf16[2048,256]{1,0:T(8,128)(2,1)S(1)}, u32[]{:S(2)}, u32[]{:S(2)}) collective-permute-start(bf16[2048,256]{1,0:T(8,128)(2,1)} %refs_0_.3), channel_id=1, source_target_pairs={{0,4},{4,0},{8,12},{12,8},{16,20},{20,16},{24,28},{28,24},{1,5},{5... | collective-permute-start | bytes 3145736 | tf_op jit(solution)/shard_map/ppermute | solution.py:48
  1.7 1.4 %collective-permute-start.1 = (f32[4,32,256]{2,1,0:T(8,128)S(1)}, f32[4,32,256]{2,1,0:T(8,128)S(1)}, u32[]{:S(2)}, u32[]{:S(2)}) collective-permute-start(f32[4,32,256]{2,1,0:T(8,128)S(1)} %get-tuple-element.39), channel_id=1, source_target_pairs={{0,4},{4,0},{8,12},{12,8},{16,20},{20,16},{24,28},{28,24},{1,5},{5... | collective-permute-start | bytes 393224 | tf_op jit(solution)/shard_map/ppermute | solution.py:48
  1.8 7.4 %collective-permute-start = (f32[4,32,256]{2,1,0:T(8,128)S(1)}, f32[4,32,256]{2,1,0:T(8,128)S(1)}, u32[]{:S(2)}, u32[]{:S(2)}) collective-permute-start(f32[4,32,256]{2,1,0:T(8,128)S(1)} %get-tuple-element.36), channel_id=1, source_target_pairs={{0,4},{4,0},{8,12},{12,8},{16,20},{20,16},{24,28},{28,24},{1,5},{5... | collective-permute-start | bytes 393224 | tf_op jit(solution)/shard_map/ppermute | solution.py:48
  3.2 6.1 %copy-start.11 = (f32[8,1024]{1,0:T(8,128)S(1)}, f32[8,1024]{1,0:T(8,128)}, u32[]{:S(2)}) copy-start(f32[8,1024]{1,0:T(8,128)} %param.13) | copy-start | bytes 98308
  3.2 8.6 %collective-permute-start.3 = (bf16[4,64,256]{2,1,0:T(8,128)(2,1)S(1)}, bf16[4,64,256]{2,1,0:T(8,128)(2,1)S(1)}, u32[]{:S(2)}, u32[]{:S(2)}) collective-permute-start(bf16[4,64,256]{2,1,0:T(8,128)(2,1)S(1)} %get-tuple-element.41.refs_4_), channel_id=1, source_target_pairs={{0,8},{4,20},{8,0},{12,28},{16,24},{20,4},{24,16},{28,12},{1,9},{5... | collective-permute-start | bytes 393224 | tf_op jit(solution)/shard_map/ppermute | solution.py:53
  6.1 7.3 %collective-permute-start.4 = (bf16[4,64,256]{2,1,0:T(8,128)(2,1)S(1)}, bf16[4,64,256]{2,1,0:T(8,128)(2,1)S(1)}, u32[]{:S(2)}, u32[]{:S(2)}) collective-permute-start(bf16[4,64,256]{2,1,0:T(8,128)(2,1)S(1)} %get-tuple-element.41.refs_4_), channel_id=1, source_target_pairs={{0,16},{4,12},{8,24},{12,4},{16,0},{20,28},{24,8},{28,20},{1,17},{... | collective-permute-start | bytes 393224 | tf_op jit(solution)/shard_map/ppermute | solution.py:53
  7.7 6.5 %collective-permute-start.5 = (bf16[4,64,256]{2,1,0:T(8,128)(2,1)S(1)}, bf16[4,64,256]{2,1,0:T(8,128)(2,1)S(1)}, u32[]{:S(2)}, u32[]{:S(2)}) collective-permute-start(bf16[4,64,256]{2,1,0:T(8,128)(2,1)S(1)} %get-tuple-element.41.refs_4_), channel_id=1, source_target_pairs={{0,24},{4,28},{8,16},{12,20},{16,8},{20,12},{24,0},{28,4},{1,25},{... | collective-permute-start | bytes 393224 | tf_op jit(solution)/shard_map/ppermute | solution.py:53
  9.3 19.7 %collective-permute-start.20 = (f32[8,1024]{1,0:T(8,128)S(1)}, f32[8,1024]{1,0:T(8,128)S(1)}, u32[]{:S(2)}, u32[]{:S(2)}) collective-permute-start(f32[8,1024]{1,0:T(8,128)S(1)} %copy-done.11), channel_id=1, source_target_pairs={{0,4},{4,0},{8,12},{12,8},{16,20},{20,16},{24,28},{28,24},{1,5},{5... | collective-permute-start | bytes 98312 | tf_op jit(solution)/shard_map/ppermute | solution.py:48
  9.4 4.7 %copy-start.1 = (bf16[2048,256]{1,0:T(8,128)(2,1)S(1)}, bf16[2048,256]{1,0:T(8,128)(2,1)}, u32[]{:S(2)}) copy-start(bf16[2048,256]{1,0:T(8,128)(2,1)} %refs_0_.3) | copy-start | bytes 3145732
  9.4 11.2 %collective-permute-start.10 = (bf16[4,64,256]{2,1,0:T(8,128)(2,1)S(1)}, bf16[4,64,256]{2,1,0:T(8,128)(2,1)S(1)}, u32[]{:S(2)}, u32[]{:S(2)}) collective-permute-start(bf16[4,64,256]{2,1,0:T(8,128)(2,1)S(1)} %get-tuple-element.47.refs_4_), channel_id=1, source_target_pairs={{0,16},{4,12},{8,24},{12,4},{16,0},{20,28},{24,8},{28,20},{1,17},{... | collective-permute-start | bytes 393224 | tf_op jit(solution)/shard_map/ppermute | solution.py:53
  11.8 10.5 %collective-permute-start.11 = (bf16[4,64,256]{2,1,0:T(8,128)(2,1)S(1)}, bf16[4,64,256]{2,1,0:T(8,128)(2,1)S(1)}, u32[]{:S(2)}, u32[]{:S(2)}) collective-permute-start(bf16[4,64,256]{2,1,0:T(8,128)(2,1)S(1)} %get-tuple-element.47.refs_4_), channel_id=1, source_target_pairs={{0,24},{4,28},{8,16},{12,20},{16,8},{20,12},{24,0},{28,4},{1,25},{... | collective-permute-start | bytes 393224 | tf_op jit(solution)/shard_map/ppermute | solution.py:53
  13.5 9.0 %collective-permute-start.9 = (bf16[4,64,256]{2,1,0:T(8,128)(2,1)S(1)}, bf16[4,64,256]{2,1,0:T(8,128)(2,1)S(1)}, u32[]{:S(2)}, u32[]{:S(2)}) collective-permute-start(bf16[4,64,256]{2,1,0:T(8,128)(2,1)S(1)} %get-tuple-element.47.refs_4_), channel_id=1, source_target_pairs={{0,8},{4,20},{8,0},{12,28},{16,24},{20,4},{24,16},{28,12},{1,9},{5... | collective-permute-start | bytes 393224 | tf_op jit(solution)/shard_map/ppermute | solution.py:53
  18.9 11.7 %collective-permute-start.6 = (bf16[4,64,256]{2,1,0:T(8,128)(2,1)S(1)}, bf16[4,64,256]{2,1,0:T(8,128)(2,1)S(1)}, u32[]{:S(2)}, u32[]{:S(2)}) collective-permute-start(bf16[4,64,256]{2,1,0:T(8,128)(2,1)S(1)} %get-tuple-element.43), channel_id=1, source_target_pairs={{0,8},{4,20},{8,0},{12,28},{16,24},{20,4},{24,16},{28,12},{1,9},{5... | collective-permute-start | bytes 393224 | tf_op jit(solution)/shard_map/ppermute | solution.py:53
  20.7 10.1 %collective-permute-start.7 = (bf16[4,64,256]{2,1,0:T(8,128)(2,1)S(1)}, bf16[4,64,256]{2,1,0:T(8,128)(2,1)S(1)}, u32[]{:S(2)}, u32[]{:S(2)}) collective-permute-start(bf16[4,64,256]{2,1,0:T(8,128)(2,1)S(1)} %get-tuple-element.44), channel_id=1, source_target_pairs={{0,16},{4,12},{8,24},{12,4},{16,0},{20,28},{24,8},{28,20},{1,17},{... | collective-permute-start | bytes 393224 | tf_op jit(solution)/shard_map/ppermute | solution.py:53
  22.3 8.5 %collective-permute-start.8 = (bf16[4,64,256]{2,1,0:T(8,128)(2,1)S(1)}, bf16[4,64,256]{2,1,0:T(8,128)(2,1)S(1)}, u32[]{:S(2)}, u32[]{:S(2)}) collective-permute-start(bf16[4,64,256]{2,1,0:T(8,128)(2,1)S(1)} %get-tuple-element.45), channel_id=1, source_target_pairs={{0,24},{4,28},{8,16},{12,20},{16,8},{20,12},{24,0},{28,4},{1,25},{... | collective-permute-start | bytes 393224 | tf_op jit(solution)/shard_map/ppermute | solution.py:53
  27.2 6.4 %collective-permute-start.12 = (bf16[4,64,256]{2,1,0:T(8,128)(2,1)S(1)}, bf16[4,64,256]{2,1,0:T(8,128)(2,1)S(1)}, u32[]{:S(2)}, u32[]{:S(2)}) collective-permute-start(bf16[4,64,256]{2,1,0:T(8,128)(2,1)S(1)} %get-tuple-element.49), channel_id=1, source_target_pairs={{0,8},{4,20},{8,0},{12,28},{16,24},{20,4},{24,16},{28,12},{1,9},{5... | collective-permute-start | bytes 393224 | tf_op jit(solution)/shard_map/ppermute | solution.py:53
  29.0 6.2 %collective-permute-start.13 = (bf16[4,64,256]{2,1,0:T(8,128)(2,1)S(1)}, bf16[4,64,256]{2,1,0:T(8,128)(2,1)S(1)}, u32[]{:S(2)}, u32[]{:S(2)}) collective-permute-start(bf16[4,64,256]{2,1,0:T(8,128)(2,1)S(1)} %get-tuple-element.50), channel_id=1, source_target_pairs={{0,16},{4,12},{8,24},{12,4},{16,0},{20,28},{24,8},{28,20},{1,17},{... | collective-permute-start | bytes 393224 | tf_op jit(solution)/shard_map/ppermute | solution.py:53
  30.6 5.9 %collective-permute-start.14 = (bf16[4,64,256]{2,1,0:T(8,128)(2,1)S(1)}, bf16[4,64,256]{2,1,0:T(8,128)(2,1)S(1)}, u32[]{:S(2)}, u32[]{:S(2)}) collective-permute-start(bf16[4,64,256]{2,1,0:T(8,128)(2,1)S(1)} %get-tuple-element.51), channel_id=1, source_target_pairs={{0,24},{4,28},{8,16},{12,20},{16,8},{20,12},{24,0},{28,4},{1,25},{... | collective-permute-start | bytes 393224 | tf_op jit(solution)/shard_map/ppermute | solution.py:53
  36.6 11.8 %collective-permute-start.15 = (bf16[8,16,256]{2,1,0:T(8,128)(2,1)S(1)}, bf16[8,16,256]{2,1,0:T(8,128)(2,1)S(1)}, u32[]{:S(2)}, u32[]{:S(2)}) collective-permute-start(bf16[8,16,256]{2,1,0:T(8,128)(2,1)S(1)} %get-tuple-element.52), channel_id=1, source_target_pairs={{0,1},{1,0},{2,3},{3,2},{4,5},{5,4},{6,7},{7,6},{8,9},{9,8},{10,11... | collective-permute-start | bytes 196616 | tf_op jit(solution)/shard_map/ppermute | solution.py:57
  38.2 7.5 %collective-permute-start.18 = (bf16[4,16,256]{2,1,0:T(8,128)(2,1)S(1)}, bf16[4,16,256]{2,1,0:T(8,128)(2,1)S(1)}, u32[]{:S(2)}, u32[]{:S(2)}) collective-permute-start(bf16[4,16,256]{2,1,0:T(8,128)(2,1)S(1)} %get-tuple-element.57), channel_id=1, source_target_pairs={{0,2},{1,3},{2,0},{3,1},{4,6},{5,7},{6,4},{7,5},{8,10},{9,11},{10,... | collective-permute-start | bytes 98312 | tf_op jit(solution)/shard_map/ppermute | solution.py:57
  40.8 5.7 %collective-permute-start.19 = (bf16[4,16,256]{2,1,0:T(8,128)(2,1)S(1)}, bf16[4,16,256]{2,1,0:T(8,128)(2,1)S(1)}, u32[]{:S(2)}, u32[]{:S(2)}) collective-permute-start(bf16[4,16,256]{2,1,0:T(8,128)(2,1)S(1)} %get-tuple-element.58), channel_id=1, source_target_pairs={{0,3},{1,2},{2,1},{3,0},{4,7},{5,6},{6,5},{7,4},{8,11},{9,10},{10,... | collective-permute-start | bytes 98312 | tf_op jit(solution)/shard_map/ppermute | solution.py:57
  41.0 5.4 %collective-permute-start.16 = (bf16[4,16,256]{2,1,0:T(8,128)(2,1)S(1)}, bf16[4,16,256]{2,1,0:T(8,128)(2,1)S(1)}, u32[]{:S(2)}, u32[]{:S(2)}) collective-permute-start(bf16[4,16,256]{2,1,0:T(8,128)(2,1)S(1)} %get-tuple-element.54), channel_id=1, source_target_pairs={{0,2},{1,3},{2,0},{3,1},{4,6},{5,7},{6,4},{7,5},{8,10},{9,11},{10,... | collective-permute-start | bytes 98312 | tf_op jit(solution)/shard_map/ppermute | solution.py:57
  42.7 5.7 %collective-permute-start.17 = (bf16[4,16,256]{2,1,0:T(8,128)(2,1)S(1)}, bf16[4,16,256]{2,1,0:T(8,128)(2,1)S(1)}, u32[]{:S(2)}, u32[]{:S(2)}) collective-permute-start(bf16[4,16,256]{2,1,0:T(8,128)(2,1)S(1)} %get-tuple-element.55), channel_id=1, source_target_pairs={{0,3},{1,2},{2,1},{3,0},{4,7},{5,6},{6,5},{7,4},{8,11},{9,10},{10,... | collective-permute-start | bytes 98312 | tf_op jit(solution)/shard_map/ppermute | solution.py:57
  45.2 3.2 %copy-start.7 = (bf16[256,256]{1,0:T(8,128)(2,1)S(1)}, bf16[256,256]{1,0:T(8,128)(2,1)}, u32[]{:S(2)}) copy-start(bf16[256,256]{1,0:T(8,128)(2,1)} %constant.40.clone.refs_13_) | copy-start | bytes 393220
  45.2 3.2 %copy-start.8 = (bf16[256,256]{1,0:T(8,128)(2,1)S(1)}, bf16[256,256]{1,0:T(8,128)(2,1)}, u32[]{:S(2)}) copy-start(bf16[256,256]{1,0:T(8,128)(2,1)} %constant.41.clone.refs_14_) | copy-start | bytes 393220
  45.4 3.0 %copy-start.3 = (bf16[256,256]{1,0:T(8,128)(2,1)S(1)}, bf16[256,256]{1,0:T(8,128)(2,1)}, u32[]{:S(2)}) copy-start(bf16[256,256]{1,0:T(8,128)(2,1)} %constant.36.clone.refs_9_) | copy-start | bytes 393220
  45.5 3.0 %copy-start.4 = (bf16[256,256]{1,0:T(8,128)(2,1)S(1)}, bf16[256,256]{1,0:T(8,128)(2,1)}, u32[]{:S(2)}) copy-start(bf16[256,256]{1,0:T(8,128)(2,1)} %constant.37.clone.refs_10_) | copy-start | bytes 393220
  45.5 3.0 %copy-start.5 = (bf16[256,256]{1,0:T(8,128)(2,1)S(1)}, bf16[256,256]{1,0:T(8,128)(2,1)}, u32[]{:S(2)}) copy-start(bf16[256,256]{1,0:T(8,128)(2,1)} %constant.38.clone.refs_11_) | copy-start | bytes 393220
  49.9 4.5 %collective-permute-start.21 = (bf16[8,16,256]{2,1,0:T(8,128)(2,1)S(1)}, bf16[8,16,256]{2,1,0:T(8,128)(2,1)S(1)}, u32[]{:S(2)}, u32[]{:S(2)}) collective-permute-start(bf16[8,16,256]{2,1,0:T(8,128)(2,1)S(1)} %get-tuple-element.60), channel_id=1, source_target_pairs={{0,1},{1,0},{2,3},{3,2},{4,5},{5,4},{6,7},{7,6},{8,9},{9,8},{10,11... | collective-permute-start | bytes 196616 | tf_op jit(solution)/shard_map/ppermute | solution.py:57
  50.8 5.9 %collective-permute-start.22 = (bf16[8,16,256]{2,1,0:T(8,128)(2,1)S(1)}, bf16[8,16,256]{2,1,0:T(8,128)(2,1)S(1)}, u32[]{:S(2)}, u32[]{:S(2)}) collective-permute-start(bf16[8,16,256]{2,1,0:T(8,128)(2,1)S(1)} %get-tuple-element.61), channel_id=1, source_target_pairs={{0,2},{1,3},{2,0},{3,1},{4,6},{5,7},{6,4},{7,5},{8,10},{9,11},{10,... | collective-permute-start | bytes 196616 | tf_op jit(solution)/shard_map/ppermute | solution.py:57
  52.4 6.1 %collective-permute-start.23 = (bf16[8,16,256]{2,1,0:T(8,128)(2,1)S(1)}, bf16[8,16,256]{2,1,0:T(8,128)(2,1)S(1)}, u32[]{:S(2)}, u32[]{:S(2)}) collective-permute-start(bf16[8,16,256]{2,1,0:T(8,128)(2,1)S(1)} %get-tuple-element.62), channel_id=1, source_target_pairs={{0,3},{1,2},{2,1},{3,0},{4,7},{5,6},{6,5},{7,4},{8,11},{9,10},{10,... | collective-permute-start | bytes 196616 | tf_op jit(solution)/shard_map/ppermute | solution.py:57
  58.6 1.4 %collective-permute-start.24 = (bf16[8,32,256]{2,1,0:T(8,128)(2,1)S(1)}, bf16[8,32,256]{2,1,0:T(8,128)(2,1)S(1)}, u32[]{:S(2)}, u32[]{:S(2)}) collective-permute-start(bf16[8,32,256]{2,1,0:T(8,128)(2,1)S(1)} %get-tuple-element.63), channel_id=1, source_target_pairs={{0,4},{4,0},{8,12},{12,8},{16,20},{20,16},{24,28},{28,24},{1,5},{5... | collective-permute-start | bytes 393224 | tf_op jit(solution)/shard_map/ppermute | solution.py:48
  (5 other events, 11.0 us)
